TPU v7x, 32 devices: a whole 2x2x4 slice. The times are simulated.
32 devices in a mesh: wide: 4 (over y, core), narrow: 8 (over z, x).
Axes of the slice: x: 2, y: 2, z: 4, core: 2. Of those that a mesh axis runs over, the one named last changes fastest.
Arguments:
- inputs: bfloat16 [64, 1024, 512], P('narrow', 'wide'), may hold values from -6 to 6
- conv_w: bfloat16 [9, 512, 512], replicated, may hold values from -0.09375 to 0.09375
- conv_b: bfloat16 [512], replicated, may hold values from -3 to 3
- ln1_gain: bfloat16 [512], replicated, may hold values from 0.25 to 1.75
- ln1_bias: bfloat16 [512], replicated, may hold values from -2 to 2
- w_in: bfloat16 [512, 2048], replicated, may hold values from -0.25 to 0.25
- b_in: bfloat16 [2048], replicated, may hold values from -3 to 3
- w_out: bfloat16 [2048, 512], replicated, may hold values from -0.125 to 0.125
- ln2_gain: bfloat16 [512], replicated, may hold values from 0.25 to 1.75
- ln2_bias: bfloat16 [512], replicated, may hold values from -2 to 2
- segments: int32 [64, 1024], P('narrow', 'wide'), may hold values from 0 to 7, never falling along the last dimension, each value on 1 to 512 neighbouring positions
- tap_mask: int32 [64, 9, 1024], P('narrow', None, 'wide'), may hold values 0 or 1
- cotangent: bfloat16 [64, 1024, 512], P('narrow', 'wide'), may hold values from -6 to 6
Outputs:
- out: bfloat16 [64, 1024, 512], P('narrow', 'wide')
- grad_inputs: float32 [64, 1024, 512], P('narrow', 'wide')
- grad_conv_w: float32 [9, 512, 512], P(None, 'narrow', 'wide')
- grad_conv_b: float32 [512], replicated
- grad_ln1_gain: float32 [512], replicated
- grad_ln1_bias: float32 [512], replicated
- grad_w_in: float32 [512, 2048], P('narrow', 'wide')
- grad_b_in: float32 [2048], replicated
- grad_w_out: float32 [2048, 512], P('narrow', 'wide')
- grad_ln2_gain: float32 [512], replicated
- grad_ln2_bias: float32 [512], replicated
Inputs may be any that keep to these rules, and one draw needn't show every extreme that they name: `segments`: ids never fall along a row; one id covers at most 512 positions of a row, and some id exactly that many.
All inputs are finite; a program needn't handle non-finite values. No bound on the sum of `tap_mask` on one device may be relied on, other than what follows from the above.
Results may differ from a plain program's by a relative error of at most 0.0073.
Values may be sent and summed in bfloat16 or wider, within the bound.
No kernel may reach another device: no remote copies, remote signals or barrier semaphores. Data moves between devices by JAX's collectives and lax.ppermute only.
A program may use at most 256 MiB of HBM per device.

v0:
```python
import jax
import jax.numpy as jnp
from jax import lax
from jax.sharding import PartitionSpec as P

DILATION_STEP = 32
MB = 4


def layer_norm(values, gain_vec, bias_vec):
    centre = jnp.mean(values, axis=-1, keepdims=True)
    centered = values - centre
    spread = jnp.mean(centered * centered, axis=-1, keepdims=True)
    return centered * lax.rsqrt(spread + 1e-05) * gain_vec + bias_vec


def exact_gelu(values):
    return jax.nn.gelu(values, approximate=False)


def after_conv(hidden, gain_vec, bias_vec):
    return layer_norm(exact_gelu(hidden), gain_vec, bias_vec)


def tap_validity(padded_info, own_info, stride, extent, kernel):
    forward_taps = []
    backward_taps = []
    own_ids = own_info[..., 0]
    for tap_number in range(kernel):
        source_rows = lax.slice_in_dim(
            padded_info, tap_number * stride, tap_number * stride + extent, axis=1
        )
        matched = (source_rows[..., 0] == own_ids) & (own_info[..., 1 + tap_number] == 1)
        forward_taps.append(jnp.where(matched, 1.0, 0.0).astype(jnp.bfloat16))
        offset = (kernel - 1 - tap_number) * stride
        target = lax.slice_in_dim(padded_info, offset, offset + extent, axis=1)
        back_matched = (target[..., 0] == own_ids) & (target[..., 1 + tap_number] == 1)
        backward_taps.append(jnp.where(back_matched, 1.0, 0.0).astype(jnp.bfloat16))
    return (jnp.stack(forward_taps), jnp.stack(backward_taps))


def conv_forward(padded_rows, valid_taps, conv_w, stride, extent):
    summed = None
    for tap_number in range(conv_w.shape[0]):
        source_rows = lax.slice_in_dim(
            padded_rows, tap_number * stride, tap_number * stride + extent, axis=1
        )
        source_rows = source_rows * valid_taps[tap_number][..., None]
        product = jnp.einsum(
            "...c,cd->...d", source_rows, conv_w[tap_number], preferred_element_type=jnp.float32
        )
        summed = product if summed is None else summed + product
    return summed


def conv_backward(
    padded_rows, padded_grad, grad_out, valid_taps, back_taps, conv_w, stride, extent
):
    kernel = conv_w.shape[0]
    features = conv_w.shape[1]
    flat_grad = grad_out.reshape(-1, features)
    weight_grads = []
    grad_source = None
    for tap_number in range(kernel):
        source_rows = lax.slice_in_dim(
            padded_rows, tap_number * stride, tap_number * stride + extent, axis=1
        )
        source_rows = source_rows * valid_taps[tap_number][..., None]
        weight_grads.append(
            lax.dot_general(
                source_rows.reshape(-1, features),
                flat_grad,
                (((0,), (0,)), ((), ())),
                preferred_element_type=jnp.float32,
            )
        )
        offset = (kernel - 1 - tap_number) * stride
        spread_grad = (
            lax.slice_in_dim(padded_grad, offset, offset + extent, axis=1)
            * back_taps[tap_number][..., None]
        )
        product = jnp.einsum(
            "...d,cd->...c", spread_grad, conv_w[tap_number], preferred_element_type=jnp.float32
        )
        grad_source = product if grad_source is None else grad_source + product
    return (jnp.stack(weight_grads), grad_source)


def outer_sum(left_rows, right_rows):
    return lax.dot_general(
        left_rows.reshape(-1, left_rows.shape[-1]),
        right_rows.reshape(-1, right_rows.shape[-1]),
        (((0,), (0,)), ((), ())),
        preferred_element_type=jnp.float32,
    )


def body(
    inputs,
    conv_w,
    conv_b,
    ln1_gain,
    ln1_bias,
    w_in,
    b_in,
    w_out,
    ln2_gain,
    ln2_bias,
    segments,
    tap_mask,
    cotangent,
):
    rows_dev, position_index, features = inputs.shape
    kernel = conv_w.shape[0]
    hidden_units = w_in.shape[1]
    half_taps = kernel // 2
    micro_rows = rows_dev // MB
    conv_bias = conv_b.astype(jnp.float32)
    gain_one = ln1_gain.astype(jnp.float32)
    bias_one = ln1_bias.astype(jnp.float32)
    bias_in = b_in.astype(jnp.float32)
    gain_two = ln2_gain.astype(jnp.float32)
    bias_two = ln2_bias.astype(jnp.float32)
    tap_info = jnp.concatenate([segments[:, :, None], jnp.transpose(tap_mask, (0, 2, 1))], axis=2)
    wide_total_count = lax.axis_size("wide")
    phase_groups = DILATION_STEP // wide_total_count
    block_list = position_index // DILATION_STEP
    all_blocks = wide_total_count * block_list
    phase_info = lax.all_to_all(
        tap_info.reshape(rows_dev, block_list, wide_total_count, phase_groups, kernel + 1),
        "wide",
        split_axis=2,
        concat_axis=1,
        tiled=True,
    )
    phase_info = phase_info.reshape(rows_dev, all_blocks, phase_groups, kernel + 1)
    padded_info = jnp.pad(phase_info, ((0, 0), (half_taps, half_taps), (0, 0), (0, 0)))
    valid_fwd, valid_back = tap_validity(padded_info, phase_info, 1, all_blocks, kernel)
    acc_conv = jnp.zeros((kernel, features, features), jnp.float32)
    acc_w_in = jnp.zeros((features, hidden_units), jnp.float32)
    acc_w_out = jnp.zeros((hidden_units, features), jnp.float32)
    acc_conv_b = jnp.zeros((features,), jnp.float32)
    acc_gain_one = jnp.zeros((features,), jnp.float32)
    acc_bias_one = jnp.zeros((features,), jnp.float32)
    acc_b_in = jnp.zeros((hidden_units,), jnp.float32)
    acc_gain_two = jnp.zeros((features,), jnp.float32)
    acc_bias_two = jnp.zeros((features,), jnp.float32)
    outputs = []
    grads_x = []
    for batch_index in range(MB):
        row_start = batch_index * micro_rows
        row_inputs = inputs[row_start : row_start + micro_rows]
        fwd_taps = valid_fwd[:, row_start : row_start + micro_rows]
        back_taps = valid_back[:, row_start : row_start + micro_rows]
        phase_rows = lax.all_to_all(
            row_inputs.reshape(micro_rows, block_list, wide_total_count, phase_groups, features),
            "wide",
            split_axis=2,
            concat_axis=1,
            tiled=True,
        )
        phase_rows = phase_rows.reshape(micro_rows, all_blocks, phase_groups, features)
        padded_rows = jnp.pad(phase_rows, ((0, 0), (half_taps, half_taps), (0, 0), (0, 0)))
        conv_sum = conv_forward(padded_rows, fwd_taps, conv_w, 1, all_blocks)
        phase_hidden = (conv_sum + conv_bias).astype(jnp.bfloat16)
        hidden = lax.all_to_all(
            phase_hidden.reshape(micro_rows, wide_total_count, block_list, phase_groups, features),
            "wide",
            split_axis=1,
            concat_axis=3,
            tiled=True,
        )
        hidden = hidden.reshape(micro_rows, position_index, features)
        normed_one, pull_one = jax.vjp(after_conv, hidden.astype(jnp.float32), gain_one, bias_one)
        mixed_rows = row_inputs.astype(jnp.float32) + normed_one
        mixed_low = mixed_rows.astype(jnp.bfloat16)
        up_value = (
            jnp.einsum("...d,df->...f", mixed_low, w_in, preferred_element_type=jnp.float32)
            + bias_in
        )
        activated, pull_act = jax.vjp(exact_gelu, up_value)
        act_low = activated.astype(jnp.bfloat16)
        projected = jnp.einsum("...f,fd->...d", act_low, w_out, preferred_element_type=jnp.float32)
        normed_two, pull_two = jax.vjp(layer_norm, projected, gain_two, bias_two)
        outputs.append((mixed_rows + normed_two).astype(jnp.bfloat16))
        ct_rows = cotangent[row_start : row_start + micro_rows].astype(jnp.float32)
        grad_proj, part_gain_two, part_bias_two = pull_two(ct_rows)
        acc_gain_two = acc_gain_two + part_gain_two
        acc_bias_two = acc_bias_two + part_bias_two
        proj_low = grad_proj.astype(jnp.bfloat16)
        acc_w_out = acc_w_out + outer_sum(act_low, proj_low)
        grad_act = jnp.einsum("...d,fd->...f", proj_low, w_out, preferred_element_type=jnp.float32)
        (grad_up,) = pull_act(grad_act)
        up_low = grad_up.astype(jnp.bfloat16)
        acc_b_in = acc_b_in + jnp.sum(up_low.astype(jnp.float32), axis=(0, 1))
        acc_w_in = acc_w_in + outer_sum(mixed_low, up_low)
        grad_mixed = ct_rows + jnp.einsum(
            "...f,df->...d", up_low, w_in, preferred_element_type=jnp.float32
        )
        grad_hidden, part_gain_one, part_bias_one = pull_one(grad_mixed)
        acc_gain_one = acc_gain_one + part_gain_one
        acc_bias_one = acc_bias_one + part_bias_one
        hidden_low = grad_hidden.astype(jnp.bfloat16)
        acc_conv_b = acc_conv_b + jnp.sum(hidden_low.astype(jnp.float32), axis=(0, 1))
        phase_grad = lax.all_to_all(
            hidden_low.reshape(micro_rows, block_list, wide_total_count, phase_groups, features),
            "wide",
            split_axis=2,
            concat_axis=1,
            tiled=True,
        )
        phase_grad = phase_grad.reshape(micro_rows, all_blocks, phase_groups, features)
        padded_grad = jnp.pad(phase_grad, ((0, 0), (half_taps, half_taps), (0, 0), (0, 0)))
        part_conv, grad_source = conv_backward(
            padded_rows, padded_grad, phase_grad, fwd_taps, back_taps, conv_w, 1, all_blocks
        )
        source_low = grad_source.astype(jnp.bfloat16)
        grad_conv_in = lax.all_to_all(
            source_low.reshape(micro_rows, wide_total_count, block_list, phase_groups, features),
            "wide",
            split_axis=1,
            concat_axis=3,
            tiled=True,
        )
        grad_conv_in = grad_conv_in.reshape(micro_rows, position_index, features)
        acc_conv = acc_conv + part_conv
        grads_x.append(grad_mixed + grad_conv_in.astype(jnp.float32))
    partial_sums = (
        lax.psum_scatter(acc_conv, "narrow", scatter_dimension=1, tiled=True),
        lax.psum_scatter(acc_w_in, "narrow", scatter_dimension=0, tiled=True),
        lax.psum_scatter(acc_w_out, "narrow", scatter_dimension=0, tiled=True),
    )
    summed_grads = (
        lax.psum_scatter(partial_sums[0], "wide", scatter_dimension=2, tiled=True),
        lax.psum_scatter(partial_sums[1], "wide", scatter_dimension=1, tiled=True),
        lax.psum_scatter(partial_sums[2], "wide", scatter_dimension=1, tiled=True),
    )
    vectors = lax.psum(
        (acc_conv_b, acc_gain_one, acc_bias_one, acc_b_in, acc_gain_two, acc_bias_two),
        ("wide", "narrow"),
    )
    return (
        jnp.concatenate(outputs, axis=0),
        jnp.concatenate(grads_x, axis=0),
        summed_grads[0],
        vectors[0],
        vectors[1],
        vectors[2],
        summed_grads[1],
        vectors[3],
        summed_grads[2],
        vectors[4],
        vectors[5],
    )


def solution(mesh):
    placed = (
        P("narrow", "wide", None),
        P(),
        P(),
        P(),
        P(),
        P(),
        P(),
        P(),
        P(),
        P(),
        P("narrow", "wide"),
        P("narrow", None, "wide"),
        P("narrow", "wide", None),
    )
    return jax.shard_map(
        body,
        mesh=mesh,
        in_specs=placed,
        out_specs=(
            P("narrow", "wide", None),
            P("narrow", "wide", None),
            P(None, "narrow", "wide"),
            P(),
            P(),
            P(),
            P("narrow", "wide"),
            P(),
            P("narrow", "wide"),
            P(),
            P(),
        ),
        check_vma=False,
    )
```

profile of v0, /device:TPU:0, one launch (start us, length us, event | category | flops | bytes accessed | tf_op | source)
XLA Modules:
  0.0 760.1 jit_solution(1259993870825719143)
XLA Ops:
  18.6 4.2 all-to-all-start.1
  38.4 3.7 copy.168
  85.8 6.2 all-to-all-done
  92.0 4.6 all-to-all-start.3
  128.4 3.6 all-to-all-start.8
  134.4 6.4 all-to-all-done.8
  154.6 4.2 all-to-all-start.4
  191.3 8.3 %fusion.201 = (bf16[2,256,512]{2,1,0:T(8,128)(2,1)S(1)}, f32[2,256,512]{2,1,0:T(8,128)S(1)}, f32[2,256,512]{2,1,0:T(8,128)}, bf16[2,256,512]{2,1,0:T(8,128)(2,1)...) fusion(f32[2,256]{1,0:T(2,128)S(1)} %rsqrt.82, ...), kind=kLoop, calls=%fused_computation.568 | loop fusion | flops 53477376 | bytes 15745024 | tf_op jit(solution)/shard_map/convert_element_type | solution.py:176
  207.8 3.7 fusion.200
  211.5 14.2 %fusion.196 = (u8[256,2048]{1,0:T(8,128)(4,1)}, u8[256,2048]{1,0:T(8,128)(4,1)}, u8[256,2048]{1,0:T(8,128)(4,1)}, u8[256,2048]{1,0:T(8,128)(4,1)}, u8[256,2048]{...) fusion(f32[2048]{0:T(1024)S(1)} %copy-done.193, ...), kind=kOutput, calls=%fused_computation.491 | convolution fusion | flops 1128267776 | bytes 23601152 | tf_op jit(solution)/shard_map/...d,df->...f/dot_general | solution.py:178
  225.7 42.3 %multiply_convert_fusion.1 = (bf16[2,256,2048]{2,1,0:T(8,128)(2,1)S(1)}, f32[2,256,2048]{2,1,0:T(8,128)}, bf16[2,256,2048]{2,1,0:T(8,128)(2,1)S(1)}, f32[2,256,2...) fusion(f32[2,256,2048]{2,1,0:T(8,128)} %fusion.46, ...), kind=kLoop, calls=%fused_computation.54 | loop fusion | flops 294649856 | bytes 46145536 | tf_op jit(solution)/shard_map/convert_element_type | solution.py:182
  268.0 4.6 fusion.607
  286.0 5.1 convert_reduce_fusion.3
  294.0 6.0 convert_reduce_fusion.1
  306.4 5.2 convert_reduce_fusion.2
  319.2 3.7 bitcast_add_fusion.3
  322.9 4.1 fusion.587
  340.3 4.5 all-to-all-start.13
  345.0 4.8 add_convert_fusion.13
  355.0 3.6 bitcast_add_fusion
  358.6 4.5 convert_reduce_fusion.11
  404.7 4.6 all-to-all-done.9
  426.5 13.0 %add_add_fusion = f32[9,512,512]{2,1,0:T(8,128)} fusion(f32[9,512,512]{2,1,0:T(8,128)} %fusion.52, f32[9,512,512]{2,1,0:T(8,128)} %fusion.61, f32[9,512,512]{2,1,0:T(8,128)S(1)} %fusion.79, f32[9,512,512]{2,1,0:T(8,128)S(1)} %fusion.70), kind=kLoop, calls=%fused_computation | loop fusion | flops 7077888 | bytes 47185920 | tf_op jit(solution)/shard_map/add | solution.py:226
  457.2 41.6 %all-reduce.9 = (f32[512]{0:T(512)}, f32[512]{0:T(512)}, f32[512]{0:T(512)}, f32[2048]{0:T(1024)}, f32[512]{0:T(512)}, /*index=5*/f32[512]{0:T(512)}) all-reduce(f32[512]{0:T(512)} %add_add_fusion.18, f32[512]{0:T(512)} %add_add_fusion.17, f32[512]{0:T(512)} %add_add_fusion.16, ...), channel_id=1, replica_groups=mesh['wide'=4,'narrow'=8] {'wide','narrow'}, use_global_device_ids=true, to_apply=%region_38.39 | all-reduce | flops 4608 | bytes 36864 | tf_op jit(solution)/shard_map/psum | solution.py:238
  509.5 4.1 all-to-all-start.14
  542.6 130.1 %reduce-scatter.7.cloned.1.call-done = f32[9,64,512]{2,1,0:T(8,128)} async-done(((f32[9,512,512]{2,1,0:T(8,128)}), f32[9,64,512]{2,1,0:T(8,128)}) %reduce-scatter.7.cloned.1.call-update) | async-done | bytes 1179664 | tf_op jit(solution)/shard_map/reduce_scatter | solution.py:229
  683.3 4.5 all-to-all-done.16
  687.7 4.1 all-to-all-start.10
  695.5 5.8 all-to-all-done.10
  701.3 4.1 all-to-all-start.12
  718.8 5.2 reduce-scatter.17.cloned.1.call-done
  724.0 28.8 %reduce-scatter.9.cloned.1.call-done = f32[9,64,128]{2,1,0:T(8,128)} async-done(((f32[9,64,512]{2,1,0:T(8,128)}), f32[9,64,128]{2,1,0:T(8,128)}) %reduce-scatter.9.cloned.1.call-update) | async-done | bytes 294928 | tf_op jit(solution)/shard_map/reduce_scatter | solution.py:234
  (844 shorter events, 348.1 us)
Async XLA Ops:
  7.2 192.4 %copy-start = (bf16[512,2048]{1,0:T(8,128)(2,1)S(1)}, bf16[512,2048]{1,0:T(8,128)(2,1)}, u32[]{:S(2)}) copy-start(bf16[512,2048]{1,0:T(8,128)(2,1)} %param.18) | copy-start | bytes 6291460
  18.6 10.5 %all-to-all-start.1 = ((s32[4,1,5120]{2,1,0:T(1,128)}), s32[4,1,5120]{2,1,0:T(1,128)S(1)}, u32[]{:S(2)}, u32[]{:S(2)}) async-start(s32[4,1,5120]{2,1,0:T(1,128)} %reshape.1547), calls=%async_computation.1 | async-start | bytes 163840 | tf_op jit(solution)/shard_map/all_to_all | solution.py:129
  29.2 37.6 %all-to-all-start.5 = ((bf16[2,8,4,8,512]{4,3,1,0,2:T(8,128)(2,1)}), bf16[2,8,4,8,512]{4,3,1,0,2:T(8,128)(2,1)S(1)}, u32[]{:S(2)}, u32[]{:S(2)}) async-start(bf16[2,8,4,8,512]{4,3,1,0,2:T(8,128)(2,1)} %copy.199), calls=%async_computation.5 | async-start | bytes 1048576 | tf_op jit(solution)/shard_map/all_to_all | solution.py:155
  44.9 77.0 %copy-start.155 = (bf16[1,2,32,8]{3,2,1,0:T(8,128)(2,1)}, bf16[1,2,32,8]{3,2,1,0:T(8,128)(2,1)S(1)}, u32[]{:S(2)}) copy-start(bf16[1,2,32,8]{3,2,1,0:T(8,128)(2,1)S(1)} %copy.309) | copy-start | bytes 3076
  45.0 69.6 %copy-start.157 = (bf16[1,2,32,8]{3,2,1,0:T(8,128)(2,1)}, bf16[1,2,32,8]{3,2,1,0:T(8,128)(2,1)S(1)}, u32[]{:S(2)}) copy-start(bf16[1,2,32,8]{3,2,1,0:T(8,128)(2,1)S(1)} %copy.311) | copy-start | bytes 3076
  45.2 73.4 %copy-start.159 = (bf16[1,2,32,8]{3,2,1,0:T(8,128)(2,1)}, bf16[1,2,32,8]{3,2,1,0:T(8,128)(2,1)S(1)}, u32[]{:S(2)}) copy-start(bf16[1,2,32,8]{3,2,1,0:T(8,128)(2,1)S(1)} %copy.308) | copy-start | bytes 3076
  66.8 12.9 %all-to-all-start.7 = ((bf16[2,8,4,8,512]{4,3,1,0,2:T(8,128)(2,1)}), bf16[2,8,4,8,512]{4,3,1,0,2:T(8,128)(2,1)S(1)}, u32[]{:S(2)}, u32[]{:S(2)}) async-start(bf16[2,8,4,8,512]{4,3,1,0,2:T(8,128)(2,1)} %copy.215), calls=%async_computation.7 | async-start | bytes 1048576 | tf_op jit(solution)/shard_map/all_to_all | solution.py:155
  79.7 12.3 %all-to-all-start = ((bf16[2,8,4,8,512]{4,3,1,0,2:T(8,128)(2,1)}), bf16[2,8,4,8,512]{4,3,1,0,2:T(8,128)(2,1)S(1)}, u32[]{:S(2)}, u32[]{:S(2)}) async-start(bf16[2,8,4,8,512]{4,3,1,0,2:T(8,128)(2,1)} %copy.165), calls=%async_computation | async-start | bytes 1048576 | tf_op jit(solution)/shard_map/all_to_all | solution.py:155
  92.0 13.5 %all-to-all-start.3 = ((bf16[2,8,4,8,512]{4,3,1,0,2:T(8,128)(2,1)}), bf16[2,8,4,8,512]{4,3,1,0,2:T(8,128)(2,1)}, u32[]{:S(2)}, u32[]{:S(2)}) async-start(bf16[2,8,4,8,512]{4,3,1,0,2:T(8,128)(2,1)} %copy.183), calls=%async_computation.3 | async-start | bytes 1048576 | tf_op jit(solution)/shard_map/all_to_all | solution.py:155
  105.5 22.9 %all-to-all-start.6 = ((bf16[2,4,8,8,512]{4,3,2,0,1:T(8,128)(2,1)}), bf16[2,4,8,8,512]{4,3,2,0,1:T(8,128)(2,1)S(1)}, u32[]{:S(2)}, u32[]{:S(2)}) async-start(bf16[2,4,8,8,512]{4,3,2,0,1:T(8,128)(2,1)} %copy.210), calls=%async_computation.6 | async-start | bytes 1048576 | tf_op jit(solution)/shard_map/all_to_all | solution.py:166
  128.4 12.4 %all-to-all-start.8 = ((bf16[2,4,8,8,512]{4,3,2,0,1:T(8,128)(2,1)}), bf16[2,4,8,8,512]{4,3,2,0,1:T(8,128)(2,1)S(1)}, u32[]{:S(2)}, u32[]{:S(2)}) async-start(bf16[2,4,8,8,512]{4,3,2,0,1:T(8,128)(2,1)} %copy.226), calls=%async_computation.8 | async-start | bytes 1048576 | tf_op jit(solution)/shard_map/all_to_all | solution.py:166
  141.7 12.9 %all-to-all-start.2 = ((bf16[2,4,8,8,512]{4,3,2,0,1:T(8,128)(2,1)}), bf16[2,4,8,8,512]{4,3,2,0,1:T(8,128)(2,1)S(1)}, u32[]{:S(2)}, u32[]{:S(2)}) async-start(bf16[2,4,8,8,512]{4,3,2,0,1:T(8,128)(2,1)} %copy.178), calls=%async_computation.2 | async-start | bytes 1048576 | tf_op jit(solution)/shard_map/all_to_all | solution.py:166
  154.6 26.4 %all-to-all-start.4 = ((bf16[2,4,8,8,512]{4,3,2,0,1:T(8,128)(2,1)}), bf16[2,4,8,8,512]{4,3,2,0,1:T(8,128)(2,1)}, u32[]{:S(2)}, u32[]{:S(2)}) async-start(bf16[2,4,8,8,512]{4,3,2,0,1:T(8,128)(2,1)} %copy.194), calls=%async_computation.4 | async-start | bytes 1048576 | tf_op jit(solution)/shard_map/all_to_all | solution.py:166
  158.7 371.5 %reduce-scatter.11.cloned.1.call-start = ((), (), s32[]{:S(2)}) async-start(), calls=%async_computation.25 | async-start | bytes 4718592 | tf_op jit(solution)/shard_map/reduce_scatter | solution.py:230
  199.6 103.4 %copy-start.2 = (f32[2,256,512]{2,1,0:T(8,128)}, f32[2,256,512]{2,1,0:T(8,128)S(1)}, u32[]{:S(2)}) copy-start(f32[2,256,512]{2,1,0:T(8,128)S(1)} %get-tuple-element.109) | copy-start | bytes 3145732
  340.3 24.6 %all-to-all-start.13 = ((bf16[2,8,4,8,512]{4,3,1,0,2:T(8,128)(2,1)}), bf16[2,8,4,8,512]{4,3,1,0,2:T(8,128)(2,1)}, u32[]{:S(2)}, u32[]{:S(2)}) async-start(bf16[2,8,4,8,512]{4,3,1,0,2:T(8,128)(2,1)} %copy.255), calls=%async_computation.13 | async-start | bytes 1048576 | tf_op jit(solution)/shard_map/all_to_all | solution.py:205
  344.9 192.0 %reduce-scatter.15.cloned.1.call-start = ((), (), s32[]{:S(2)}) async-start(), calls=%async_computation.27 | async-start | bytes 4718592 | tf_op jit(solution)/shard_map/reduce_scatter | solution.py:231
  364.9 16.0 %all-to-all-start.15 = ((bf16[2,8,4,8,512]{4,3,1,0,2:T(8,128)(2,1)}), bf16[2,8,4,8,512]{4,3,1,0,2:T(8,128)(2,1)S(1)}, u32[]{:S(2)}, u32[]{:S(2)}) async-start(bf16[2,8,4,8,512]{4,3,1,0,2:T(8,128)(2,1)} %copy.267), calls=%async_computation.15 | async-start | bytes 1048576 | tf_op jit(solution)/shard_map/all_to_all | solution.py:205
  380.9 16.0 %all-to-all-start.11 = ((bf16[2,8,4,8,512]{4,3,1,0,2:T(8,128)(2,1)}), bf16[2,8,4,8,512]{4,3,1,0,2:T(8,128)(2,1)S(1)}, u32[]{:S(2)}, u32[]{:S(2)}) async-start(bf16[2,8,4,8,512]{4,3,1,0,2:T(8,128)(2,1)} %copy.243), calls=%async_computation.11 | async-start | bytes 1048576 | tf_op jit(solution)/shard_map/all_to_all | solution.py:205
  397.0 12.3 %all-to-all-start.9 = ((bf16[2,8,4,8,512]{4,3,1,0,2:T(8,128)(2,1)}), bf16[2,8,4,8,512]{4,3,1,0,2:T(8,128)(2,1)S(1)}, u32[]{:S(2)}, u32[]{:S(2)}) async-start(bf16[2,8,4,8,512]{4,3,1,0,2:T(8,128)(2,1)} %copy.231), calls=%async_computation.9 | async-start | bytes 1048576 | tf_op jit(solution)/shard_map/all_to_all | solution.py:205
  400.4 272.3 %reduce-scatter.7.cloned.1.call-start = ((), (), s32[]{:S(2)}) async-start(), calls=%async_computation.23 | async-start | bytes 10616832 | tf_op jit(solution)/shard_map/reduce_scatter | solution.py:229
  439.6 59.2 %copy-start.152 = (bf16[2,256,512]{2,1,0:T(8,128)(2,1)S(1)}, bf16[2,256,512]{2,1,0:T(8,128)(2,1)}, u32[]{:S(2)}) copy-start(bf16[2,256,512]{2,1,0:T(8,128)(2,1)} %get-tuple-element.120) | copy-start | bytes 1572868
  439.7 62.2 %copy-start.162 = (bf16[1,2,32,8]{3,2,1,0:T(8,128)(2,1)S(1)}, bf16[1,2,32,8]{3,2,1,0:T(8,128)(2,1)}, u32[]{:S(2)}) copy-start(bf16[1,2,32,8]{3,2,1,0:T(8,128)(2,1)} %copy-done.161) | copy-start | bytes 3076
  444.0 60.7 %slice-start.4 = ((s8[4718592]{0:T(1024)(128)(4,1)}), s8[524288]{0:T(1024)(128)(4,1)S(1)}, s32[]{:S(2)}) async-start(s8[4718592]{0:T(1024)(128)(4,1)} %bitcast.1007), calls=%async_computation.33 | async-start | bytes 1048576
  509.5 165.8 %all-to-all-start.14 = ((bf16[2,4,8,8,512]{4,3,2,0,1:T(8,128)(2,1)}), bf16[2,4,8,8,512]{4,3,2,0,1:T(8,128)(2,1)}, u32[]{:S(2)}, u32[]{:S(2)}) async-start(bf16[2,4,8,8,512]{4,3,2,0,1:T(8,128)(2,1)} %copy.265), calls=%async_computation.14 | async-start | bytes 1048576 | tf_op jit(solution)/shard_map/all_to_all | solution.py:218
  513.7 205.1 %reduce-scatter.13.cloned.1.call-start = ((), (), s32[]{:S(2)}) async-start(), calls=%async_computation.26 | async-start | bytes 655360 | tf_op jit(solution)/shard_map/reduce_scatter | solution.py:235
  530.3 193.8 %reduce-scatter.17.cloned.1.call-start = ((), (), s32[]{:S(2)}) async-start(), calls=%async_computation.28 | async-start | bytes 655360 | tf_op jit(solution)/shard_map/reduce_scatter | solution.py:236
  536.9 215.9 %reduce-scatter.9.cloned.1.call-start = ((), (), s32[]{:S(2)}) async-start(), calls=%async_computation.24 | async-start | bytes 1474560 | tf_op jit(solution)/shard_map/reduce_scatter | solution.py:234
  540.3 138.7 %copy-start.202 = (bf16[2,32,8]{2,1,0:T(8,128)(2,1)S(1)}, bf16[2,32,8]{2,1,0:T(8,128)(2,1)}, u32[]{:S(2)}) copy-start(bf16[2,32,8]{2,1,0:T(8,128)(2,1)} %copy.240) | copy-start | bytes 3076
  675.3 12.4 %all-to-all-start.16 = ((bf16[2,4,8,8,512]{4,3,2,0,1:T(8,128)(2,1)}), bf16[2,4,8,8,512]{4,3,2,0,1:T(8,128)(2,1)S(1)}, u32[]{:S(2)}, u32[]{:S(2)}) async-start(bf16[2,4,8,8,512]{4,3,2,0,1:T(8,128)(2,1)} %copy.277), calls=%async_computation.16 | async-start | bytes 1048576 | tf_op jit(solution)/shard_map/all_to_all | solution.py:218
  687.7 13.5 %all-to-all-start.10 = ((bf16[2,4,8,8,512]{4,3,2,0,1:T(8,128)(2,1)}), bf16[2,4,8,8,512]{4,3,2,0,1:T(8,128)(2,1)}, u32[]{:S(2)}, u32[]{:S(2)}) async-start(bf16[2,4,8,8,512]{4,3,2,0,1:T(8,128)(2,1)} %copy.241), calls=%async_computation.10 | async-start | bytes 1048576 | tf_op jit(solution)/shard_map/all_to_all | solution.py:218
  701.3 13.1 %all-to-all-start.12 = ((bf16[2,4,8,8,512]{4,3,2,0,1:T(8,128)(2,1)}), bf16[2,4,8,8,512]{4,3,2,0,1:T(8,128)(2,1)}, u32[]{:S(2)}, u32[]{:S(2)}) async-start(bf16[2,4,8,8,512]{4,3,2,0,1:T(8,128)(2,1)} %copy.253), calls=%async_computation.12 | async-start | bytes 1048576 | tf_op jit(solution)/shard_map/all_to_all | solution.py:218
  (216 other events, 1334.6 us)
Sparse Core Ops, SparseCore 0:
  323.0 90.1 reduce-scatter.10
  417.3 88.3 reduce-scatter.14
  509.2 163.4 reduce-scatter.6
  675.7 21.2 reduce-scatter.12
  700.0 23.9 reduce-scatter.16
  727.0 25.7 reduce-scatter.8
where the time goes:
time: 772 us; the launch traced here: 760 us
  waiting for transfers between devices  195 us (25%)
  matrix products  182 us (24%)
  other arithmetic  159 us (21%)
  local copies, waits for them, and re-layouts  98.4 us (13%)
  starting transfers between devices  65.9 us (9%)
  blocking collectives  41.6 us (5%)
  between operations  18.4 us (2%)
    reduce_scatter x1, waiting for transfers between devices, body(): lax.psum_scatter(acc_conv, 'narrow', scatter_dimension=1, tiled=True)  130 us
    dot_general x36, matrix products, conv_backward(): lax.dot_general(source_rows.reshape(-1, features), flat_grad, (((0,), (0,...  43.2 us
    convert_element_type x1, other arithmetic, body(): act_low = activated.astype(jnp.bfloat16)  42.3 us
    psum x1, blocking collectives, body(): lax.psum((acc_conv_b, acc_gain_one, acc_bias_one, acc_b_in, acc_gain_two,...  41.6 us
    dot_general x36, matrix products, conv_backward(): jnp.einsum('...d,cd->...c', spread_grad, conv_w[tap_number], preferred_el...  37.5 us
    reduce_scatter x1, waiting for transfers between devices, body(): lax.psum_scatter(partial_sums[0], 'wide', scatter_dimension=2, tiled=True)  28.8 us
    dot_general x36, matrix products, conv_forward(): jnp.einsum('...c,cd->...d', source_rows, conv_w[tap_number], preferred_el...  24.8 us
    unnamed x452, local copies, waits for them, and re-layouts  22.2 us
  transfers between devices with their start and end apart: 23, of which 10 were waited for; matrix products, arithmetic and copies ran while one was open for 37% of the time, Pallas kernels for 0%

commit v1 on v0

v1 whole, which is shorter than its diff:
```python
import functools

import jax
import jax.numpy as jnp
from jax import lax
from jax.experimental import pallas as pl
from jax.experimental.pallas import tpu as pltpu
from jax.sharding import PartitionSpec as P

STEP = 32
BF = jnp.bfloat16
F32 = jnp.float32
RSQRT2 = 0.7071067811865476
RSQRT2PI = 0.3989422804014327
EPS = 1e-05
VMEM_LIMIT = 56 * 1024 * 1024


def params():
    return pltpu.CompilerParams(vmem_limit_bytes=VMEM_LIMIT)


def cost(flops, moved, transcendentals=0):
    return pl.CostEstimate(
        flops=int(flops), bytes_accessed=int(moved), transcendentals=int(transcendentals)
    )


def whole(shape):
    rank = len(shape)
    return pl.BlockSpec(shape, lambda *_: (0,) * rank, pipeline_mode=pl.Buffered(1))


def shape(dims, dtype):
    return jax.ShapeDtypeStruct(dims, dtype)


def mask_columns(matched):
    return jnp.where(matched, 1.0, 0.0).astype(F32).T


def spread(column, width):
    wide = jnp.broadcast_to(column, (column.shape[0], 128)).astype(BF)
    return jnp.concatenate([wide] * (width // 128), axis=1)


def dot(left, right, left_dim, right_dim):
    return lax.dot_general(
        left, right, (((left_dim,), (right_dim,)), ((), ())), preferred_element_type=F32
    )


def cdf_and_exp(values):
    return 0.5 + 0.5 * lax.erf(values * RSQRT2), jnp.exp(-0.5 * values * values)


def fold(values):
    return values.reshape(-1, 8, values.shape[-1]).sum(0)


def conv_inner_kernel(info_ref, x_ref, w_ref, acc_ref):
    tap = pl.program_id(0)
    rows, own, features = x_ref.shape
    taps = info_ref.shape[0] - 1
    half = taps // 2
    ids = info_ref[0]

    def run(k):
        shift = STEP * (k - half)
        low, high = max(0, -shift), own - max(0, shift)
        matched = (ids[:, low + shift : high + shift] == ids[:, low:high]) & (
            info_ref[1 + k][:, low:high] == 1
        )
        columns = mask_columns(matched)
        lhs = jnp.concatenate(
            [
                x_ref[r, low + shift : high + shift, :] * spread(columns[:, r : r + 1], features)
                for r in range(rows)
            ],
            axis=0,
        )
        product = dot(lhs, w_ref[0], 1, 0).reshape(rows, high - low, features)
        if k == half:
            acc_ref[...] = product
        else:
            acc_ref[:, low:high, :] += product

    for k in range(taps):
        place = 0 if k == half else (k + 1 if k < half else k)
        pl.when(tap == place)(functools.partial(run, k))


def conv_inner(info, x, conv_w):
    rows, own, features = x.shape
    taps = conv_w.shape[0]
    half = taps // 2

    def tap_of(i):
        return jnp.where(i == 0, half, jnp.where(i <= half, i - 1, i))

    return pl.pallas_call(
        conv_inner_kernel,
        grid=(taps,),
        in_specs=[
            whole(info.shape),
            whole(x.shape),
            pl.BlockSpec((1, features, features), lambda i: (tap_of(i), 0, 0)),
        ],
        out_specs=whole(x.shape),
        out_shape=shape(x.shape, F32),
        compiler_params=params(),
        cost_estimate=cost(2 * rows * own * features * features * taps * 0.72, 11e6),
        name="conv_inner",
    )(info, x, conv_w)


def place_block(out_ref, value, dest_wide, dest_narrow, rows_at, blocks):
    if blocks == (1, 1):
        out_ref[0, 0, rows_at, :] = value
        return
    rel_wide = lax.axis_index("wide") ^ dest_wide
    rel_narrow = lax.axis_index("narrow") ^ dest_narrow
    index = (rel_wide >> 1) * 8 + (rel_narrow & 1) * 4 + (rel_narrow >> 1)
    out_ref[rel_wide & 1, index, rows_at, :] = value


def ship(scratch, keep_ref, send_ref, sems):
    first = pltpu.make_async_copy(scratch.at[0], keep_ref, sems.at[0])
    second = pltpu.make_async_copy(scratch.at[1], send_ref, sems.at[1])
    first.start()
    second.start()
    first.wait()
    second.wait()


def forward_kernel(
    blocks,
    info_ref, acc_ref, left_ref, right_ref, x_ref, ct_ref, conv_w_ref, w_in_ref, w_out_ref,
    vec_ref, b_in_ref,
    out_ref, low_ref, hidden_ref, gproj_ref, slope_ref, gain_ref, bias_ref, *rest,
):
    if blocks == (1, 1):
        gw_ref, halo_acc, act_scr, gp_scr = rest
    else:
        keep_ref, send_ref, halo_acc, act_scr, gp_scr, gw_ref, sems = rest
    step = pl.program_id(0)
    steps = pl.num_programs(0)
    rows, own, features = halo_acc.shape
    taps = info_ref.shape[0] - 1
    half = taps // 2
    reach = STEP * half
    block_rows = x_ref.shape[0]
    size = block_rows * own
    hidden_units = w_in_ref.shape[1]

    @pl.when(step == 0)
    def _():
        gain_ref[...] = jnp.zeros_like(gain_ref)
        bias_ref[...] = jnp.zeros_like(bias_ref)
        ids = info_ref[0]
        for side in (0, 1):
            halo = left_ref if side == 0 else right_ref
            for d in range(half, 0, -1):
                k = half - d if side == 0 else half + d
                n = STEP * d
                shift = STEP * (k - half)
                low = 0 if side == 0 else own - n
                source = reach - n if side == 0 else 0
                near = info_ref[1 + k][:, reach + low : reach + low + n] == 1
                matched = near & (
                    ids[:, reach + low + shift : reach + low + shift + n]
                    == ids[:, reach + low : reach + low + n]
                )
                columns = mask_columns(matched)
                lhs = jnp.concatenate(
                    [
                        halo[r, source : source + n, :] * spread(columns[:, r : r + 1], features)
                        for r in range(rows)
                    ],
                    axis=0,
                )
                product = dot(lhs, conv_w_ref[k], 1, 0).reshape(rows, n, features)
                if d == half:
                    halo_acc[:, low : low + n, :] = product
                else:
                    halo_acc[:, low : low + n, :] += product

    conv_bias = vec_ref[0:1, :]
    gain_one = vec_ref[1:2, :]
    bias_one = vec_ref[2:3, :]
    gain_two = vec_ref[3:4, :]
    bias_two = vec_ref[4:5, :]
    at = pl.ds(step * block_rows, block_rows)
    span = pl.ds(step * size, size)
    conv = (acc_ref[...] + halo_acc[at, :, :]).reshape(size, features)
    hidden = (conv + conv_bias).astype(BF)
    hidden_ref[...] = hidden.reshape(hidden_ref.shape)
    hid = hidden.astype(F32)
    act = hid * (0.5 + 0.5 * lax.erf(hid * RSQRT2))
    centered = act - jnp.mean(act, axis=1, keepdims=True)
    scale = lax.rsqrt(jnp.mean(centered * centered, axis=1, keepdims=True) + EPS)
    mixed = x_ref[...].reshape(size, features).astype(F32) + (
        centered * scale * gain_one + bias_one
    )
    mixed_low = mixed.astype(BF)
    low_ref[...] = mixed_low.reshape(low_ref.shape)
    chunk = 512
    projected = None
    for j in range(hidden_units // chunk):
        cols = slice(j * chunk, (j + 1) * chunk)
        up = dot(mixed_low, w_in_ref[:, cols], 1, 0) + b_in_ref[:, cols]
        cdf, bell = cdf_and_exp(up)
        act_low = (up * cdf).astype(BF)
        slope_ref[:, cols] = (cdf + up * bell * RSQRT2PI).astype(BF)
        act_scr[span, cols] = act_low
        part = dot(act_low, w_out_ref[cols, :], 1, 0)
        projected = part if projected is None else projected + part
    centered = projected - jnp.mean(projected, axis=1, keepdims=True)
    scale = lax.rsqrt(jnp.mean(centered * centered, axis=1, keepdims=True) + EPS)
    xhat = centered * scale
    out_ref[...] = (mixed + (xhat * gain_two + bias_two)).astype(BF).reshape(out_ref.shape)
    ct = ct_ref[...].reshape(size, features).astype(F32)
    ct_xhat = ct * xhat
    gain_ref[...] += fold(ct_xhat)
    bias_ref[...] += fold(ct)
    e = ct * gain_two
    mean_e = jnp.mean(e, axis=1, keepdims=True)
    mean_ex = jnp.mean(e * xhat, axis=1, keepdims=True)
    gproj = (scale * (e - mean_e - xhat * mean_ex)).astype(BF)
    gproj_ref[...] = gproj
    gp_scr[span, :] = gproj

    @pl.when(step == steps - 1)
    def _():
        n_wide, n_narrow = blocks
        height, width = hidden_units // n_narrow, features // n_wide
        for n in range(n_narrow):
            product = dot(act_scr[:, n * height : (n + 1) * height], gp_scr[...], 0, 0).astype(BF)
            for w in range(n_wide):
                place_block(
                    gw_ref, product[:, w * width : (w + 1) * width], w, n, slice(0, height), blocks
                )
        if blocks != (1, 1):
            ship(gw_ref, keep_ref, send_ref, sems)


def gradient_outputs(blocks, height, width):
    if blocks == (1, 1):
        dims = (1, 1, height, width)
        return [shape(dims, BF)], [whole(dims)], []
    n_wide, n_narrow = blocks
    dims = (n_wide * n_narrow // 2, height // n_narrow, width // n_wide)
    return (
        [shape(dims, BF)] * 2,
        [pl.BlockSpec(memory_space=pl.ANY)] * 2,
        [pltpu.VMEM((2,) + dims, BF), pltpu.SemaphoreType.DMA((2,))],
    )


def forward(blocks, info, acc, left, right, x, ct, conv_w, w_in, w_out, vec, b_in):
    rows, own, features = x.shape
    hidden_units = w_in.shape[1]
    block_rows = 2
    steps = rows // block_rows
    size = block_rows * own
    total = rows * own
    row_block = pl.BlockSpec((block_rows, own, features), lambda i: (i, 0, 0))
    shapes, specs, scratch = gradient_outputs(blocks, hidden_units, features)
    return pl.pallas_call(
        functools.partial(forward_kernel, blocks),
        grid=(steps,),
        in_specs=[
            whole(info.shape), row_block, whole(left.shape), whole(right.shape), row_block,
            row_block, whole(conv_w.shape), whole(w_in.shape), whole(w_out.shape),
            whole(vec.shape), whole(b_in.shape),
        ],
        out_specs=[
            row_block, row_block, row_block,
            pl.BlockSpec((size, features), lambda i: (i, 0)),
            pl.BlockSpec((size, hidden_units), lambda i: (i, 0)),
            whole((8, features)), whole((8, features)),
        ] + specs,
        out_shape=[
            shape(x.shape, BF), shape(x.shape, BF), shape(x.shape, BF),
            shape((total, features), BF), shape((total, hidden_units), BF),
            shape((8, features), F32), shape((8, features), F32),
        ] + shapes,
        scratch_shapes=[
            pltpu.VMEM(x.shape, F32), pltpu.VMEM((total, hidden_units), BF),
            pltpu.VMEM((total, features), BF),
        ] + scratch,
        compiler_params=params(),
        cost_estimate=cost(2 * total * features * (3 * hidden_units + 2.5 * features), 40e6),
        name="forward",
    )(info, acc, left, right, x, ct, conv_w, w_in, w_out, vec, b_in)


def backward_kernel(
    blocks,
    gproj_ref, slope_ref, low_ref, hidden_ref, ct_ref, w_in_ref, w_out_ref, vec_ref,
    gmixed_ref, gh_ref, b_in_ref, gain_ref, bias_ref, conv_b_ref, *rest,
):
    if blocks == (1, 1):
        gw_ref, up_scr, low_scr = rest
    else:
        keep_ref, send_ref, up_scr, low_scr, gw_ref, sems = rest
    step = pl.program_id(0)
    steps = pl.num_programs(0)
    size = gproj_ref.shape[0]
    features = low_ref.shape[-1]
    hidden_units = w_in_ref.shape[1]

    @pl.when(step == 0)
    def _():
        for ref in (b_in_ref, gain_ref, bias_ref, conv_b_ref):
            ref[...] = jnp.zeros_like(ref)

    span = pl.ds(step * size, size)
    gain_one = vec_ref[1:2, :]
    gproj = gproj_ref[...]
    chunk = 512
    total = None
    for j in range(hidden_units // chunk):
        cols = slice(j * chunk, (j + 1) * chunk)
        g_act = dot(gproj, w_out_ref[cols, :], 1, 1)
        up_low = (g_act * slope_ref[:, cols].astype(F32)).astype(BF)
        up_scr[span, cols] = up_low
        b_in_ref[:, cols] += fold(up_low.astype(F32))
        part = dot(up_low, w_in_ref[:, cols], 1, 1)
        total = part if total is None else total + part
    mixed_low = low_ref[...].reshape(size, features)
    low_scr[span, :] = mixed_low
    g_mixed = ct_ref[...].reshape(size, features).astype(F32) + total
    gmixed_ref[...] = g_mixed.reshape(gmixed_ref.shape)
    hid = hidden_ref[...].reshape(size, features).astype(F32)
    cdf, bell = cdf_and_exp(hid)
    act = hid * cdf
    centered = act - jnp.mean(act, axis=1, keepdims=True)
    scale = lax.rsqrt(jnp.mean(centered * centered, axis=1, keepdims=True) + EPS)
    yhat = centered * scale
    gain_ref[...] += fold(g_mixed * yhat)
    bias_ref[...] += fold(g_mixed)
    e = g_mixed * gain_one
    mean_e = jnp.mean(e, axis=1, keepdims=True)
    mean_ey = jnp.mean(e * yhat, axis=1, keepdims=True)
    g_hidden = scale * (e - mean_e - yhat * mean_ey) * (cdf + hid * bell * RSQRT2PI)
    g_low = g_hidden.astype(BF)
    gh_ref[...] = g_low.reshape(gh_ref.shape)
    conv_b_ref[...] += fold(g_low.astype(F32))

    @pl.when(step == steps - 1)
    def _():
        n_wide, n_narrow = blocks
        height, width = features // n_narrow, hidden_units // n_wide
        for w in range(n_wide):
            product = dot(low_scr[...], up_scr[:, w * width : (w + 1) * width], 0, 0).astype(BF)
            for n in range(n_narrow):
                place_block(
                    gw_ref, product[n * height : (n + 1) * height, :], w, n, slice(0, height), blocks
                )
        if blocks != (1, 1):
            ship(gw_ref, keep_ref, send_ref, sems)


def backward(blocks, gproj, slope, mixed_low, hidden, ct, w_in, w_out, vec):
    rows, own, features = hidden.shape
    hidden_units = w_in.shape[1]
    block_rows = 2
    steps = rows // block_rows
    size = block_rows * own
    total = rows * own
    row_block = pl.BlockSpec((block_rows, own, features), lambda i: (i, 0, 0))
    shapes, specs, scratch = gradient_outputs(blocks, features, hidden_units)
    return pl.pallas_call(
        functools.partial(backward_kernel, blocks),
        grid=(steps,),
        in_specs=[
            pl.BlockSpec((size, features), lambda i: (i, 0)),
            pl.BlockSpec((size, hidden_units), lambda i: (i, 0)),
            row_block, row_block, row_block, whole(w_in.shape), whole(w_out.shape),
            whole(vec.shape),
        ],
        out_specs=[
            row_block, row_block, whole((8, hidden_units)), whole((8, features)),
            whole((8, features)), whole((8, features)),
        ] + specs,
        out_shape=[
            shape(hidden.shape, F32), shape(hidden.shape, BF), shape((8, hidden_units), F32),
            shape((8, features), F32), shape((8, features), F32), shape((8, features), F32),
        ] + shapes,
        scratch_shapes=[
            pltpu.VMEM((total, hidden_units), BF), pltpu.VMEM((total, features), BF),
        ] + scratch,
        compiler_params=params(),
        cost_estimate=cost(2 * total * features * 3 * hidden_units, 30e6),
        name="backward",
    )(gproj, slope, mixed_low, hidden, ct, w_in, w_out, vec)


def weight_kernel(blocks, info_ref, x_ref, left_ref, right_ref, gh_ref, *rest):
    if blocks == (1, 1):
        gw_ref, ext = rest
    else:
        keep_ref, send_ref, ext, gw_ref, sems = rest
    tap = pl.program_id(0)
    taps = pl.num_programs(0)
    rows, own, features = x_ref.shape
    reach = left_ref.shape[1]

    @pl.when(tap == 0)
    def _():
        ext[:, 0:reach, :] = left_ref[...]
        ext[:, reach : reach + own, :] = x_ref[...]
        ext[:, reach + own : own + 2 * reach, :] = right_ref[...]

    ids = info_ref[0]
    whole_row = own + 2 * reach
    moved = pltpu.roll(ids, whole_row - STEP * tap, 1)[:, :own]
    matched = (moved == ids[:, reach : reach + own]) & (
        info_ref[1 + tap][:, reach : reach + own] == 1
    )
    columns = mask_columns(matched)
    at = pl.ds(pl.multiple_of(STEP * tap, STEP), own)
    lhs = jnp.concatenate(
        [ext[r, at, :] * spread(columns[:, r : r + 1], features) for r in range(rows)], axis=0
    )
    product = dot(lhs, gh_ref[...].reshape(rows * own, features), 0, 0).astype(BF)
    n_wide, n_narrow = blocks
    height, width = features // n_narrow, features // n_wide
    rows_at = pl.ds(pl.multiple_of(tap * height, height), height)
    for n in range(n_narrow):
        for w in range(n_wide):
            place_block(
                gw_ref,
                product[n * height : (n + 1) * height, w * width : (w + 1) * width],
                w, n, rows_at, blocks,
            )

    if blocks != (1, 1):

        @pl.when(tap == taps - 1)
        def _():
            ship(gw_ref, keep_ref, send_ref, sems)


def weight_gradient(blocks, info, x, left, right, gh, taps):
    rows, own, features = x.shape
    reach = left.shape[1]
    shapes, specs, scratch = gradient_outputs(blocks, taps * features, features)
    return pl.pallas_call(
        functools.partial(weight_kernel, blocks),
        grid=(taps,),
        in_specs=[whole(v.shape) for v in (info, x, left, right, gh)],
        out_specs=specs,
        out_shape=shapes,
        scratch_shapes=[pltpu.VMEM((rows, own + 2 * reach, features), BF)] + scratch,
        compiler_params=params(),
        cost_estimate=cost(2 * rows * own * features * features * taps, 12e6),
        name="weight_gradient",
    )(info, x, left, right, gh)


def input_kernel(info_ref, gmixed_ref, gh_ref, left_ref, right_ref, wt_ref, gx_ref, patches):
    block_rows, own, features = gh_ref.shape
    reach = left_ref.shape[1]
    taps = info_ref.shape[1] - 1
    for r in range(block_rows):
        ids = info_ref[r, 0:1, :]
        matched = []
        for k in range(taps):
            start = STEP * (taps - 1 - k)
            same = (ids[:, start : start + own] == ids[:, reach : reach + own]) & (
                info_ref[r, 1 + k : 2 + k, start : start + own] == 1
            )
            matched.append(jnp.where(same, 1.0, 0.0).astype(F32))
        matched.append(jnp.zeros((16 - taps, own), F32))
        columns = jnp.concatenate(matched, axis=0).T
        for k in range(taps):
            start = STEP * (taps - 1 - k)
            mask = spread(columns[:, k : k + 1], features)
            cols = slice(k * features, (k + 1) * features)
            base = r * own
            if start < reach:
                n = reach - start
                patches[base : base + n, cols] = left_ref[r, start:reach, :] * mask[:n]
                patches[base + n : base + own, cols] = gh_ref[r, : own - n, :] * mask[n:]
            elif start == reach:
                patches[base : base + own, cols] = gh_ref[r] * mask
            else:
                n = own - (start - reach)
                patches[base : base + n, cols] = gh_ref[r, start - reach :, :] * mask[:n]
                patches[base + n : base + own, cols] = right_ref[r, : own - n, :] * mask[n:]
    g_in = dot(patches[...], wt_ref[...], 1, 0).astype(BF).astype(F32)
    gx_ref[...] = gmixed_ref[...] + g_in.reshape(gx_ref.shape)


def input_gradient(info, gmixed, gh, left, right, wt):
    rows, own, features = gh.shape
    reach = left.shape[1]
    block_rows = 2
    row_block = pl.BlockSpec((block_rows, own, features), lambda i: (i, 0, 0))
    halo_block = pl.BlockSpec((block_rows, reach, features), lambda i: (i, 0, 0))
    return pl.pallas_call(
        input_kernel,
        grid=(rows // block_rows,),
        in_specs=[
            pl.BlockSpec((block_rows,) + info.shape[1:], lambda i: (i, 0, 0)),
            row_block, row_block, halo_block, halo_block, whole(wt.shape),
        ],
        out_specs=row_block,
        out_shape=shape(gh.shape, F32),
        scratch_shapes=[pltpu.VMEM((block_rows * own, wt.shape[0]), BF)],
        compiler_params=params(),
        cost_estimate=cost(2 * rows * own * wt.shape[0] * features, 18e6),
        name="input_gradient",
    )(info, gmixed, gh, left, right, wt)


def flip(value, axis, bit):
    size = lax.axis_size(axis)
    return lax.ppermute(value, axis, [(i, i ^ bit) for i in range(size)])


def add(a, b):
    return a.astype(F32) + b.astype(F32)


def after_core_kernel(keep, got, a_keep, a_send, b_keep, b_send):
    rows = keep.shape[1] // 2
    for y in range(2):
        for x in range(2):
            src = slice(8 * y + 4 * x, 8 * y + 4 * x + 4)
            top = add(keep[src, :rows, :], got[src, :rows, :]).astype(BF)
            (a_send if x else a_keep)[4 * y : 4 * y + 4] = top
            bottom = add(keep[src, rows:, :], got[src, rows:, :]).astype(BF)
            (b_send if y else b_keep)[4 * x : 4 * x + 4] = bottom


def after_first_kernel(a_keep, a_got, b_keep, b_got, a_next, a_send, b_next, b_send):
    for keep, got, stay, send in ((a_keep, a_got, a_next, a_send), (b_keep, b_got, b_next, b_send)):
        stay[...] = add(keep[:4], got[:4]).astype(BF)
        send[...] = add(keep[4:], got[4:]).astype(BF)


def after_second_kernel(a_keep, a_got, b_keep, b_got, z0, z1, z2, z3):
    rows = a_keep.shape[1]
    for i, ref in enumerate((z0, z1, z2, z3)):
        ref[:rows, :] = add(a_keep[i], a_got[i]).astype(BF)
        ref[rows:, :] = add(b_keep[i], b_got[i]).astype(BF)


def last_kernel(z0, z1, z2, z3, out):
    out[...] = add(z0[...], z1[...]) + add(z2[...], z3[...])


def small(kernel, operands, dims, dtype=BF):
    moved = sum(v.size * v.dtype.itemsize for v in operands) * 2
    return pl.pallas_call(
        kernel,
        out_shape=[shape(d, dtype) for d in dims],
        compiler_params=params(),
        cost_estimate=cost(moved / 2, moved),
        name=kernel.__name__,
    )(*operands)


def scatter_sum(keep, send):
    _, rows, width = keep.shape
    got = flip(send, "wide", 1)
    half = (8, rows // 2, width)
    a_keep, a_send, b_keep, b_send = small(after_core_kernel, (keep, got), [half] * 4)
    a_got, b_got = flip(a_send, "narrow", 1), flip(b_send, "wide", 2)
    quarter = (4, rows // 2, width)
    a_keep, a_send, b_keep, b_send = small(
        after_first_kernel, (a_keep, a_got, b_keep, b_got), [quarter] * 4
    )
    a_got, b_got = flip(a_send, "wide", 2), flip(b_send, "narrow", 1)
    z = small(after_second_kernel, (a_keep, a_got, b_keep, b_got), [(rows, width)] * 4)
    others = [flip(z[i], "narrow", 2 * i) for i in (1, 2, 3)]
    return small(last_kernel, (z[0], *others), [(rows, width)], F32)[0]


def body(
    inputs, conv_w, conv_b, ln1_gain, ln1_bias, w_in, b_in, w_out, ln2_gain, ln2_bias,
    segments, tap_mask, cotangent,
):
    rows, own, features = inputs.shape
    taps = conv_w.shape[0]
    reach = STEP * (taps // 2)
    hidden_units = w_in.shape[1]
    n_wide, n_narrow = lax.axis_size("wide"), lax.axis_size("narrow")
    by_hand = (n_wide, n_narrow) == (4, 8)
    blocks = (4, 8) if by_hand else (1, 1)

    to_right = [(i, i + 1) for i in range(n_wide - 1)]
    to_left = [(i + 1, i) for i in range(n_wide - 1)]

    def halos(value, dim):
        last = value.shape[dim]
        left = lax.ppermute(lax.slice_in_dim(value, last - reach, last, axis=dim), "wide", to_right)
        right = lax.ppermute(lax.slice_in_dim(value, 0, reach, axis=dim), "wide", to_left)
        return left, right

    info = jnp.concatenate([segments[None] + 1, jnp.transpose(tap_mask, (1, 0, 2))], axis=0)
    info_left, info_right = halos(info, 2)
    x_left, x_right = halos(inputs, 1)
    info_ext = jnp.concatenate([info_left, info, info_right], axis=2)
    info_rows = jnp.transpose(info_ext, (1, 0, 2))
    vec = jnp.stack([conv_b, ln1_gain, ln1_bias, ln2_gain, ln2_bias]).astype(F32)
    vec = jnp.pad(vec, ((0, 3), (0, 0)))
    wt = jnp.transpose(conv_w, (0, 2, 1)).reshape(taps * features, features)

    acc = conv_inner(info, inputs, conv_w)
    out, mixed_low, hidden, gproj, slope, gain_two, bias_two, *gw_out = forward(
        blocks, info_ext, acc, x_left, x_right, inputs, cotangent, conv_w, w_in, w_out, vec,
        b_in.astype(F32)[None],
    )
    gmixed, gh, gb_in, gain_one, bias_one, gconv_b, *gw_in = backward(
        blocks, gproj, slope, mixed_low, hidden, cotangent, w_in, w_out, vec
    )
    gh_left, gh_right = halos(gh, 1)
    gconv = weight_gradient(blocks, info_ext, inputs, x_left, x_right, gh, taps)
    grad_inputs = input_gradient(info_rows, gmixed, gh, gh_left, gh_right, wt)

    if by_hand:
        grad_w_out = scatter_sum(*gw_out)
        grad_w_in = scatter_sum(*gw_in)
        grad_conv = scatter_sum(*gconv).reshape(taps, features // n_narrow, features // n_wide)
    else:

        def reduce(value, dims, wide_dim, narrow_dim):
            value = lax.psum_scatter(
                value.reshape(dims), "narrow", scatter_dimension=narrow_dim, tiled=True
            )
            return lax.psum_scatter(value, "wide", scatter_dimension=wide_dim, tiled=True).astype(
                F32
            )

        grad_w_out = reduce(gw_out[0], (hidden_units, features), 1, 0)
        grad_w_in = reduce(gw_in[0], (features, hidden_units), 1, 0)
        grad_conv = reduce(gconv[0], (taps, features, features), 2, 1)
    sums = jnp.concatenate(
        [v.sum(0) for v in (gconv_b, gain_one, bias_one, gb_in, gain_two, bias_two)]
    )
    sums = lax.psum(sums, ("wide", "narrow"))
    cuts = [features, 2 * features, 3 * features]
    cuts += [cuts[-1] + hidden_units, cuts[-1] + hidden_units + features]
    vectors = jnp.split(sums, cuts)
    return (
        out, grad_inputs, grad_conv, vectors[0], vectors[1], vectors[2], grad_w_in, vectors[3],
        grad_w_out, vectors[4], vectors[5],
    )


def solution(mesh):
    split = P("narrow", "wide", None)
    placed = (split,) + (P(),) * 9 + (P("narrow", "wide"), P("narrow", None, "wide"), split)
    return jax.shard_map(
        body,
        mesh=mesh,
        in_specs=placed,
        out_specs=(
            split, split, P(None, "narrow", "wide"), P(), P(), P(), P("narrow", "wide"), P(),
            P("narrow", "wide"), P(), P(),
        ),
        check_vma=False,
    )
```

time: 772 us -> 268 us (0.35); the launches traced: 760 us -> 267 us
  matrix products: 182 us -> 0 us
  waiting for transfers between devices: 195 us -> 18.6 us
  other arithmetic: 159 us -> 2.67 us
  Pallas kernels: 0 us -> 139 us
  local copies, waits for them, and re-layouts: 98.4 us -> 17.3 us
  starting transfers between devices: 65.9 us -> 41.1 us
  between operations: 18.4 us -> 1.14 us
    dot_general x132 -> x0, matrix products: 182 us -> none  [the longest x36 43.2 us: conv_backward(): lax.dot_general(source_rows.reshape(-1, features), flat_grad, (((0,), (0,...]
    reduce_scatter x6 -> x0, waiting for transfers between devices: 164 us -> none  [the longest x1 130 us: body(): lax.psum_scatter(acc_conv, 'narrow', scatter_dimension=1, tiled=True)]
    pallas_call x0 -> x17, Pallas kernels: none -> 139 us  [the longest x1 34.9 us: forward(): pl.pallas_call(functools.partial(forward_kernel, blocks), grid=(steps,),...]
    convert_element_type x20 -> x0, other arithmetic: 69.3 us -> none  [the longest x1 42.3 us: body(): act_low = activated.astype(jnp.bfloat16)]
    all_to_all x17 -> x0, starting transfers between devices: 65.3 us -> none  [the longest x4 16 us: body(): lax.all_to_all(source_low.reshape(micro_rows, wide_total_count, block_lis...]
    mul x85 -> x0, local copies, waits for them, and re-layouts: 41.8 us -> none  [the longest x40 20.5 us: conv_forward(): source_rows = source_rows * valid_taps[tap_number][..., None]]
    ppermute x0 -> x30, starting transfers between devices: none -> 41.1 us  [the longest x24 27.4 us: flip(): return lax.ppermute(value, axis, [(i, i ^ bit) for i in range(size)])]
    reduce_sum x14 -> x6, other arithmetic: 37.6 us -> 0.11 us  [body(): v.sum(0)]
  transfers between devices with their start and end apart: 23 -> 30, of which waited for: 10 -> 4; matrix products, arithmetic and copies ran while one was open for 37% -> 5% of each run, Pallas kernels for 0% -> 21%
where the time goes in v1:
time: 268 us; the launch traced here: 267 us
  Pallas kernels  139 us (52%)
  blocking collectives  46.7 us (17%)
  starting transfers between devices  41.1 us (15%)
  waiting for transfers between devices  18.6 us (7%)
  local copies, waits for them, and re-layouts  17.3 us (6%)
    psum x1, blocking collectives, body(): sums = lax.psum(sums, ('wide', 'narrow'))  46.7 us
    pallas_call x1, Pallas kernels, forward(): pl.pallas_call(functools.partial(forward_kernel, blocks), grid=(steps,),...  34.9 us
    ppermute x24, starting transfers between devices, flip(): return lax.ppermute(value, axis, [(i, i ^ bit) for i in range(size)])  27.4 us
    pallas_call x12, Pallas kernels, small(): pl.pallas_call(kernel, out_shape=[shape(d, dtype) for d in dims], compile...  26.9 us
    pallas_call x1, Pallas kernels, backward(): pl.pallas_call(functools.partial(backward_kernel, blocks), grid=(steps,),...  25.6 us
    pallas_call x1, Pallas kernels, weight_gradient(): pl.pallas_call(functools.partial(weight_kernel, blocks), grid=(taps,), in...  19.7 us
    ppermute x24, waiting for transfers between devices, flip(): return lax.ppermute(value, axis, [(i, i ^ bit) for i in range(size)])  18.6 us
    pallas_call x1, Pallas kernels, input_gradient(): pl.pallas_call(input_kernel, grid=(rows // block_rows,), in_specs=[pl.Blo...  16.9 us
  transfers between devices with their start and end apart: 30, of which 4 were waited for; matrix products, arithmetic and copies ran while one was open for 5% of the time, Pallas kernels for 21%

profile of v1, /device:TPU:0, one launch (start us, length us, event | category | flops | bytes accessed | tf_op | source)
XLA Modules:
  0.0 267.0 jit_solution(4413141294767341078)
XLA Ops:
  0.7 1.8 fusion.4
  2.5 3.4 %collective-permute-start.2 = (bf16[8,128,512]{2,1,0:T(8,128)(2,1)S(1)}, bf16[8,128,512]{2,1,0:T(8,128)(2,1)}, u32[]{:S(2)}, u32[]{:S(2)}) collective-permute-start(bf16[8,128,512]{2,1,0:T(8,128)(2,1)S(1)} %get-tuple-element.124), channel_id=1, source_target_pairs={{0,8},{8,16},{16,24},{1,9},{9,17},{17,25},{2,10},{10,18},{18,26},{... | collective-permute-start | bytes 3145736 | tf_op jit(solution)/shard_map/ppermute | solution.py:600
  7.2 4.2 %collective-permute-start = (s32[10,8,128]{2,1,0:T(8,128)S(1)}, s32[10,8,128]{2,1,0:T(8,128)S(1)}, u32[]{:S(2)}, u32[]{:S(2)}) collective-permute-start(s32[10,8,128]{2,1,0:T(8,128)S(1)} %get-tuple-element.127), channel_id=1, source_target_pairs={{0,8},{8,16},{16,24},{1,9},{9,17},{17,25},{2,10},{10,18},{18,26},{... | collective-permute-start | bytes 122888 | tf_op jit(solution)/shard_map/ppermute | solution.py:600
  13.5 15.5 %conv_inner.1.acc_ref = f32[8,256,512]{2,1,0:T(8,128)} custom-call(s32[10,8,256]{2,1,0:T(8,128)} %pad_add_fusion.1.info_ref, bf16[8,256,512]{2,1,0:T(8,128)(2,1)} %x_ref.5, bf16[9,512,512]{2,1,0:T(8,128)(2,1)} %conv_w_ref.1), custom_call_target="tpu_custom_call" | custom-call | flops 6957847040 | bytes 11000000 | tf_op jit(solution)/shard_map/conv_inner/pallas_call | solution.py:101
  30.9 34.9 %forward.1 = (bf16[8,256,512]{2,1,0:T(8,128)(2,1)}, bf16[8,256,512]{2,1,0:T(8,128)(2,1)}, bf16[8,256,512]{2,1,0:T(8,128)(2,1)}, bf16[2048,512]{1,0:T(8,128)(2,1)...) custom-call(s32[10,8,512]{2,1,0:T(8,128)} %get-tuple-element.126.inf, ...), custom_call_target="tpu_custom_call" | custom-call | flops 15569256448 | bytes 40000000 | tf_op jit(solution)/shard_map/forward/pallas_call | solution.py:269
  65.9 25.6 %backward.1 = (f32[8,256,512]{2,1,0:T(8,128)}, bf16[8,256,512]{2,1,0:T(8,128)(2,1)}, f32[8,2048]{1,0:T(8,128)}, f32[8,512]{1,0:T(8,128)}, f32[8,512]{1,0:T(8,128...) custom-call(bf16[2048,512]{1,0:T(8,128)(2,1)} %get-tuple-element.67.gproj_ref, ...), custom_call_target="tpu_custom_call" | custom-call | flops 12884901888 | bytes 30000000 | tf_op jit(solution)/shard_map/backward/pallas_call | solution.py:374
  91.5 19.7 %weight_gradient.1 = (bf16[16,576,128]{2,1,0:T(8,128)(2,1)}, bf16[16,576,128]{2,1,0:T(8,128)(2,1)}) custom-call(s32[10,8,512]{2,1,0:T(8,128)} %get-tuple-element.126.info_ref, bf16[8,256,512]{2,1,0:T(8,128)(2,1)} %x_ref.5, bf16[8,128,512]{2,1,0:T(8,128)(2,1)} %collective-permute-done.2.left_ref, bf16[8,128,512]{2,1,0:T(8,128)(2,1)} %collective-permute-done.3.right_ref, ...), custom_call_target="tpu_custom_call" | custom-call | flops 9663676416 | bytes 12000000 | tf_op jit(solution)/shard_map/weight_gradient/pallas_call | solution.py:450
  111.2 2.4 collective-permute-start.6
  114.1 5.0 %collective-permute-done.22.got = bf16[16,256,128]{2,1,0:T(8,128)(2,1)S(1)} collective-permute-done((bf16[16,256,128]{2,1,0:T(8,128)(2,1)S(1)}, bf16[16,256,128]{2,1,0:T(8,128)(2,1)S(1)}, u32[]{:S(2)}, u32[]{:S(2)}) %collective-permute-start.22) | collective-permute-done | bytes 1048608 | tf_op jit(solution)/shard_map/ppermute | solution.py:521
  120.1 2.6 after_core_kernel.5
  124.2 1.8 collective-permute-start.24
  127.0 2.6 after_core_kernel.4
  131.5 4.1 %after_core_kernel.3 = (bf16[8,288,128]{2,1,0:T(8,128)(2,1)}, bf16[8,288,128]{2,1,0:T(8,128)(2,1)}, bf16[8,288,128]{2,1,0:T(8,128)(2,1)}, bf16[8,288,128]{2,1,0:T(8,128)(2,1)}) custom-call(bf16[16,576,128]{2,1,0:T(8,128)(2,1)} %get-tuple-element.73.keep, bf16[16,576,128]{2,1,0:T(8,128)(2,1)} %copy-done), custom_call_target="tpu_custom_call" | custom-call | flops 4718592 | bytes 9437184 | tf_op jit(solution)/shard_map/after_core_kernel/pallas_call | solution.py:558
  138.3 2.3 collective-permute-start.4
  140.6 2.0 collective-permute-start.16
  144.6 6.7 %copy.24 = bf16[9,512,512]{2,1,0:T(8,128)(2,1)} copy(bf16[9,512,512]{1,2,0:T(8,128)(2,1)} %bitcast.9) | data formatting | bytes 9437184 | tf_op jit(solution)/shard_map/transpose | solution.py:611
  152.2 2.0 after_first_kernel.5
  154.2 7.5 %collective-permute-done.16.b_got = bf16[8,32,512]{2,1,0:T(8,128)(2,1)S(1)} collective-permute-done((bf16[8,32,512]{2,1,0:T(8,128)(2,1)}, bf16[8,32,512]{2,1,0:T(8,128)(2,1)S(1)}, u32[]{:S(2)}, u32[]{:S(2)}) %collective-permute-start.16) | collective-permute-done | bytes 262176 | tf_op jit(solution)/shard_map/ppermute | solution.py:521
  163.1 2.0 after_first_kernel.4
  166.4 2.7 %after_first_kernel.3 = (bf16[4,288,128]{2,1,0:T(8,128)(2,1)}, bf16[4,288,128]{2,1,0:T(8,128)(2,1)}, bf16[4,288,128]{2,1,0:T(8,128)(2,1)}, bf16[4,288,128]{2,1,0:T(8,128)(2,1)}) custom-call(bf16[8,288,128]{2,1,0:T(8,128)(2,1)} %get-tuple-element.75.a_keep, bf16[8,288,128]{2,1,0:T(8,128)(2,1)} %collective-permute-done.7.a_got, ...), custom_call_target="tpu_custom_call" | custom-call | flops 2359296 | bytes 4718592 | tf_op jit(solution)/shard_map/after_first_kernel/pallas_call | solution.py:558
  169.1 5.2 %collective-permute-done.25.a_got = bf16[4,128,128]{2,1,0:T(8,128)(2,1)S(1)} collective-permute-done((bf16[4,128,128]{2,1,0:T(8,128)(2,1)}, bf16[4,128,128]{2,1,0:T(8,128)(2,1)S(1)}, u32[]{:S(2)}, u32[]{:S(2)}) %collective-permute-start.25) | collective-permute-done | bytes 131104 | tf_op jit(solution)/shard_map/ppermute | solution.py:521
  176.5 46.7 %psum.7 = f32[4608]{0:T(1024)S(1)} all-reduce(f32[4608]{0:T(1024)S(1)} %constant_dynamic-update-slice_fusion), channel_id=1, replica_groups=mesh['wide'=4,'narrow'=8] {'wide','narrow'}, use_global_device_ids=true, to_apply=%region_6.7 | all-reduce | flops 4608 | bytes 36864 | tf_op jit(solution)/shard_map/psum | solution.py:645
  223.2 1.8 after_second_kernel.5
  225.0 1.6 collective-permute-start.27
  226.6 1.8 after_second_kernel.4
  233.2 2.1 after_second_kernel.3
  235.3 2.3 collective-permute-start.20
  239.2 2.8 %collective-permute-start.12 = (bf16[576,128]{1,0:T(8,128)(2,1)}, bf16[576,128]{1,0:T(8,128)(2,1)S(1)}, u32[]{:S(2)}, u32[]{:S(2)}) collective-permute-start(bf16[576,128]{1,0:T(8,128)(2,1)} %get-tuple-element.85), channel_id=1, source_target_pairs={{0,4},{1,5},{2,6},{3,7},{4,0},{5,1},{6,2},{7,3},{8,12},{9,13},{10,... | collective-permute-start | bytes 442376 | tf_op jit(solution)/shard_map/ppermute | solution.py:521
  243.6 16.9 %input_gradient.1 = f32[8,256,512]{2,1,0:T(8,128)} custom-call(s32[8,10,512]{2,1,0:T(8,128)} %copy.25.info_ref, f32[8,256,512]{2,1,0:T(8,128)} %get-tuple-element.71.gmixed_ref, bf16[8,256,512]{2,1,0:T(8,128)(2,1)} %get-tuple-element.72.gh_ref, bf16[8,128,512]{2,1,0:T(8,128)(2,1)} %collective-permute-done.4.left_ref, ...), custom_call_target="tpu_custom_call" | custom-call | flops 9663676416 | bytes 18000000 | tf_op jit(solution)/shard_map/input_gradient/pallas_call | solution.py:503
  260.4 1.6 last_kernel.5
  262.7 1.6 last_kernel.4
  265.1 1.9 last_kernel.3
  (159 shorter events, 30.8 us)
Async XLA Ops:
  2.5 28.4 %collective-permute-start.2 = (bf16[8,128,512]{2,1,0:T(8,128)(2,1)S(1)}, bf16[8,128,512]{2,1,0:T(8,128)(2,1)}, u32[]{:S(2)}, u32[]{:S(2)}) collective-permute-start(bf16[8,128,512]{2,1,0:T(8,128)(2,1)S(1)} %get-tuple-element.124), channel_id=1, source_target_pairs={{0,8},{8,16},{16,24},{1,9},{9,17},{17,25},{2,10},{10,18},{18,26},{... | collective-permute-start | bytes 3145736 | tf_op jit(solution)/shard_map/ppermute | solution.py:600
  5.9 25.0 %collective-permute-start.3 = (bf16[8,128,512]{2,1,0:T(8,128)(2,1)S(1)}, bf16[8,128,512]{2,1,0:T(8,128)(2,1)}, u32[]{:S(2)}, u32[]{:S(2)}) collective-permute-start(bf16[8,128,512]{2,1,0:T(8,128)(2,1)S(1)} %get-tuple-element.123), channel_id=1, source_target_pairs={{8,0},{16,8},{24,16},{9,1},{17,9},{25,17},{10,2},{18,10},{26,18},{... | collective-permute-start | bytes 3145736 | tf_op jit(solution)/shard_map/ppermute | solution.py:601
  7.2 23.0 %collective-permute-start = (s32[10,8,128]{2,1,0:T(8,128)S(1)}, s32[10,8,128]{2,1,0:T(8,128)S(1)}, u32[]{:S(2)}, u32[]{:S(2)}) collective-permute-start(s32[10,8,128]{2,1,0:T(8,128)S(1)} %get-tuple-element.127), channel_id=1, source_target_pairs={{0,8},{8,16},{16,24},{1,9},{9,17},{17,25},{2,10},{10,18},{18,26},{... | collective-permute-start | bytes 122888 | tf_op jit(solution)/shard_map/ppermute | solution.py:600
  11.4 18.8 %collective-permute-start.1 = (s32[10,8,128]{2,1,0:T(8,128)S(1)}, s32[10,8,128]{2,1,0:T(8,128)S(1)}, u32[]{:S(2)}, u32[]{:S(2)}) collective-permute-start(s32[10,8,128]{2,1,0:T(8,128)S(1)} %get-tuple-element.128), channel_id=1, source_target_pairs={{8,0},{16,8},{24,16},{9,1},{17,9},{25,17},{10,2},{18,10},{26,18},{... | collective-permute-start | bytes 122888 | tf_op jit(solution)/shard_map/ppermute | solution.py:601
  111.2 18.9 %collective-permute-start.6 = (bf16[16,576,128]{2,1,0:T(8,128)(2,1)}, bf16[16,576,128]{2,1,0:T(8,128)(2,1)S(1)}, u32[]{:S(2)}, u32[]{:S(2)}) collective-permute-start(bf16[16,576,128]{2,1,0:T(8,128)(2,1)} %get-tuple-element.74), channel_id=1, source_target_pairs={{0,8},{8,0},{16,24},{24,16},{1,9},{9,1},{17,25},{25,17},{2,10},{10... | collective-permute-start | bytes 7077896 | tf_op jit(solution)/shard_map/ppermute | solution.py:521
  113.6 5.5 %collective-permute-start.22 = (bf16[16,256,128]{2,1,0:T(8,128)(2,1)S(1)}, bf16[16,256,128]{2,1,0:T(8,128)(2,1)S(1)}, u32[]{:S(2)}, u32[]{:S(2)}) collective-permute-start(bf16[16,256,128]{2,1,0:T(8,128)(2,1)S(1)} %copy-done.39), channel_id=1, source_target_pairs={{0,8},{8,0},{16,24},{24,16},{1,9},{9,1},{17,25},{25,17},{2,10},{10... | collective-permute-start | bytes 3145736 | tf_op jit(solution)/shard_map/ppermute | solution.py:521
  113.7 12.3 %collective-permute-start.14 = (bf16[16,64,512]{2,1,0:T(8,128)(2,1)S(1)}, bf16[16,64,512]{2,1,0:T(8,128)(2,1)S(1)}, u32[]{:S(2)}, u32[]{:S(2)}) collective-permute-start(bf16[16,64,512]{2,1,0:T(8,128)(2,1)S(1)} %copy-done.38), channel_id=1, source_target_pairs={{0,8},{8,0},{16,24},{24,16},{1,9},{9,1},{17,25},{25,17},{2,10},{10... | collective-permute-start | bytes 3145736 | tf_op jit(solution)/shard_map/ppermute | solution.py:521
  122.7 17.8 %collective-permute-start.23 = (bf16[8,128,128]{2,1,0:T(8,128)(2,1)}, bf16[8,128,128]{2,1,0:T(8,128)(2,1)S(1)}, u32[]{:S(2)}, u32[]{:S(2)}) collective-permute-start(bf16[8,128,128]{2,1,0:T(8,128)(2,1)} %get-tuple-element.110), channel_id=1, source_target_pairs={{0,1},{1,0},{2,3},{3,2},{4,5},{5,4},{6,7},{7,6},{8,9},{9,8},{10,11... | collective-permute-start | bytes 786440 | tf_op jit(solution)/shard_map/ppermute | solution.py:521
  124.2 16.3 %collective-permute-start.24 = (bf16[8,128,128]{2,1,0:T(8,128)(2,1)}, bf16[8,128,128]{2,1,0:T(8,128)(2,1)S(1)}, u32[]{:S(2)}, u32[]{:S(2)}) collective-permute-start(bf16[8,128,128]{2,1,0:T(8,128)(2,1)} %get-tuple-element.112), channel_id=1, source_target_pairs={{0,16},{8,24},{16,0},{24,8},{1,17},{9,25},{17,1},{25,9},{2,18},{10... | collective-permute-start | bytes 786440 | tf_op jit(solution)/shard_map/ppermute | solution.py:521
  129.6 13.0 %collective-permute-start.15 = (bf16[8,32,512]{2,1,0:T(8,128)(2,1)}, bf16[8,32,512]{2,1,0:T(8,128)(2,1)S(1)}, u32[]{:S(2)}, u32[]{:S(2)}) collective-permute-start(bf16[8,32,512]{2,1,0:T(8,128)(2,1)} %get-tuple-element.96), channel_id=1, source_target_pairs={{0,1},{1,0},{2,3},{3,2},{4,5},{5,4},{6,7},{7,6},{8,9},{9,8},{10,11... | collective-permute-start | bytes 786440 | tf_op jit(solution)/shard_map/ppermute | solution.py:521
  135.6 27.0 %collective-permute-start.7 = (bf16[8,288,128]{2,1,0:T(8,128)(2,1)}, bf16[8,288,128]{2,1,0:T(8,128)(2,1)}, u32[]{:S(2)}, u32[]{:S(2)}) collective-permute-start(bf16[8,288,128]{2,1,0:T(8,128)(2,1)} %get-tuple-element.76), channel_id=1, source_target_pairs={{0,1},{1,0},{2,3},{3,2},{4,5},{5,4},{6,7},{7,6},{8,9},{9,8},{10,11... | collective-permute-start | bytes 1769480 | tf_op jit(solution)/shard_map/ppermute | solution.py:521
  138.3 90.2 %collective-permute-start.4 = (bf16[8,128,512]{2,1,0:T(8,128)(2,1)}, bf16[8,128,512]{2,1,0:T(8,128)(2,1)}, u32[]{:S(2)}, u32[]{:S(2)}) collective-permute-start(bf16[8,128,512]{2,1,0:T(8,128)(2,1)} %get-tuple-element.122), channel_id=1, source_target_pairs={{0,8},{8,16},{16,24},{1,9},{9,17},{17,25},{2,10},{10,18},{18,26},{... | collective-permute-start | bytes 3145736 | tf_op jit(solution)/shard_map/ppermute | solution.py:600
  140.5 24.6 %collective-permute-start.8 = (bf16[8,288,128]{2,1,0:T(8,128)(2,1)}, bf16[8,288,128]{2,1,0:T(8,128)(2,1)S(1)}, u32[]{:S(2)}, u32[]{:S(2)}) collective-permute-start(bf16[8,288,128]{2,1,0:T(8,128)(2,1)} %get-tuple-element.78), channel_id=1, source_target_pairs={{0,16},{8,24},{16,0},{24,8},{1,17},{9,25},{17,1},{25,9},{2,18},{10... | collective-permute-start | bytes 1769480 | tf_op jit(solution)/shard_map/ppermute | solution.py:521
  140.6 21.1 %collective-permute-start.16 = (bf16[8,32,512]{2,1,0:T(8,128)(2,1)}, bf16[8,32,512]{2,1,0:T(8,128)(2,1)S(1)}, u32[]{:S(2)}, u32[]{:S(2)}) collective-permute-start(bf16[8,32,512]{2,1,0:T(8,128)(2,1)} %get-tuple-element.98), channel_id=1, source_target_pairs={{0,16},{8,24},{16,0},{24,8},{1,17},{9,25},{17,1},{25,9},{2,18},{10... | collective-permute-start | bytes 786440 | tf_op jit(solution)/shard_map/ppermute | solution.py:521
  143.3 92.0 %collective-permute-start.5 = (bf16[8,128,512]{2,1,0:T(8,128)(2,1)S(1)}, bf16[8,128,512]{2,1,0:T(8,128)(2,1)}, u32[]{:S(2)}, u32[]{:S(2)}) collective-permute-start(bf16[8,128,512]{2,1,0:T(8,128)(2,1)S(1)} %get-tuple-element.121), channel_id=1, source_target_pairs={{8,0},{16,8},{24,16},{9,1},{17,9},{25,17},{10,2},{18,10},{26,18},{... | collective-permute-start | bytes 3145736 | tf_op jit(solution)/shard_map/ppermute | solution.py:601
  161.7 12.6 %collective-permute-start.25 = (bf16[4,128,128]{2,1,0:T(8,128)(2,1)}, bf16[4,128,128]{2,1,0:T(8,128)(2,1)S(1)}, u32[]{:S(2)}, u32[]{:S(2)}) collective-permute-start(bf16[4,128,128]{2,1,0:T(8,128)(2,1)} %get-tuple-element.114), channel_id=1, source_target_pairs={{0,16},{8,24},{16,0},{24,8},{1,17},{9,25},{17,1},{25,9},{2,18},{10... | collective-permute-start | bytes 393224 | tf_op jit(solution)/shard_map/ppermute | solution.py:521
  162.5 12.3 %collective-permute-start.26 = (bf16[4,128,128]{2,1,0:T(8,128)(2,1)}, bf16[4,128,128]{2,1,0:T(8,128)(2,1)S(1)}, u32[]{:S(2)}, u32[]{:S(2)}) collective-permute-start(bf16[4,128,128]{2,1,0:T(8,128)(2,1)} %get-tuple-element.116), channel_id=1, source_target_pairs={{0,1},{1,0},{2,3},{3,2},{4,5},{5,4},{6,7},{7,6},{8,9},{9,8},{10,11... | collective-permute-start | bytes 393224 | tf_op jit(solution)/shard_map/ppermute | solution.py:521
  165.1 10.6 %collective-permute-start.17 = (bf16[4,32,512]{2,1,0:T(8,128)(2,1)}, bf16[4,32,512]{2,1,0:T(8,128)(2,1)S(1)}, u32[]{:S(2)}, u32[]{:S(2)}) collective-permute-start(bf16[4,32,512]{2,1,0:T(8,128)(2,1)} %get-tuple-element.100), channel_id=1, source_target_pairs={{0,16},{8,24},{16,0},{24,8},{1,17},{9,25},{17,1},{25,9},{2,18},{10... | collective-permute-start | bytes 393224 | tf_op jit(solution)/shard_map/ppermute | solution.py:521
  174.3 48.9 %copy-start.15 = (bf16[4,128,128]{2,1,0:T(8,128)(2,1)}, bf16[4,128,128]{2,1,0:T(8,128)(2,1)S(1)}, u32[]{:S(2)}) copy-start(bf16[4,128,128]{2,1,0:T(8,128)(2,1)S(1)} %collective-permute-done.25.a_got) | copy-start | bytes 393220
  174.3 55.5 %collective-permute-start.10 = (bf16[4,288,128]{2,1,0:T(8,128)(2,1)}, bf16[4,288,128]{2,1,0:T(8,128)(2,1)S(1)}, u32[]{:S(2)}, u32[]{:S(2)}) collective-permute-start(bf16[4,288,128]{2,1,0:T(8,128)(2,1)} %get-tuple-element.82), channel_id=1, source_target_pairs={{0,1},{1,0},{2,3},{3,2},{4,5},{5,4},{6,7},{7,6},{8,9},{9,8},{10,11... | collective-permute-start | bytes 884744 | tf_op jit(solution)/shard_map/ppermute | solution.py:521
  174.9 56.5 %collective-permute-start.9 = (bf16[4,288,128]{2,1,0:T(8,128)(2,1)}, bf16[4,288,128]{2,1,0:T(8,128)(2,1)S(1)}, u32[]{:S(2)}, u32[]{:S(2)}) collective-permute-start(bf16[4,288,128]{2,1,0:T(8,128)(2,1)} %get-tuple-element.80), channel_id=1, source_target_pairs={{0,16},{8,24},{16,0},{24,8},{1,17},{9,25},{17,1},{25,9},{2,18},{10... | collective-permute-start | bytes 884744 | tf_op jit(solution)/shard_map/ppermute | solution.py:521
  175.7 50.9 %copy-start.17 = (bf16[4,32,512]{2,1,0:T(8,128)(2,1)}, bf16[4,32,512]{2,1,0:T(8,128)(2,1)S(1)}, u32[]{:S(2)}) copy-start(bf16[4,32,512]{2,1,0:T(8,128)(2,1)S(1)} %collective-permute-done.17.a_got) | copy-start | bytes 393220
  175.7 49.3 %collective-permute-start.18 = (bf16[4,32,512]{2,1,0:T(8,128)(2,1)S(1)}, bf16[4,32,512]{2,1,0:T(8,128)(2,1)S(1)}, u32[]{:S(2)}, u32[]{:S(2)}) collective-permute-start(bf16[4,32,512]{2,1,0:T(8,128)(2,1)S(1)} %copy-done.40), channel_id=1, source_target_pairs={{0,1},{1,0},{2,3},{3,2},{4,5},{5,4},{6,7},{7,6},{8,9},{9,8},{10,11... | collective-permute-start | bytes 393224 | tf_op jit(solution)/shard_map/ppermute | solution.py:521
  225.0 12.6 %collective-permute-start.27 = (bf16[256,128]{1,0:T(8,128)(2,1)}, bf16[256,128]{1,0:T(8,128)(2,1)S(1)}, u32[]{:S(2)}, u32[]{:S(2)}) collective-permute-start(bf16[256,128]{1,0:T(8,128)(2,1)} %get-tuple-element.118), channel_id=1, source_target_pairs={{0,2},{1,3},{2,0},{3,1},{4,6},{5,7},{6,4},{7,5},{8,10},{9,11},{10,... | collective-permute-start | bytes 196616 | tf_op jit(solution)/shard_map/ppermute | solution.py:521
  228.4 10.7 %collective-permute-start.28 = (bf16[256,128]{1,0:T(8,128)(2,1)}, bf16[256,128]{1,0:T(8,128)(2,1)S(1)}, u32[]{:S(2)}, u32[]{:S(2)}) collective-permute-start(bf16[256,128]{1,0:T(8,128)(2,1)} %get-tuple-element.119), channel_id=1, source_target_pairs={{0,4},{1,5},{2,6},{3,7},{4,0},{5,1},{6,2},{7,3},{8,12},{9,13},{10,... | collective-permute-start | bytes 196616 | tf_op jit(solution)/shard_map/ppermute | solution.py:521
  229.9 9.3 %collective-permute-start.29 = (bf16[256,128]{1,0:T(8,128)(2,1)}, bf16[256,128]{1,0:T(8,128)(2,1)S(1)}, u32[]{:S(2)}, u32[]{:S(2)}) collective-permute-start(bf16[256,128]{1,0:T(8,128)(2,1)} %get-tuple-element.120), channel_id=1, source_target_pairs={{0,6},{1,7},{2,4},{3,5},{4,2},{5,3},{6,0},{7,1},{8,14},{9,15},{10,... | collective-permute-start | bytes 196616 | tf_op jit(solution)/shard_map/ppermute | solution.py:521
  231.4 10.6 %collective-permute-start.19 = (bf16[64,512]{1,0:T(8,128)(2,1)}, bf16[64,512]{1,0:T(8,128)(2,1)S(1)}, u32[]{:S(2)}, u32[]{:S(2)}) collective-permute-start(bf16[64,512]{1,0:T(8,128)(2,1)} %get-tuple-element.104), channel_id=1, source_target_pairs={{0,2},{1,3},{2,0},{3,1},{4,6},{5,7},{6,4},{7,5},{8,10},{9,11},{10,... | collective-permute-start | bytes 196616 | tf_op jit(solution)/shard_map/ppermute | solution.py:521
  235.3 26.8 %collective-permute-start.20 = (bf16[64,512]{1,0:T(8,128)(2,1)}, bf16[64,512]{1,0:T(8,128)(2,1)S(1)}, u32[]{:S(2)}, u32[]{:S(2)}) collective-permute-start(bf16[64,512]{1,0:T(8,128)(2,1)} %get-tuple-element.105), channel_id=1, source_target_pairs={{0,4},{1,5},{2,6},{3,7},{4,0},{5,1},{6,2},{7,3},{8,12},{9,13},{10,... | collective-permute-start | bytes 196616 | tf_op jit(solution)/shard_map/ppermute | solution.py:521
  237.6 24.5 %collective-permute-start.21 = (bf16[64,512]{1,0:T(8,128)(2,1)}, bf16[64,512]{1,0:T(8,128)(2,1)S(1)}, u32[]{:S(2)}, u32[]{:S(2)}) collective-permute-start(bf16[64,512]{1,0:T(8,128)(2,1)} %get-tuple-element.106), channel_id=1, source_target_pairs={{0,6},{1,7},{2,4},{3,5},{4,2},{5,3},{6,0},{7,1},{8,14},{9,15},{10,... | collective-permute-start | bytes 196616 | tf_op jit(solution)/shard_map/ppermute | solution.py:521
  239.2 25.2 %collective-permute-start.11 = (bf16[576,128]{1,0:T(8,128)(2,1)}, bf16[576,128]{1,0:T(8,128)(2,1)S(1)}, u32[]{:S(2)}, u32[]{:S(2)}) collective-permute-start(bf16[576,128]{1,0:T(8,128)(2,1)} %get-tuple-element.84), channel_id=1, source_target_pairs={{0,2},{1,3},{2,0},{3,1},{4,6},{5,7},{6,4},{7,5},{8,10},{9,11},{10,... | collective-permute-start | bytes 442376 | tf_op jit(solution)/shard_map/ppermute | solution.py:521
  239.2 25.2 %collective-permute-start.12 = (bf16[576,128]{1,0:T(8,128)(2,1)}, bf16[576,128]{1,0:T(8,128)(2,1)S(1)}, u32[]{:S(2)}, u32[]{:S(2)}) collective-permute-start(bf16[576,128]{1,0:T(8,128)(2,1)} %get-tuple-element.85), channel_id=1, source_target_pairs={{0,4},{1,5},{2,6},{3,7},{4,0},{5,1},{6,2},{7,3},{8,12},{9,13},{10,... | collective-permute-start | bytes 442376 | tf_op jit(solution)/shard_map/ppermute | solution.py:521
  242.0 22.3 %collective-permute-start.13 = (bf16[576,128]{1,0:T(8,128)(2,1)}, bf16[576,128]{1,0:T(8,128)(2,1)S(1)}, u32[]{:S(2)}, u32[]{:S(2)}) collective-permute-start(bf16[576,128]{1,0:T(8,128)(2,1)} %get-tuple-element.86), channel_id=1, source_target_pairs={{0,6},{1,7},{2,4},{3,5},{4,2},{5,3},{6,0},{7,1},{8,14},{9,15},{10,... | collective-permute-start | bytes 442376 | tf_op jit(solution)/shard_map/ppermute | solution.py:521
  (39 other events, 392.5 us)

commit v2 on v1

v2 whole, which is shorter than its diff:
```python
import functools
from typing import Any, NamedTuple

import jax
import jax.numpy as jnp
from jax import lax
from jax.experimental import pallas as pl
from jax.experimental.pallas import tpu as pltpu
from jax.sharding import PartitionSpec as P

STEP = 32
BF = jnp.bfloat16
F32 = jnp.float32
RSQRT2 = 0.7071067811865476
RSQRT2PI = 0.3989422804014327
EPS = 1e-05


def params(mebibytes):
    return pltpu.CompilerParams(vmem_limit_bytes=mebibytes * 1024 * 1024)


def cost(flops, moved, transcendentals=0):
    return pl.CostEstimate(
        flops=int(flops), bytes_accessed=int(moved), transcendentals=int(transcendentals)
    )


def whole(shape):
    rank = len(shape)
    return pl.BlockSpec(shape, lambda *_: (0,) * rank, pipeline_mode=pl.Buffered(1))


def shape(dims, dtype):
    return jax.ShapeDtypeStruct(dims, dtype)


def mask_columns(matched):
    return jnp.where(matched, 1.0, 0.0).astype(F32).T


def spread(column, width):
    wide = jnp.broadcast_to(column, (column.shape[0], 128)).astype(BF)
    return jnp.concatenate([wide] * (width // 128), axis=1)


def dot(left, right, left_dim, right_dim):
    return lax.dot_general(
        left, right, (((left_dim,), (right_dim,)), ((), ())), preferred_element_type=F32
    )


def cdf_and_exp(values):
    return 0.5 + 0.5 * lax.erf(values * RSQRT2), jnp.exp(-0.5 * values * values)


def fold(values):
    return values.reshape(-1, 8, values.shape[-1]).sum(0)


def put_masked(lhs, sources, columns, n, features):
    for r, source in enumerate(sources):
        lhs[r * n : (r + 1) * n, :] = source * spread(columns[:, r : r + 1], features)


def conv_inner_kernel(info_ref, x_ref, w_ref, acc_ref, even, odd):
    step = pl.program_id(0)
    rows, own, features = x_ref.shape
    taps = info_ref.shape[0] - 1
    half = taps // 2
    order = [half] + [k for k in range(taps) if k != half]
    buffers = (even, odd)

    def span(k):
        shift = STEP * (k - half)
        return max(0, -shift), own - max(0, shift), shift

    def build(i):
        k = order[i]
        low, high, shift = span(k)
        ids = info_ref[0]
        matched = (ids[:, low + shift : high + shift] == ids[:, low:high]) & (
            info_ref[1 + k][:, low:high] == 1
        )
        put_masked(
            buffers[i % 2],
            [x_ref[r, low + shift : high + shift, :] for r in range(rows)],
            mask_columns(matched), high - low, features,
        )

    def run(i):
        low, high, _ = span(order[i])
        n = high - low
        if i + 1 < taps:
            build(i + 1)
        product = dot(buffers[i % 2][: rows * n, :], w_ref[0], 1, 0).reshape(rows, n, features)
        if i == 0:
            acc_ref[...] = product
        else:
            acc_ref[:, low:high, :] += product

    pl.when(step == 0)(functools.partial(build, 0))
    for i in range(taps):
        pl.when(step == i)(functools.partial(run, i))


def conv_inner(info, x, conv_w):
    rows, own, features = x.shape
    taps = conv_w.shape[0]
    half = taps // 2

    def tap_of(i):
        return jnp.where(i == 0, half, jnp.where(i <= half, i - 1, i))

    return pl.pallas_call(
        conv_inner_kernel,
        grid=(taps,),
        in_specs=[
            whole(info.shape),
            whole(x.shape),
            pl.BlockSpec((1, features, features), lambda i: (tap_of(i), 0, 0)),
        ],
        out_specs=whole(x.shape),
        out_shape=shape(x.shape, F32),
        scratch_shapes=[pltpu.VMEM((rows * own, features), BF)] * 2,
        compiler_params=params(20),
        cost_estimate=cost(2 * rows * own * features * features * taps * 0.72, 11e6),
        name="conv_inner",
    )(info, x, conv_w)


def conv_outer_kernel(info_ref, left_ref, right_ref, w_ref, vec_ref, acc_hbm, hidden_ref, acc, even, odd, sem):
    step = pl.program_id(0)
    rows, own, features = hidden_ref.shape
    taps = info_ref.shape[0] - 1
    half = taps // 2
    reach = STEP * half
    order = [k for k in range(taps) if k != half]
    buffers = (even, odd)
    load = pltpu.make_async_copy(acc_hbm, acc, sem)

    def span(k):
        n = STEP * abs(k - half)
        return (0 if k < half else own - n), n

    def build(i):
        k = order[i]
        low, n = span(k)
        left = k < half
        source = reach - n if left else 0
        shift = -n if left else n
        at = reach + low
        ids = info_ref[0]
        matched = (info_ref[1 + k][:, at : at + n] == 1) & (
            ids[:, at + shift : at + shift + n] == ids[:, at : at + n]
        )
        halo = left_ref if left else right_ref
        put_masked(
            buffers[i % 2], [halo[r, source : source + n, :] for r in range(rows)],
            mask_columns(matched), n, features,
        )

    def run(i):
        low, n = span(order[i])
        if i + 1 < len(order):
            build(i + 1)
        product = dot(buffers[i % 2][: rows * n, :], w_ref[0], 1, 0).reshape(rows, n, features)
        acc[:, low : low + n, :] += product

    @pl.when(step == 0)
    def _():
        load.start()
        build(0)
        load.wait()

    for i in range(len(order)):
        pl.when(step == i)(functools.partial(run, i))

    @pl.when(step == len(order) - 1)
    def _():
        hidden_ref[...] = (acc[...] + vec_ref[0:1, :]).astype(BF)


def conv_outer(info, acc, left, right, conv_w, vec):
    rows, own, features = acc.shape
    reach = left.shape[1]
    taps = conv_w.shape[0]
    half = taps // 2
    return pl.pallas_call(
        conv_outer_kernel,
        grid=(taps - 1,),
        in_specs=[
            whole(info.shape),
            whole(left.shape),
            whole(right.shape),
            pl.BlockSpec((1, features, features), lambda i: (jnp.where(i < half, i, i + 1), 0, 0)),
            whole(vec.shape),
            pl.BlockSpec(memory_space=pl.ANY),
        ],
        out_specs=whole(acc.shape),
        out_shape=shape(acc.shape, BF),
        scratch_shapes=[pltpu.VMEM(acc.shape, F32)]
        + [pltpu.VMEM((rows * reach, features), BF)] * 2
        + [pltpu.SemaphoreType.DMA],
        compiler_params=params(18),
        cost_estimate=cost(2 * rows * own * features * features * taps * 0.28, 11e6),
        name="conv_outer",
    )(info, left, right, conv_w, vec, acc)


def place_block(out_ref, value, dest_wide, dest_narrow, rows_at, blocks):
    if blocks == (1, 1):
        out_ref[0, 0, rows_at, :] = value
        return
    rel_wide = lax.axis_index("wide") ^ dest_wide
    rel_narrow = lax.axis_index("narrow") ^ dest_narrow
    index = (rel_wide >> 1) * 8 + (rel_narrow & 1) * 4 + (rel_narrow >> 1)
    out_ref[rel_wide & 1, index, rows_at, :] = value


def ship(pairs, sems):
    copies = [pltpu.make_async_copy(src, dst, sems.at[i]) for i, (src, dst) in enumerate(pairs)]
    for copy in copies:
        copy.start()
    for copy in copies:
        copy.wait()


def gradient_outputs(blocks, height, width, lanes=None):
    if blocks == (1, 1):
        dims = (1, 1, height, width)
        return [shape(dims, BF)], [whole(dims)], []
    n_wide, n_narrow = blocks
    height, width = height // n_narrow, width // n_wide
    if lanes is not None:
        height, width = height * width // lanes, lanes
    dims = (n_wide * n_narrow // 2, height, width)
    return (
        [shape(dims, BF)] * 2,
        [pl.BlockSpec(memory_space=pl.ANY)] * 2,
        [pltpu.VMEM((2,) + dims, BF), pltpu.SemaphoreType.DMA((2,))],
    )


def moments(values):
    centered = values - jnp.mean(values, axis=1, keepdims=True)
    return centered, lax.rsqrt(jnp.mean(centered * centered, axis=1, keepdims=True) + EPS)


def middle_kernel(
    blocks,
    hidden_ref, x_ref, ct_ref, w_in_ref, w_out_ref, vec_ref, b_in_ref,
    out_ref, gmixed_ref, gh_ref, sums_ref, *rest,
):
    if blocks == (1, 1):
        gw_out_ref, gw_in_ref, *rest = rest
    else:
        (keep_out, send_out, keep_in, send_in, *rest) = rest
    (
        act_scr, slope_scr, up_scr, gp_scr, gw_out_acc, gw_in_acc, b_in_acc, gain_one_acc,
        bias_one_acc, gain_two_acc, bias_two_acc, conv_b_acc, *rest,
    ) = rest
    if blocks != (1, 1):
        gw_out_ref, gw_in_ref, sems = rest
    step = pl.program_id(0)
    steps = pl.num_programs(0)
    size = act_scr.shape[0]
    features, hidden_units = w_in_ref.shape

    @pl.when(step == 0)
    def _():
        for ref in (
            act_scr, gp_scr, gw_out_acc, gw_in_acc, b_in_acc, gain_one_acc, bias_one_acc,
            gain_two_acc, bias_two_acc, conv_b_acc,
        ):
            ref[...] = jnp.zeros_like(ref)

    gain_one = vec_ref[1:2, :]
    bias_one = vec_ref[2:3, :]
    gain_two = vec_ref[3:4, :]
    bias_two = vec_ref[4:5, :]
    chunk = 512
    count = hidden_units // chunk
    pieces = [slice(j * chunk, (j + 1) * chunk) for j in range(count)]

    def out_part(cols):
        gw_out_acc[cols, :] += dot(act_scr[:, cols], gp_scr[...], 0, 0)

    for cols in pieces:
        out_part(cols)
    hid = hidden_ref[...].reshape(size, features).astype(F32)
    centered, scale = moments(hid * (0.5 + 0.5 * lax.erf(hid * RSQRT2)))
    mixed = x_ref[...].reshape(size, features).astype(F32) + (
        centered * scale * gain_one + bias_one
    )
    mixed_low = mixed.astype(BF)

    def up_part(cols):
        return dot(mixed_low, w_in_ref[:, cols], 1, 0) + b_in_ref[:, cols]

    projected = None
    up = up_part(pieces[0])
    for j, cols in enumerate(pieces):
        ahead = up_part(pieces[j + 1]) if j + 1 < count else None
        cdf, bell = cdf_and_exp(up)
        act_low = (up * cdf).astype(BF)
        slope_scr[:, cols] = cdf + up * bell * RSQRT2PI
        act_scr[:, cols] = act_low
        part = dot(act_low, w_out_ref[cols, :], 1, 0)
        projected = part if projected is None else projected + part
        up = ahead
    centered, scale = moments(projected)
    xhat = centered * scale
    out_ref[...] = (mixed + (xhat * gain_two + bias_two)).astype(BF).reshape(out_ref.shape)
    ct = ct_ref[...].reshape(size, features).astype(F32)
    gain_two_acc[...] += fold(ct * xhat)
    bias_two_acc[...] += fold(ct)
    e = ct * gain_two
    mean_e = jnp.mean(e, axis=1, keepdims=True)
    mean_ex = jnp.mean(e * xhat, axis=1, keepdims=True)
    gproj = (scale * (e - mean_e - xhat * mean_ex)).astype(BF)
    gp_scr[...] = gproj

    for cols in pieces:
        g_act = dot(gproj, w_out_ref[cols, :], 1, 1)
        up_low = (g_act * slope_scr[:, cols]).astype(BF)
        up_scr[:, cols] = up_low
        b_in_acc[:, cols] += fold(up_low.astype(F32))
    total = dot(up_scr[...], w_in_ref[...], 1, 1)
    for cols in pieces:
        gw_in_acc[:, cols] += dot(mixed_low, up_scr[:, cols], 0, 0)
    g_mixed = ct_ref[...].reshape(size, features).astype(F32) + total
    gmixed_ref[...] = g_mixed.reshape(gmixed_ref.shape)
    hid = hidden_ref[...].reshape(size, features).astype(F32)
    cdf, bell = cdf_and_exp(hid)
    centered, scale = moments(hid * cdf)
    yhat = centered * scale
    gain_one_acc[...] += fold(g_mixed * yhat)
    bias_one_acc[...] += fold(g_mixed)
    e = g_mixed * gain_one
    mean_e = jnp.mean(e, axis=1, keepdims=True)
    mean_ey = jnp.mean(e * yhat, axis=1, keepdims=True)
    g_hidden = scale * (e - mean_e - yhat * mean_ey) * (cdf + hid * bell * RSQRT2PI)
    g_low = g_hidden.astype(BF)
    gh_ref[...] = g_low.reshape(gh_ref.shape)
    conv_b_acc[...] += fold(g_low.astype(F32))

    @pl.when(step == steps - 1)
    def _():
        for cols in pieces:
            out_part(cols)
        row = 0
        for ref in (conv_b_acc, gain_one_acc, bias_one_acc, b_in_acc, gain_two_acc, bias_two_acc):
            summed = jnp.sum(ref[...], axis=0, keepdims=True)
            for j in range(ref.shape[1] // 128):
                sums_ref[row : row + 1, :] = summed[:, j * 128 : (j + 1) * 128]
                row += 1
        sums_ref[row:, :] = jnp.zeros_like(sums_ref[row:, :])
        n_wide, n_narrow = blocks
        height, width = features // n_narrow, hidden_units // n_wide
        lanes = gw_in_ref.shape[-1]
        for w in range(n_wide):
            product = gw_in_acc[:, w * width : (w + 1) * width].astype(BF)
            for n in range(n_narrow):
                for j in range(width // lanes):
                    place_block(
                        gw_in_ref,
                        product[n * height : (n + 1) * height, j * lanes : (j + 1) * lanes],
                        w, n, slice(j * height, (j + 1) * height), blocks,
                    )
        height, width = hidden_units // n_narrow, features // n_wide
        for n in range(n_narrow):
            product = gw_out_acc[n * height : (n + 1) * height, :].astype(BF)
            for w in range(n_wide):
                place_block(
                    gw_out_ref, product[:, w * width : (w + 1) * width], w, n, slice(0, height),
                    blocks,
                )
        if blocks != (1, 1):
            ship(
                (
                    (gw_in_ref.at[0], keep_in), (gw_in_ref.at[1], send_in),
                    (gw_out_ref.at[0], keep_out), (gw_out_ref.at[1], send_out),
                ),
                sems,
            )


def middle(blocks, hidden, x, ct, w_in, w_out, vec, b_in):
    rows, own, features = x.shape
    hidden_units = w_in.shape[1]
    block_rows = 2
    size = block_rows * own
    total = rows * own
    row_block = pl.BlockSpec((block_rows, own, features), lambda i: (i, 0, 0))
    out_shapes, out_specs, out_scratch = gradient_outputs(blocks, hidden_units, features)
    in_shapes, in_specs, in_scratch = gradient_outputs(blocks, features, hidden_units, 128)
    sums = ((5 * features + hidden_units) // 128 + 63) // 64 * 64
    sems = [] if blocks == (1, 1) else [pltpu.SemaphoreType.DMA((4,))]
    narrow = pltpu.VMEM((8, features), F32)
    return pl.pallas_call(
        functools.partial(middle_kernel, blocks),
        grid=(rows // block_rows,),
        in_specs=[
            row_block, row_block, row_block, whole(w_in.shape), whole(w_out.shape),
            whole(vec.shape), whole(b_in.shape),
        ],
        out_specs=[row_block, row_block, row_block, whole((sums, 128))] + out_specs + in_specs,
        out_shape=[
            shape(x.shape, BF), shape(x.shape, F32), shape(x.shape, BF), shape((sums, 128), F32),
        ] + out_shapes + in_shapes,
        scratch_shapes=[
            pltpu.VMEM((size, hidden_units), BF), pltpu.VMEM((size, hidden_units), F32),
            pltpu.VMEM((size, hidden_units), BF), pltpu.VMEM((size, features), BF),
            pltpu.VMEM((hidden_units, features), F32), pltpu.VMEM((features, hidden_units), F32),
            pltpu.VMEM((8, hidden_units), F32), narrow, narrow, narrow, narrow, narrow,
        ] + out_scratch[:1] + in_scratch[:1] + sems,
        compiler_params=params(46),
        cost_estimate=cost(2 * total * features * 6 * hidden_units, 34e6),
        name="middle",
    )(hidden, x, ct, w_in, w_out, vec, b_in)


def by_parity(step, run, even, odd):
    pl.when(step % 2 == 0)(lambda: run(even, odd))
    pl.when(step % 2 == 1)(lambda: run(odd, even))


def fill_copies(ext, left_hbm, own_hbm, right_hbm, sems):
    reach, own = left_hbm.shape[1], own_hbm.shape[1]
    return [
        pltpu.make_async_copy(own_hbm, ext.at[:, pl.ds(reach, own), :], sems.at[0]),
        pltpu.make_async_copy(left_hbm, ext.at[:, pl.ds(0, reach), :], sems.at[1]),
        pltpu.make_async_copy(right_hbm, ext.at[:, pl.ds(reach + own, reach), :], sems.at[2]),
    ]


def build_masked(lhs, ext, info_ref, tap, forward_masks, first=0):
    rows, extended, features = ext.shape
    taps = info_ref.shape[0] - 1
    reach = STEP * (taps // 2)
    own = extended - 2 * reach
    offset = STEP * tap if forward_masks else STEP * (taps - 1 - tap)
    ids = info_ref[0]
    moved = pltpu.roll(ids, extended - offset, 1)[:, :own]
    used = info_ref[1 + tap]
    if forward_masks:
        used = used[:, reach : reach + own]
    else:
        used = pltpu.roll(used, extended - offset, 1)[:, :own]
    columns = mask_columns((moved == ids[:, reach : reach + own]) & (used == 1))
    at = pl.ds(pl.multiple_of(offset, STEP), own)
    for r in range(rows):
        lhs[r * own : (r + 1) * own, :] = ext[r, at, :] * spread(
            columns[:, first + r : first + r + 1], features
        )


class Rider(NamedTuple):
    fn: Any
    operands: tuple
    in_specs: list
    out_specs: list
    out_shape: list
    steps: int


NO_RIDER = Rider(None, (), [], [], [], 0)


def ride(rider, step, ins, outs):
    if rider.fn is not None:
        pl.when(step < rider.steps)(lambda: rider.fn(ins, outs))


def rider_kernel(rider, *refs):
    count = len(rider.operands)
    rider.fn(refs[:count], refs[count:])


def alone(rider):
    moved = 3 * sum(v.size for v in rider.operands)
    return pl.pallas_call(
        functools.partial(rider_kernel, rider._replace(operands=(None,) * len(rider.operands))),
        grid=(rider.steps,),
        in_specs=rider.in_specs,
        out_specs=rider.out_specs,
        out_shape=rider.out_shape,
        compiler_params=params(8),
        cost_estimate=cost(moved / 2, moved),
        name="additions",
    )(*rider.operands)


def weight_kernel(blocks, rider, info_ref, gh_ref, x_hbm, left_hbm, right_hbm, *rest):
    ins, rest = rest[: len(rider.operands)], rest[len(rider.operands) :]
    if blocks == (1, 1):
        gw_ref, ext, lhs_even, lhs_odd, fill_sems = rest
        outs = ()
    else:
        keep_ref, send_ref, *rest = rest
        outs, rest = rest[: len(rider.out_shape)], rest[len(rider.out_shape) :]
        ext, lhs_even, lhs_odd, fill_sems, gw_ref, sems = rest
    tap = pl.program_id(0)
    taps = pl.num_programs(0)
    rows, own, features = gh_ref.shape

    @pl.when(tap == 0)
    def _():
        copies = fill_copies(ext, left_hbm, x_hbm, right_hbm, fill_sems)
        for copy in copies:
            copy.start()
        for copy in copies:
            copy.wait()
        build_masked(lhs_even, ext, info_ref, 0, True)

    n_wide, n_narrow = blocks
    height, width = features // n_narrow, features // n_wide
    rows_at = pl.ds(pl.multiple_of(tap * height, height), height)
    ride(rider, tap, ins, outs)

    def run(lhs, lhs_next):
        build_masked(lhs_next, ext, info_ref, jnp.minimum(tap + 1, taps - 1), True)
        product = dot(lhs[...], gh_ref[...].reshape(rows * own, features), 0, 0).astype(BF)
        for n in range(n_narrow):
            for w in range(n_wide):
                place_block(
                    gw_ref,
                    product[n * height : (n + 1) * height, w * width : (w + 1) * width],
                    w, n, rows_at, blocks,
                )

    by_parity(tap, run, lhs_even, lhs_odd)

    if blocks != (1, 1):

        def shipping(at):
            rows_of = pl.ds(pl.multiple_of(at * height, height), height)
            return [
                pltpu.make_async_copy(
                    gw_ref.at[i, :, rows_of, :], ref.at[:, rows_of, :], sems.at[i]
                )
                for i, ref in enumerate((keep_ref, send_ref))
            ]

        @pl.when(tap > 0)
        def _():
            for copy in shipping(tap - 1):
                copy.wait()

        for copy in shipping(tap):
            copy.start()

        @pl.when(tap == taps - 1)
        def _():
            for copy in shipping(tap):
                copy.wait()


def weight_gradient(blocks, info, gh, x, left, right, taps, rider=NO_RIDER):
    rows, own, features = x.shape
    reach = left.shape[1]
    shapes, specs, scratch = gradient_outputs(blocks, taps * features, features)
    light = rider._replace(operands=(None,) * len(rider.operands))
    return pl.pallas_call(
        functools.partial(weight_kernel, blocks, light),
        grid=(taps,),
        in_specs=[whole(info.shape), whole(gh.shape)]
        + [pl.BlockSpec(memory_space=pl.ANY)] * 3
        + rider.in_specs,
        out_specs=specs + rider.out_specs,
        out_shape=shapes + rider.out_shape,
        scratch_shapes=[
            pltpu.VMEM((rows, own + 2 * reach, features), BF),
            pltpu.VMEM((rows * own, features), BF),
            pltpu.VMEM((rows * own, features), BF),
            pltpu.SemaphoreType.DMA((3,)),
        ]
        + scratch,
        compiler_params=params(28),
        cost_estimate=cost(2 * rows * own * features * features * taps, 12e6),
        name="weight_gradient",
    )(info, gh, x, left, right, *rider.operands)


def input_kernel(first, rider, info_ref, w_ref, gh_hbm, left_hbm, right_hbm, gmixed_hbm, *rest):
    ins, rest = rest[: len(rider.operands)], rest[len(rider.operands) :]
    gx_hbm, *rest = rest
    outs, rest = rest[: len(rider.out_shape)], rest[len(rider.out_shape) :]
    ext, lhs_even, lhs_odd, acc, gmixed, fill_sems, in_sem, out_sems = rest
    tap = pl.program_id(0)
    taps = pl.num_programs(0)
    rows, own, features = gmixed.shape
    batch = pl.ds(first, rows)
    base = pltpu.make_async_copy(gmixed_hbm.at[batch], gmixed, in_sem)

    @pl.when(tap == 0)
    def _():
        copies = fill_copies(
            ext, left_hbm.at[batch], gh_hbm.at[batch], right_hbm.at[batch], fill_sems
        )
        for copy in copies:
            copy.start()
        base.start()
        acc[...] = jnp.zeros_like(acc)
        for copy in copies:
            copy.wait()
        build_masked(lhs_even, ext, info_ref, 0, False, first)

    ride(rider, tap, ins, outs)

    def run(lhs, lhs_next):
        build_masked(lhs_next, ext, info_ref, jnp.minimum(tap + 1, taps - 1), False, first)
        acc[...] += dot(lhs[...], w_ref[0], 1, 1)

    by_parity(tap, run, lhs_even, lhs_odd)

    @pl.when(tap == taps - 1)
    def _():
        base.wait()
        copies = []
        for r in range(rows):
            g_in = acc[r * own : (r + 1) * own, :].astype(BF).astype(F32)
            gmixed[r] = gmixed[r] + g_in
            copies.append(pltpu.make_async_copy(gmixed.at[r], gx_hbm.at[first + r], out_sems.at[r]))
            copies[-1].start()
        for copy in copies:
            copy.wait()


def input_gradient(info, conv_w, gh, left, right, gmixed, first, rows, rider=NO_RIDER):
    _, own, features = gh.shape
    reach = left.shape[1]
    taps = conv_w.shape[0]
    light = rider._replace(operands=(None,) * len(rider.operands))
    return pl.pallas_call(
        functools.partial(input_kernel, first, light),
        grid=(taps,),
        in_specs=[
            whole(info.shape),
            pl.BlockSpec((1, features, features), lambda i: (i, 0, 0)),
        ]
        + [pl.BlockSpec(memory_space=pl.ANY)] * 4
        + rider.in_specs,
        out_specs=[pl.BlockSpec(memory_space=pl.ANY)] + rider.out_specs,
        out_shape=[shape(gmixed.shape, F32)] + rider.out_shape,
        input_output_aliases={5: 0},
        scratch_shapes=[
            pltpu.VMEM((rows, own + 2 * reach, features), BF),
            pltpu.VMEM((rows * own, features), BF),
            pltpu.VMEM((rows * own, features), BF),
            pltpu.VMEM((rows * own, features), F32),
            pltpu.VMEM((rows, own, features), F32),
            pltpu.SemaphoreType.DMA((3,)),
            pltpu.SemaphoreType.DMA,
            pltpu.SemaphoreType.DMA((rows,)),
        ],
        compiler_params=params(20),
        cost_estimate=cost(2 * rows * own * features * features * taps, 12e6),
        name="input_gradient",
    )(info, conv_w, gh, left, right, gmixed, *rider.operands)


def flip(value, axis, bit):
    size = lax.axis_size(axis)
    return lax.ppermute(value, axis, [(i, i ^ bit) for i in range(size)])


def add(a, b):
    return a.astype(F32) + b.astype(F32)


def in_pair(value):
    high = value.astype(BF)
    return high, (value - high.astype(F32)).astype(BF)


def pair_sum(pair):
    return pair[0].astype(F32) + pair[1].astype(F32)


def stepwise(block, axis, steps):
    return pl.BlockSpec(
        block,
        lambda i: tuple(jnp.minimum(i, steps - 1) if d == axis else 0 for d in range(len(block))),
    )


def after_core(pairs, sums=()):
    count = len(pairs)
    half = sum(keep.shape[1] for keep, _ in pairs) // 2
    extra = 16 if sums else 0
    operands = [v.reshape((2, 2, 4) + v.shape[1:]) for side in zip(*pairs, strict=True) for v in side]

    def fn(ins, outs):
        a_keep, a_send, b_keep, b_send = outs
        base = 0
        for keep, got in zip(ins[:count], ins[count : 2 * count], strict=True):
            rows = keep.shape[3] // 2
            at = slice(base, base + rows)
            for y in range(2):
                for x in range(2):
                    total = add(keep[y, x, 0], got[y, x, 0]).astype(BF)
                    (a_send if x else a_keep)[y, 0, at, :] = total[:rows]
                    (b_send if y else b_keep)[x, 0, at, :] = total[rows:]
            base += rows
        if extra:
            high, low = in_pair(ins[-2][...] + ins[-1][...])
            for ref in (a_keep, a_send):
                ref[0, 0, half:, :] = high
                ref[1, 0, half:, :] = low

    tops = (2, 4, half + extra, 128), (2, 4, half + extra, 128), (2, 4, half, 128), (2, 4, half, 128)
    return Rider(
        fn,
        (*operands, *sums),
        [stepwise((2, 2, 1) + v.shape[3:], 2, 4) for v in operands]
        + [stepwise((16, 128), 0, 4) for _ in sums],
        [stepwise((2, 1) + d[2:], 1, 4) for d in tops],
        [shape(d, BF) for d in tops],
        4,
    )


def after_first(a_keep, a_got, b_keep, b_got):
    half = b_keep.shape[2]
    extra = a_keep.shape[2] - half

    def fn(ins, outs):
        a_keep, a_got, b_keep, b_got = ins
        a_next, a_send, b_next, b_send = outs
        for keep, got, stay, send in (
            (a_keep, a_got, a_next, a_send),
            (b_keep, b_got, b_next, b_send),
        ):
            stay[0, :half] = add(keep[0, 0, :half], got[0, 0, :half]).astype(BF)
            send[0, :half] = add(keep[1, 0, :half], got[1, 0, :half]).astype(BF)
        if extra:
            total = add(a_keep[0, 0, half:], a_keep[1, 0, half:]) + add(
                a_got[0, 0, half:], a_got[1, 0, half:]
            )
            high, low = in_pair(total)
            for ref in (a_next, a_send):
                ref[0, half : half + extra] = high
                ref[0, half + extra :] = low

    tops = [(4, half + 2 * extra, 128)] * 2 + [(4, half, 128)] * 2
    operands = (a_keep, a_got, b_keep, b_got)
    return Rider(
        fn,
        operands,
        [stepwise((2, 1) + v.shape[2:], 1, 4) for v in operands],
        [stepwise((1,) + d[1:], 0, 4) for d in tops],
        [shape(d, BF) for d in tops],
        4,
    )


def after_second_kernel(a_keep, a_got, b_keep, b_got, *outs):
    half = b_keep.shape[1]
    extra = (a_keep.shape[1] - half) // 2
    for i, ref in enumerate(outs):
        ref[0, :half] = add(a_keep[i, :half], a_got[i, :half]).astype(BF)
        ref[1, :half] = add(b_keep[i], b_got[i]).astype(BF)
    if extra:
        middle_at, end = half + extra, half + 2 * extra
        for z in range(4):
            total = add(a_keep[z, half:middle_at], a_keep[z, middle_at:end]) + add(
                a_got[z, half:middle_at], a_got[z, middle_at:end]
            )
            high, low = in_pair(total)
            at = slice(half + extra * z, half + extra * (z + 1))
            for ref in outs:
                ref[0, at] = high
                ref[1, at] = low


def after_second(a_keep, a_got, b_keep, b_got):
    half = b_keep.shape[1]
    rows = half + 2 * (a_keep.shape[1] - half)
    z = small(after_second_kernel, (a_keep, a_got, b_keep, b_got), [(2, rows, 128)] * 4)
    return (z[0], *(flip(z[i], "narrow", 2 * i) for i in (1, 2, 3)))


def last_ff_kernel(z0, z1, z2, z3, w_out_ref, w_in_ref, sums_ref):
    half = w_out_ref.shape[0] // 2
    height = w_in_ref.shape[0]
    count = w_in_ref.shape[1] // 128
    total = add(z0[...], z1[...]) + add(z2[...], z3[...])
    w_out_ref[:half] = total[0, :half]
    w_out_ref[half:] = total[1, :half]
    for j in range(count):
        side, at = divmod(j, count // 2)
        w_in_ref[:, 128 * j : 128 * (j + 1)] = total[side, half + at * height : half + (at + 1) * height]
    first = half + height * count // 2
    sums_ref[...] = total[0, first:] + total[1, first:]


def last_conv_kernel(z0, z1, z2, z3, out):
    total = add(z0[...], z1[...]) + add(z2[...], z3[...])
    half = total.shape[1]
    out[:half] = total[0]
    out[half:] = total[1]


def small(kernel, operands, dims, dtype=BF):
    moved = sum(v.size * v.dtype.itemsize for v in operands) * 2
    return pl.pallas_call(
        kernel,
        out_shape=[shape(d, dtype) for d in dims],
        compiler_params=params(12),
        cost_estimate=cost(moved / 2, moved),
        name=kernel.__name__,
    )(*operands)


def after(value, *others):
    return lax.optimization_barrier((value, others))[0]


def body(
    inputs, conv_w, conv_b, ln1_gain, ln1_bias, w_in, b_in, w_out, ln2_gain, ln2_bias,
    segments, tap_mask, cotangent,
):
    rows, own, features = inputs.shape
    taps = conv_w.shape[0]
    reach = STEP * (taps // 2)
    hidden_units = w_in.shape[1]
    n_wide, n_narrow = lax.axis_size("wide"), lax.axis_size("narrow")
    by_hand = (n_wide, n_narrow) == (4, 8)
    blocks = (4, 8) if by_hand else (1, 1)

    to_right = [(i, i + 1) for i in range(n_wide - 1)]
    to_left = [(i + 1, i) for i in range(n_wide - 1)]

    def halos(value, dim):
        last = value.shape[dim]
        left = lax.ppermute(lax.slice_in_dim(value, last - reach, last, axis=dim), "wide", to_right)
        right = lax.ppermute(lax.slice_in_dim(value, 0, reach, axis=dim), "wide", to_left)
        return left, right

    x_left, x_right = halos(inputs, 1)
    info = jnp.concatenate([segments[None] + 1, jnp.transpose(tap_mask, (1, 0, 2))], axis=0)
    info_left, info_right = halos(info, 2)
    info_ext = jnp.concatenate([info_left, info, info_right], axis=2)
    vec = jnp.stack([conv_b, ln1_gain, ln1_bias, ln2_gain, ln2_bias]).astype(F32)
    vec = jnp.pad(vec, ((0, 3), (0, 0)))

    acc = conv_inner(info, inputs, conv_w)
    hidden = conv_outer(info_ext, acc, x_left, x_right, conv_w, vec)
    out, gmixed, gh, sums, *grads = middle(
        blocks, hidden, inputs, cotangent, w_in, w_out, vec, b_in.astype(F32)[None]
    )
    gh_left, gh_right = halos(gh, 1)
    half_rows = rows // 2
    if not by_hand:
        gconv = weight_gradient(blocks, info_ext, gh, inputs, x_left, x_right, taps)
        gx = input_gradient(info_ext, conv_w, gh, gh_left, gh_right, gmixed, 0, half_rows)[0]
        gx = input_gradient(info_ext, conv_w, gh, gh_left, gh_right, gx, half_rows, half_rows)[0]

        def reduce(value, dims, wide_dim, narrow_dim):
            value = lax.psum_scatter(
                value.reshape(dims), "narrow", scatter_dimension=narrow_dim, tiled=True
            )
            return lax.psum_scatter(value, "wide", scatter_dimension=wide_dim, tiled=True).astype(
                F32
            )

        grad_w_out = reduce(grads[0], (hidden_units, features), 1, 0)
        grad_w_in = reduce(grads[1], (features, hidden_units), 1, 0)
        grad_conv = reduce(gconv[0], (taps, features, features), 2, 1)
        sums = lax.psum(sums, ("wide", "narrow"))
    else:
        got_out, got_in = flip(grads[1], "wide", 1), flip(grads[3], "wide", 1)
        got_sums = flip(sums, "wide", 1)
        rider = after_core(((grads[0], got_out), (grads[2], got_in)), (sums, got_sums))
        c_keep, c_send, *f = weight_gradient(
            blocks, info_ext, gh, inputs, x_left, x_right, taps, rider
        )
        c_send, f[1], f[3] = after((c_send, f[1], f[3]), gh_left, gh_right)
        c_got = flip(c_send, "wide", 1)
        f_got = flip(f[1], "narrow", 1), flip(f[3], "wide", 2)
        gx, *c = input_gradient(
            info_ext, conv_w, gh, gh_left, gh_right, gmixed, 0, half_rows,
            after_core(((c_keep, c_got),)),
        )
        c_got = flip(c[1], "narrow", 1), flip(c[3], "wide", 2)
        gx, *f = input_gradient(
            info_ext, conv_w, gh, gh_left, gh_right, gx, half_rows, half_rows,
            after_first(f[0], f_got[0], f[2], f_got[1]),
        )
        f_got = flip(f[1], "wide", 2), flip(f[3], "narrow", 1)
        c = after((c[0], c_got[0], c[2], c_got[1]), gx, f[1], f[3])
        c = alone(after_first(*c))
        c_got = flip(c[1], "wide", 2), flip(c[3], "narrow", 1)
        f = after_second(*after((f[0], f_got[0], f[2], f_got[1]), c[1], c[3]))
        c = after_second(*after((c[0], c_got[0], c[2], c_got[1]), f[0]))
        grad_w_out, grad_w_in, sums = small(
            last_ff_kernel, f,
            [
                (hidden_units // n_narrow, 128), (features // n_narrow, hidden_units // n_wide),
                sums.shape,
            ],
            F32,
        )
        grad_conv = small(last_conv_kernel, c, [(taps * features // n_narrow, 128)], F32)[0]
        grad_conv = grad_conv.reshape(taps, features // n_narrow, features // n_wide)
    sums = sums.reshape(-1)
    starts = [0, features, 2 * features, 3 * features]
    starts += [starts[-1] + hidden_units, starts[-1] + hidden_units + features]
    sizes = [features, features, features, hidden_units, features, features]
    vectors = [sums[a : a + n] for a, n in zip(starts, sizes, strict=True)]
    return (
        out, gx, grad_conv, vectors[0], vectors[1], vectors[2], grad_w_in, vectors[3],
        grad_w_out, vectors[4], vectors[5],
    )


def solution(mesh):
    split = P("narrow", "wide", None)
    placed = (split,) + (P(),) * 9 + (P("narrow", "wide"), P("narrow", None, "wide"), split)
    return jax.shard_map(
        body,
        mesh=mesh,
        in_specs=placed,
        out_specs=(
            split, split, P(None, "narrow", "wide"), P(), P(), P(), P("narrow", "wide"), P(),
            P("narrow", "wide"), P(), P(),
        ),
        check_vma=False,
    )
```

time: 268 us -> 176 us (0.66)
  blocking collectives: 46.7 us -> 0 us
  Pallas kernels: 139 us -> 98.2 us
  waiting for transfers between devices: 18.6 us -> 29.7 us
  local copies, waits for them, and re-layouts: 17.3 us -> 8.37 us
  starting transfers between devices: 41.1 us -> 38.1 us
    psum x1 -> x0, blocking collectives: 46.7 us -> none  [body(): sums = lax.psum(sums, ('wide', 'narrow'))]
    pallas_call x12 -> x4, Pallas kernels: 26.9 us -> 1.79 us  [small(): pl.pallas_call(kernel, out_shape=[shape(d, dtype) for d in dims], compile...]
    ppermute x24 -> x18, waiting for transfers between devices: 18.6 us -> 29.7 us  [flip(): return lax.ppermute(value, axis, [(i, i ^ bit) for i in range(size)])]
    pallas_call x4 -> x6, Pallas kernels: 97.1 us -> 86.9 us  [the longest x1 42.1 us: middle(): pl.pallas_call(functools.partial(middle_kernel, blocks), grid=(rows // bl...]
    transpose x2 -> x0, local copies, waits for them, and re-layouts: 7.47 us -> none  [the longest x1 6.66 us: body(): wt = jnp.transpose(conv_w, (0, 2, 1)).reshape(taps * features, features)]
    pallas_call x1, Pallas kernels: 15.5 us -> 9.56 us  [conv_inner(): pl.pallas_call(conv_inner_kernel, grid=(taps,), in_specs=[whole(info.shap...]
    ppermute x24 -> x18, starting transfers between devices: 27.4 us -> 23.5 us  [flip(): return lax.ppermute(value, axis, [(i, i ^ bit) for i in range(size)])]
    unnamed x87 -> x28, local copies, waits for them, and re-layouts: 5.63 us -> 3.72 us
  transfers between devices with their start and end apart: 30 -> 24, of which waited for: 4 -> 10; matrix products, arithmetic and copies ran while one was open for 5% -> 1% of each run, Pallas kernels for 21% -> 27%
where the time goes in v2:
time: 176 us
  Pallas kernels  98.2 us (56%)
  starting transfers between devices  38.1 us (22%)
  waiting for transfers between devices  29.7 us (17%)
  local copies, waits for them, and re-layouts  8.37 us (5%)
    pallas_call x1, Pallas kernels, middle(): pl.pallas_call(functools.partial(middle_kernel, blocks), grid=(rows // bl...  42.1 us
    ppermute x18, waiting for transfers between devices, flip(): return lax.ppermute(value, axis, [(i, i ^ bit) for i in range(size)])  29.7 us
    ppermute x18, starting transfers between devices, flip(): return lax.ppermute(value, axis, [(i, i ^ bit) for i in range(size)])  23.5 us
    pallas_call x2, Pallas kernels, input_gradient(): pl.pallas_call(functools.partial(input_kernel, first, light), grid=(taps,...  20.5 us
    pallas_call x1, Pallas kernels, weight_gradient(): pl.pallas_call(functools.partial(weight_kernel, blocks, light), grid=(tap...  16.6 us
    ppermute x3, starting transfers between devices, halos(): lax.ppermute(lax.slice_in_dim(value, last - reach, last, axis=dim), 'wide...  10.7 us
    pallas_call x1, Pallas kernels, conv_inner(): pl.pallas_call(conv_inner_kernel, grid=(taps,), in_specs=[whole(info.shap...  9.56 us
    pallas_call x1, Pallas kernels, conv_outer(): pl.pallas_call(conv_outer_kernel, grid=(taps - 1,), in_specs=[whole(info....  7.04 us
  transfers between devices with their start and end apart: 24, of which 10 were waited for; matrix products, arithmetic and copies ran while one was open for 1% of the time, Pallas kernels for 27%

profile of v2, /device:TPU:0, one launch (start us, length us, event | category | flops | bytes accessed | tf_op | source)
XLA Modules:
  0.0 175.5 jit_solution(7747995933299035076)
XLA Ops:
  0.7 3.2 %fusion.3 = (bf16[8,128,512]{2,1,0:T(8,128)(2,1)}, bf16[8,128,512]{2,1,0:T(8,128)(2,1)}) fusion(bf16[8,256,512]{2,1,0:T(8,128)(2,1)} %x_hbm.1), kind=kLoop, calls=%fused_computation.17 | loop fusion | bytes 4194304 | tf_op jit(solution)/shard_map/slice | solution.py:839
  3.9 1.3 collective-permute-start.3
  5.2 4.0 %collective-permute-start.2 = (bf16[8,128,512]{2,1,0:T(8,128)(2,1)}, bf16[8,128,512]{2,1,0:T(8,128)(2,1)}, u32[]{:S(2)}, u32[]{:S(2)}) collective-permute-start(bf16[8,128,512]{2,1,0:T(8,128)(2,1)} %get-tuple-element.122), channel_id=1, source_target_pairs={{0,8},{8,16},{16,24},{1,9},{9,17},{17,25},{2,10},{10,18},{18,26},{... | collective-permute-start | bytes 3145736 | tf_op jit(solution)/shard_map/ppermute | solution.py:838
  9.2 3.6 %collective-permute-start = (s32[10,8,128]{2,1,0:T(8,128)S(1)}, s32[10,8,128]{2,1,0:T(8,128)S(1)}, u32[]{:S(2)}, u32[]{:S(2)}) collective-permute-start(s32[10,8,128]{2,1,0:T(8,128)S(1)} %get-tuple-element.123), channel_id=1, source_target_pairs={{0,8},{8,16},{16,24},{1,9},{9,17},{17,25},{2,10},{10,18},{18,26},{... | collective-permute-start | bytes 122888 | tf_op jit(solution)/shard_map/ppermute | solution.py:838
  12.8 1.3 collective-permute-start.1
  14.3 2.3 %copy-done = bf16[9,512,512]{2,1,0:T(8,128)(2,1)S(1)} copy-done((bf16[9,512,512]{2,1,0:T(8,128)(2,1)S(1)}, bf16[9,512,512]{2,1,0:T(8,128)(2,1)}, u32[]{:S(2)}) %copy-start) | copy-done | bytes 4718616
  16.6 9.6 %conv_inner.1.acc_hbm = f32[8,256,512]{2,1,0:T(8,128)S(1)} custom-call(s32[10,8,256]{2,1,0:T(8,128)S(1)} %pad_add_fusion.1.info_ref, bf16[8,256,512]{2,1,0:T(8,128)(2,1)S(1)} %copy-done.2, bf16[9,512,512]{2,1,0:T(8,128)(2,1)S(1)} %copy-done), custom_call_target="tpu_custom_call" | custom-call | flops 6957847040 | bytes 11000000 | tf_op jit(solution)/shard_map/conv_inner/pallas_call | solution.py:115
  26.3 7.0 %conv_outer.1.hidden_ref = bf16[8,256,512]{2,1,0:T(8,128)(2,1)S(1)} custom-call(s32[10,8,512]{2,1,0:T(8,128)S(1)} %pad_add_fusion.info_ref, bf16[8,128,512]{2,1,0:T(8,128)(2,1)} %collective-permute-done.2.left_ref.left_hbm, bf16[8,128,512]{2,1,0:T(8,128)(2,1)} %collective-permute-done.3.right_ref.right_hbm, bf16[9,512,512]{2,1,0:T(8,128)(2,1)S(1)} %bitcast.24, ...), custom_call_target="tpu_custom_call" | custom-call | flops 2705829376 | bytes 11000000 | tf_op jit(solution)/shard_map/conv_outer/pallas_call | solution.py:189
  33.4 1.3 copy-done.1
  34.7 42.1 %middle.1 = (bf16[8,256,512]{2,1,0:T(8,128)(2,1)}, f32[8,256,512]{2,1,0:T(8,128)}, bf16[8,256,512]{2,1,0:T(8,128)(2,1)S(1)}, f32[64,128]{1,0:T(8,128)S(1)}, bf16...) custom-call(bf16[8,256,512]{2,1,0:T(8,128)(2,1)} %copy-done.1, ...), custom_call_target="tpu_custom_call" | custom-call | flops 25769803776 | bytes 34000000 | tf_op jit(solution)/shard_map/middle/pallas_call | solution.py:401
  76.8 2.2 %collective-permute-start.6 = (bf16[16,256,128]{2,1,0:T(8,128)(2,1)S(1)}, bf16[16,256,128]{2,1,0:T(8,128)(2,1)S(1)}, u32[]{:S(2)}, u32[]{:S(2)}) collective-permute-start(bf16[16,256,128]{2,1,0:T(8,128)(2,1)S(1)} %get-tuple-element.70), channel_id=1, source_target_pairs={{0,8},{8,0},{16,24},{24,16},{1,9},{9,1},{17,25},{25,17},{2,10},{10... | collective-permute-start | bytes 3145736 | tf_op jit(solution)/shard_map/ppermute | solution.py:666
  79.3 1.4 collective-permute-start.5
  80.7 3.1 %collective-permute-start.4 = (bf16[8,128,512]{2,1,0:T(8,128)(2,1)S(1)}, bf16[8,128,512]{2,1,0:T(8,128)(2,1)S(1)}, u32[]{:S(2)}, u32[]{:S(2)}) collective-permute-start(bf16[8,128,512]{2,1,0:T(8,128)(2,1)S(1)} %get-tuple-element.120), channel_id=1, source_target_pairs={{0,8},{8,16},{16,24},{1,9},{9,17},{17,25},{2,10},{10,18},{18,26},{... | collective-permute-start | bytes 3145736 | tf_op jit(solution)/shard_map/ppermute | solution.py:838
  83.8 1.7 collective-permute-start.8
  86.4 16.6 %weight_gradient.1 = (bf16[16,576,128]{2,1,0:T(8,128)(2,1)S(1)}, bf16[16,576,128]{2,1,0:T(8,128)(2,1)S(1)}, bf16[2,4,272,128]{3,2,1,0:T(8,128)(2,1)S(1)}, bf16[2...) custom-call(s32[10,8,512]{2,1,0:T(8,128)S(1)} %pad_add_fusion.info_ref, ...), custom_call_target="tpu_custom_call" | custom-call | flops 9663676416 | bytes 12000000 | tf_op jit(solution)/shard_map/weight_gradient/pallas_call | solution.py:565
  103.4 1.5 collective-permute-start.10
  104.9 1.9 %collective-permute-start.11 = (bf16[2,4,256,128]{3,2,1,0:T(8,128)(2,1)S(1)}, bf16[2,4,256,128]{3,2,1,0:T(8,128)(2,1)S(1)}, u32[]{:S(2)}, u32[]{:S(2)}) collective-permute-start(bf16[2,4,256,128]{3,2,1,0:T(8,128)(2,1)S(1)} %get-tuple-element.82), channel_id=1, source_target_pairs={{0,16},{8,24},{16,0},{24,8},{1,17},{9,25},{17,1},{25,9},{2,18},{10... | collective-permute-start | bytes 1572872 | tf_op jit(solution)/shard_map/ppermute | solution.py:666
  107.6 10.6 %input_gradient.2 = (f32[8,256,512]{2,1,0:T(8,128)}, bf16[2,4,288,128]{3,2,1,0:T(8,128)(2,1)S(1)}, bf16[2,4,288,128]{3,2,1,0:T(8,128)(2,1)S(1)}, bf16[2,4,288,12...) custom-call(s32[10,8,512]{2,1,0:T(8,128)S(1)} %pad_add_fusion.info_ref, ...), custom_call_target="tpu_custom_call", output_to_operand_aliasing={{0}: (5, {})} | custom-call | flops 4831838208 | bytes 12000000 | tf_op jit(solution)/shard_map/input_gradient/pallas_call | solution.py:636
  118.3 1.6 collective-permute-start.12
  119.8 1.8 %collective-permute-start.13 = (bf16[2,4,288,128]{3,2,1,0:T(8,128)(2,1)S(1)}, bf16[2,4,288,128]{3,2,1,0:T(8,128)(2,1)S(1)}, u32[]{:S(2)}, u32[]{:S(2)}) collective-permute-start(bf16[2,4,288,128]{3,2,1,0:T(8,128)(2,1)S(1)} %get-tuple-element.87), channel_id=1, source_target_pairs={{0,16},{8,24},{16,0},{24,8},{1,17},{9,25},{17,1},{25,9},{2,18},{10... | collective-permute-start | bytes 1769480 | tf_op jit(solution)/shard_map/ppermute | solution.py:666
  121.6 9.9 %input_gradient.3 = (f32[8,256,512]{2,1,0:T(8,128)}, bf16[4,288,128]{2,1,0:T(8,128)(2,1)S(1)}, bf16[4,288,128]{2,1,0:T(8,128)(2,1)S(1)}, bf16[4,256,128]{2,1,0:T(8,128)(2,1)S(1)}, bf16[4,256,128]{2,1,0:T(8,128)(2,1)S(1)}) custom-call(s32[10,8,512]{2,1,0:T(8,128)S(1)} %pad_add_fusion.info_ref, ...), custom_call_target="tpu_custom_call", output_to_operand_aliasing={{0}: (5, {})} | custom-call | flops 4831838208 | bytes 12000000 | tf_op jit(solution)/shard_map/input_gradient/pallas_call | solution.py:636
  132.4 1.5 collective-permute-done.12.refs_1_
  133.9 2.1 %collective-permute-done.13.refs_3_ = bf16[2,4,288,128]{3,2,1,0:T(8,128)(2,1)S(1)} collective-permute-done((bf16[2,4,288,128]{3,2,1,0:T(8,128)(2,1)S(1)}, bf16[2,4,288,128]{3,2,1,0:T(8,128)(2,1)S(1)}, u32[]{:S(2)}, u32[]{:S(2)}) %collective-permute-start.13) | collective-permute-done | bytes 589856 | tf_op jit(solution)/shard_map/ppermute | solution.py:666
  136.5 3.2 %collective-permute-done.17.b_got = bf16[4,256,128]{2,1,0:T(8,128)(2,1)S(1)} collective-permute-done((bf16[4,256,128]{2,1,0:T(8,128)(2,1)S(1)}, bf16[4,256,128]{2,1,0:T(8,128)(2,1)S(1)}, u32[]{:S(2)}, u32[]{:S(2)}) %collective-permute-start.17) | collective-permute-done | bytes 262176 | tf_op jit(solution)/shard_map/ppermute | solution.py:666
  139.7 1.8 %collective-permute-done.16.a_got = bf16[4,288,128]{2,1,0:T(8,128)(2,1)S(1)} collective-permute-done((bf16[4,288,128]{2,1,0:T(8,128)(2,1)S(1)}, bf16[4,288,128]{2,1,0:T(8,128)(2,1)S(1)}, u32[]{:S(2)}, u32[]{:S(2)}) %collective-permute-start.16) | collective-permute-done | bytes 294944 | tf_op jit(solution)/shard_map/ppermute | solution.py:666
  141.7 1.6 collective-permute-start.21
  143.3 2.6 %collective-permute-start.22 = (bf16[2,320,128]{2,1,0:T(8,128)(2,1)S(1)}, bf16[2,320,128]{2,1,0:T(8,128)(2,1)S(1)}, u32[]{:S(2)}, u32[]{:S(2)}) collective-permute-start(bf16[2,320,128]{2,1,0:T(8,128)(2,1)S(1)} %get-tuple-element.114), channel_id=1, source_target_pairs={{0,4},{1,5},{2,6},{3,7},{4,0},{5,1},{6,2},{7,3},{8,12},{9,13},{10,... | collective-permute-start | bytes 491528 | tf_op jit(solution)/shard_map/ppermute | solution.py:666
  146.1 1.7 collective-permute-start.14
  149.2 8.9 %collective-permute-done.22.z2 = bf16[2,320,128]{2,1,0:T(8,128)(2,1)S(1)} collective-permute-done((bf16[2,320,128]{2,1,0:T(8,128)(2,1)S(1)}, bf16[2,320,128]{2,1,0:T(8,128)(2,1)S(1)}, u32[]{:S(2)}, u32[]{:S(2)}) %collective-permute-start.22) | collective-permute-done | bytes 163872 | tf_op jit(solution)/shard_map/ppermute | solution.py:666
  159.7 2.4 %collective-permute-start.18 = (bf16[2,288,128]{2,1,0:T(8,128)(2,1)S(1)}, bf16[2,288,128]{2,1,0:T(8,128)(2,1)S(1)}, u32[]{:S(2)}, u32[]{:S(2)}) collective-permute-start(bf16[2,288,128]{2,1,0:T(8,128)(2,1)S(1)} %get-tuple-element.110), channel_id=1, source_target_pairs={{0,2},{1,3},{2,0},{3,1},{4,6},{5,7},{6,4},{7,5},{8,10},{9,11},{10,... | collective-permute-start | bytes 442376 | tf_op jit(solution)/shard_map/ppermute | solution.py:666
  163.2 1.4 collective-permute-start.20
  166.4 8.3 %collective-permute-done.19.z2 = bf16[2,288,128]{2,1,0:T(8,128)(2,1)S(1)} collective-permute-done((bf16[2,288,128]{2,1,0:T(8,128)(2,1)S(1)}, bf16[2,288,128]{2,1,0:T(8,128)(2,1)S(1)}, u32[]{:S(2)}, u32[]{:S(2)}) %collective-permute-start.19) | collective-permute-done | bytes 147488 | tf_op jit(solution)/shard_map/ppermute | solution.py:666
  (72 shorter events, 10.9 us)
Async XLA Ops:
  0.6 13.6 %copy-start.2 = (bf16[8,256,512]{2,1,0:T(8,128)(2,1)S(1)}, bf16[8,256,512]{2,1,0:T(8,128)(2,1)}, u32[]{:S(2)}) copy-start(bf16[8,256,512]{2,1,0:T(8,128)(2,1)} %x_hbm.1) | copy-start | bytes 6291460
  0.7 13.4 %copy-start.7 = (bf16[512]{0:T(512)(128)(2,1)S(1)}, bf16[512]{0:T(512)(128)(2,1)}, u32[]{:S(2)}) copy-start(bf16[512]{0:T(512)(128)(2,1)} %param.15) | copy-start | bytes 3076
  0.7 13.5 %copy-start.8 = (bf16[512]{0:T(512)(128)(2,1)S(1)}, bf16[512]{0:T(512)(128)(2,1)}, u32[]{:S(2)}) copy-start(bf16[512]{0:T(512)(128)(2,1)} %param.16) | copy-start | bytes 3076
  0.7 13.5 %copy-start.9 = (bf16[512]{0:T(512)(128)(2,1)S(1)}, bf16[512]{0:T(512)(128)(2,1)}, u32[]{:S(2)}) copy-start(bf16[512]{0:T(512)(128)(2,1)} %param.17) | copy-start | bytes 3076
  0.7 13.5 %copy-start.10 = (bf16[512]{0:T(512)(128)(2,1)S(1)}, bf16[512]{0:T(512)(128)(2,1)}, u32[]{:S(2)}) copy-start(bf16[512]{0:T(512)(128)(2,1)} %param.21) | copy-start | bytes 3076
  0.7 13.5 %copy-start.11 = (bf16[512]{0:T(512)(128)(2,1)S(1)}, bf16[512]{0:T(512)(128)(2,1)}, u32[]{:S(2)}) copy-start(bf16[512]{0:T(512)(128)(2,1)} %param.22) | copy-start | bytes 3076
  0.7 25.6 %slice-start = ((s8[4718592]{0:T(1024)(128)(4,1)}), s8[524288]{0:T(1024)(128)(4,1)S(1)}, s32[]{:S(2)}) async-start(s8[4718592]{0:T(1024)(128)(4,1)} %bitcast.23), calls=%async_computation | async-start | bytes 1048576
  3.9 22.3 %collective-permute-start.3 = (bf16[8,128,512]{2,1,0:T(8,128)(2,1)}, bf16[8,128,512]{2,1,0:T(8,128)(2,1)}, u32[]{:S(2)}, u32[]{:S(2)}) collective-permute-start(bf16[8,128,512]{2,1,0:T(8,128)(2,1)} %get-tuple-element.121), channel_id=1, source_target_pairs={{8,0},{16,8},{24,16},{9,1},{17,9},{25,17},{10,2},{18,10},{26,18},{... | collective-permute-start | bytes 3145736 | tf_op jit(solution)/shard_map/ppermute | solution.py:839
  5.2 21.1 %collective-permute-start.2 = (bf16[8,128,512]{2,1,0:T(8,128)(2,1)}, bf16[8,128,512]{2,1,0:T(8,128)(2,1)}, u32[]{:S(2)}, u32[]{:S(2)}) collective-permute-start(bf16[8,128,512]{2,1,0:T(8,128)(2,1)} %get-tuple-element.122), channel_id=1, source_target_pairs={{0,8},{8,16},{16,24},{1,9},{9,17},{17,25},{2,10},{10,18},{18,26},{... | collective-permute-start | bytes 3145736 | tf_op jit(solution)/shard_map/ppermute | solution.py:838
  9.2 17.0 %collective-permute-start = (s32[10,8,128]{2,1,0:T(8,128)S(1)}, s32[10,8,128]{2,1,0:T(8,128)S(1)}, u32[]{:S(2)}, u32[]{:S(2)}) collective-permute-start(s32[10,8,128]{2,1,0:T(8,128)S(1)} %get-tuple-element.123), channel_id=1, source_target_pairs={{0,8},{8,16},{16,24},{1,9},{9,17},{17,25},{2,10},{10,18},{18,26},{... | collective-permute-start | bytes 122888 | tf_op jit(solution)/shard_map/ppermute | solution.py:838
  12.8 13.4 %collective-permute-start.1 = (s32[10,8,128]{2,1,0:T(8,128)S(1)}, s32[10,8,128]{2,1,0:T(8,128)S(1)}, u32[]{:S(2)}, u32[]{:S(2)}) collective-permute-start(s32[10,8,128]{2,1,0:T(8,128)S(1)} %get-tuple-element.124), channel_id=1, source_target_pairs={{8,0},{16,8},{24,16},{9,1},{17,9},{25,17},{10,2},{18,10},{26,18},{... | collective-permute-start | bytes 122888 | tf_op jit(solution)/shard_map/ppermute | solution.py:839
  16.6 9.7 %slice-start.1 = ((s8[4718592]{0:T(1024)(128)(4,1)}), s8[4194304]{0:T(1024)(128)(4,1)S(1)}, s32[]{:S(2)}) async-start(s8[4718592]{0:T(1024)(128)(4,1)} %bitcast.23), calls=%async_computation.1 | async-start | bytes 8388608
  76.8 9.5 %collective-permute-start.6 = (bf16[16,256,128]{2,1,0:T(8,128)(2,1)S(1)}, bf16[16,256,128]{2,1,0:T(8,128)(2,1)S(1)}, u32[]{:S(2)}, u32[]{:S(2)}) collective-permute-start(bf16[16,256,128]{2,1,0:T(8,128)(2,1)S(1)} %get-tuple-element.70), channel_id=1, source_target_pairs={{0,8},{8,0},{16,24},{24,16},{1,9},{9,1},{17,25},{25,17},{2,10},{10... | collective-permute-start | bytes 3145736 | tf_op jit(solution)/shard_map/ppermute | solution.py:666
  79.0 7.4 %collective-permute-start.7 = (bf16[16,256,128]{2,1,0:T(8,128)(2,1)S(1)}, bf16[16,256,128]{2,1,0:T(8,128)(2,1)S(1)}, u32[]{:S(2)}, u32[]{:S(2)}) collective-permute-start(bf16[16,256,128]{2,1,0:T(8,128)(2,1)S(1)} %get-tuple-element.71), channel_id=1, source_target_pairs={{0,8},{8,0},{16,24},{24,16},{1,9},{9,1},{17,25},{25,17},{2,10},{10... | collective-permute-start | bytes 3145736 | tf_op jit(solution)/shard_map/ppermute | solution.py:666
  79.3 23.7 %collective-permute-start.5 = (bf16[8,128,512]{2,1,0:T(8,128)(2,1)S(1)}, bf16[8,128,512]{2,1,0:T(8,128)(2,1)S(1)}, u32[]{:S(2)}, u32[]{:S(2)}) collective-permute-start(bf16[8,128,512]{2,1,0:T(8,128)(2,1)S(1)} %get-tuple-element.119), channel_id=1, source_target_pairs={{8,0},{16,8},{24,16},{9,1},{17,9},{25,17},{10,2},{18,10},{26,18},{... | collective-permute-start | bytes 3145736 | tf_op jit(solution)/shard_map/ppermute | solution.py:839
  80.7 22.3 %collective-permute-start.4 = (bf16[8,128,512]{2,1,0:T(8,128)(2,1)S(1)}, bf16[8,128,512]{2,1,0:T(8,128)(2,1)S(1)}, u32[]{:S(2)}, u32[]{:S(2)}) collective-permute-start(bf16[8,128,512]{2,1,0:T(8,128)(2,1)S(1)} %get-tuple-element.120), channel_id=1, source_target_pairs={{0,8},{8,16},{16,24},{1,9},{9,17},{17,25},{2,10},{10,18},{18,26},{... | collective-permute-start | bytes 3145736 | tf_op jit(solution)/shard_map/ppermute | solution.py:838
  83.8 2.5 %collective-permute-start.8 = (f32[64,128]{1,0:T(8,128)S(1)}, f32[64,128]{1,0:T(8,128)S(1)}, u32[]{:S(2)}, u32[]{:S(2)}) collective-permute-start(f32[64,128]{1,0:T(8,128)S(1)} %get-tuple-element.72.rest_4_), channel_id=1, source_target_pairs={{0,8},{8,0},{16,24},{24,16},{1,9},{9,1},{17,25},{25,17},{2,10},{10... | collective-permute-start | bytes 98312 | tf_op jit(solution)/shard_map/ppermute | solution.py:666
  103.0 4.6 %collective-permute-start.9 = (bf16[16,576,128]{2,1,0:T(8,128)(2,1)S(1)}, bf16[16,576,128]{2,1,0:T(8,128)(2,1)S(1)}, u32[]{:S(2)}, u32[]{:S(2)}) collective-permute-start(bf16[16,576,128]{2,1,0:T(8,128)(2,1)S(1)} %get-tuple-element.77), channel_id=1, source_target_pairs={{0,8},{8,0},{16,24},{24,16},{1,9},{9,1},{17,25},{25,17},{2,10},{10... | collective-permute-start | bytes 7077896 | tf_op jit(solution)/shard_map/ppermute | solution.py:666
  103.4 18.2 %collective-permute-start.10 = (bf16[2,4,272,128]{3,2,1,0:T(8,128)(2,1)S(1)}, bf16[2,4,272,128]{3,2,1,0:T(8,128)(2,1)S(1)}, u32[]{:S(2)}, u32[]{:S(2)}) collective-permute-start(bf16[2,4,272,128]{3,2,1,0:T(8,128)(2,1)S(1)} %get-tuple-element.80), channel_id=1, source_target_pairs={{0,1},{1,0},{2,3},{3,2},{4,5},{5,4},{6,7},{7,6},{8,9},{9,8},{10,11... | collective-permute-start | bytes 1671176 | tf_op jit(solution)/shard_map/ppermute | solution.py:666
  104.9 16.7 %collective-permute-start.11 = (bf16[2,4,256,128]{3,2,1,0:T(8,128)(2,1)S(1)}, bf16[2,4,256,128]{3,2,1,0:T(8,128)(2,1)S(1)}, u32[]{:S(2)}, u32[]{:S(2)}) collective-permute-start(bf16[2,4,256,128]{3,2,1,0:T(8,128)(2,1)S(1)} %get-tuple-element.82), channel_id=1, source_target_pairs={{0,16},{8,24},{16,0},{24,8},{1,17},{9,25},{17,1},{25,9},{2,18},{10... | collective-permute-start | bytes 1572872 | tf_op jit(solution)/shard_map/ppermute | solution.py:666
  118.3 15.6 %collective-permute-start.12 = (bf16[2,4,288,128]{3,2,1,0:T(8,128)(2,1)S(1)}, bf16[2,4,288,128]{3,2,1,0:T(8,128)(2,1)S(1)}, u32[]{:S(2)}, u32[]{:S(2)}) collective-permute-start(bf16[2,4,288,128]{3,2,1,0:T(8,128)(2,1)S(1)} %get-tuple-element.85), channel_id=1, source_target_pairs={{0,1},{1,0},{2,3},{3,2},{4,5},{5,4},{6,7},{7,6},{8,9},{9,8},{10,11... | collective-permute-start | bytes 1769480 | tf_op jit(solution)/shard_map/ppermute | solution.py:666
  119.8 16.2 %collective-permute-start.13 = (bf16[2,4,288,128]{3,2,1,0:T(8,128)(2,1)S(1)}, bf16[2,4,288,128]{3,2,1,0:T(8,128)(2,1)S(1)}, u32[]{:S(2)}, u32[]{:S(2)}) collective-permute-start(bf16[2,4,288,128]{3,2,1,0:T(8,128)(2,1)S(1)} %get-tuple-element.87), channel_id=1, source_target_pairs={{0,16},{8,24},{16,0},{24,8},{1,17},{9,25},{17,1},{25,9},{2,18},{10... | collective-permute-start | bytes 1769480 | tf_op jit(solution)/shard_map/ppermute | solution.py:666
  131.6 10.0 %collective-permute-start.16 = (bf16[4,288,128]{2,1,0:T(8,128)(2,1)S(1)}, bf16[4,288,128]{2,1,0:T(8,128)(2,1)S(1)}, u32[]{:S(2)}, u32[]{:S(2)}) collective-permute-start(bf16[4,288,128]{2,1,0:T(8,128)(2,1)S(1)} %get-tuple-element.88), channel_id=1, source_target_pairs={{0,16},{8,24},{16,0},{24,8},{1,17},{9,25},{17,1},{25,9},{2,18},{10... | collective-permute-start | bytes 884744 | tf_op jit(solution)/shard_map/ppermute | solution.py:666
  131.8 7.9 %collective-permute-start.17 = (bf16[4,256,128]{2,1,0:T(8,128)(2,1)S(1)}, bf16[4,256,128]{2,1,0:T(8,128)(2,1)S(1)}, u32[]{:S(2)}, u32[]{:S(2)}) collective-permute-start(bf16[4,256,128]{2,1,0:T(8,128)(2,1)S(1)} %get-tuple-element.89), channel_id=1, source_target_pairs={{0,1},{1,0},{2,3},{3,2},{4,5},{5,4},{6,7},{7,6},{8,9},{9,8},{10,11... | collective-permute-start | bytes 786440 | tf_op jit(solution)/shard_map/ppermute | solution.py:666
  141.7 7.6 %collective-permute-start.21 = (bf16[2,320,128]{2,1,0:T(8,128)(2,1)S(1)}, bf16[2,320,128]{2,1,0:T(8,128)(2,1)S(1)}, u32[]{:S(2)}, u32[]{:S(2)}) collective-permute-start(bf16[2,320,128]{2,1,0:T(8,128)(2,1)S(1)} %get-tuple-element.113), channel_id=1, source_target_pairs={{0,2},{1,3},{2,0},{3,1},{4,6},{5,7},{6,4},{7,5},{8,10},{9,11},{10,... | collective-permute-start | bytes 491528 | tf_op jit(solution)/shard_map/ppermute | solution.py:666
  143.3 14.9 %collective-permute-start.22 = (bf16[2,320,128]{2,1,0:T(8,128)(2,1)S(1)}, bf16[2,320,128]{2,1,0:T(8,128)(2,1)S(1)}, u32[]{:S(2)}, u32[]{:S(2)}) collective-permute-start(bf16[2,320,128]{2,1,0:T(8,128)(2,1)S(1)} %get-tuple-element.114), channel_id=1, source_target_pairs={{0,4},{1,5},{2,6},{3,7},{4,0},{5,1},{6,2},{7,3},{8,12},{9,13},{10,... | collective-permute-start | bytes 491528 | tf_op jit(solution)/shard_map/ppermute | solution.py:666
  145.9 12.3 %collective-permute-start.23 = (bf16[2,320,128]{2,1,0:T(8,128)(2,1)S(1)}, bf16[2,320,128]{2,1,0:T(8,128)(2,1)S(1)}, u32[]{:S(2)}, u32[]{:S(2)}) collective-permute-start(bf16[2,320,128]{2,1,0:T(8,128)(2,1)S(1)} %get-tuple-element.115), channel_id=1, source_target_pairs={{0,6},{1,7},{2,4},{3,5},{4,2},{5,3},{6,0},{7,1},{8,14},{9,15},{10,... | collective-permute-start | bytes 491528 | tf_op jit(solution)/shard_map/ppermute | solution.py:666
  146.1 13.4 %collective-permute-start.14 = (bf16[4,288,128]{2,1,0:T(8,128)(2,1)S(1)}, bf16[4,288,128]{2,1,0:T(8,128)(2,1)S(1)}, u32[]{:S(2)}, u32[]{:S(2)}) collective-permute-start(bf16[4,288,128]{2,1,0:T(8,128)(2,1)S(1)} %get-tuple-element.95), channel_id=1, source_target_pairs={{0,16},{8,24},{16,0},{24,8},{1,17},{9,25},{17,1},{25,9},{2,18},{10... | collective-permute-start | bytes 884744 | tf_op jit(solution)/shard_map/ppermute | solution.py:666
  147.9 11.7 %collective-permute-start.15 = (bf16[4,288,128]{2,1,0:T(8,128)(2,1)S(1)}, bf16[4,288,128]{2,1,0:T(8,128)(2,1)S(1)}, u32[]{:S(2)}, u32[]{:S(2)}) collective-permute-start(bf16[4,288,128]{2,1,0:T(8,128)(2,1)S(1)} %get-tuple-element.97), channel_id=1, source_target_pairs={{0,1},{1,0},{2,3},{3,2},{4,5},{5,4},{6,7},{7,6},{8,9},{9,8},{10,11... | collective-permute-start | bytes 884744 | tf_op jit(solution)/shard_map/ppermute | solution.py:666
  159.7 6.7 %collective-permute-start.18 = (bf16[2,288,128]{2,1,0:T(8,128)(2,1)S(1)}, bf16[2,288,128]{2,1,0:T(8,128)(2,1)S(1)}, u32[]{:S(2)}, u32[]{:S(2)}) collective-permute-start(bf16[2,288,128]{2,1,0:T(8,128)(2,1)S(1)} %get-tuple-element.110), channel_id=1, source_target_pairs={{0,2},{1,3},{2,0},{3,1},{4,6},{5,7},{6,4},{7,5},{8,10},{9,11},{10,... | collective-permute-start | bytes 442376 | tf_op jit(solution)/shard_map/ppermute | solution.py:666
  162.0 12.7 %collective-permute-start.19 = (bf16[2,288,128]{2,1,0:T(8,128)(2,1)S(1)}, bf16[2,288,128]{2,1,0:T(8,128)(2,1)S(1)}, u32[]{:S(2)}, u32[]{:S(2)}) collective-permute-start(bf16[2,288,128]{2,1,0:T(8,128)(2,1)S(1)} %get-tuple-element.111), channel_id=1, source_target_pairs={{0,4},{1,5},{2,6},{3,7},{4,0},{5,1},{6,2},{7,3},{8,12},{9,13},{10,... | collective-permute-start | bytes 442376 | tf_op jit(solution)/shard_map/ppermute | solution.py:666
  163.2 11.6 %collective-permute-start.20 = (bf16[2,288,128]{2,1,0:T(8,128)(2,1)S(1)}, bf16[2,288,128]{2,1,0:T(8,128)(2,1)S(1)}, u32[]{:S(2)}, u32[]{:S(2)}) collective-permute-start(bf16[2,288,128]{2,1,0:T(8,128)(2,1)S(1)} %get-tuple-element.112), channel_id=1, source_target_pairs={{0,6},{1,7},{2,4},{3,5},{4,2},{5,3},{6,0},{7,1},{8,14},{9,15},{10,... | collective-permute-start | bytes 442376 | tf_op jit(solution)/shard_map/ppermute | solution.py:666
  (6 other events, 37.7 us)

commit v3 on v2

v3 whole, which is shorter than its diff:
```python
import functools
from typing import Any, NamedTuple

import jax
import jax.numpy as jnp
from jax import lax
from jax.experimental import pallas as pl
from jax.experimental.pallas import tpu as pltpu
from jax.sharding import PartitionSpec as P

STEP = 32
BF = jnp.bfloat16
F32 = jnp.float32
RSQRT2 = 0.7071067811865476
RSQRT2PI = 0.3989422804014327
EPS = 1e-05


def params(mebibytes):
    return pltpu.CompilerParams(vmem_limit_bytes=mebibytes * 1024 * 1024)


def cost(flops, moved):
    return pl.CostEstimate(
        flops=int(flops / 50), bytes_accessed=int(moved / 50), transcendentals=0
    )


def whole(shape):
    rank = len(shape)
    return pl.BlockSpec(shape, lambda *_: (0,) * rank, pipeline_mode=pl.Buffered(1))


def shape(dims, dtype):
    return jax.ShapeDtypeStruct(dims, dtype)


def mask_columns(matched):
    return jnp.where(matched, 1.0, 0.0).astype(F32).T


def spread(column, width):
    wide = jnp.broadcast_to(column, (column.shape[0], 128)).astype(BF)
    return jnp.concatenate([wide] * (width // 128), axis=1)


def dot(left, right, left_dim, right_dim):
    return lax.dot_general(
        left, right, (((left_dim,), (right_dim,)), ((), ())), preferred_element_type=F32
    )


def cdf_and_exp(values):
    return 0.5 + 0.5 * lax.erf(values * RSQRT2), jnp.exp(-0.5 * values * values)


def in_pair(value):
    high = value.astype(BF)
    return high, (value - high.astype(F32)).astype(BF)


def fold(values):
    return values.reshape(-1, 8, values.shape[-1]).sum(0)


PACK_ROWS = 32


def pack_kernel(
    x_hbm, ids_hbm, used_hbm, left_ref, right_ref, info_ref, ids, sems, info_sems
):
    rows, own, features = x_hbm.shape
    count = info_ref.shape[0]
    reach = (left_ref.shape[0] - PACK_ROWS) // rows
    loads = [
        pltpu.make_async_copy(ids_hbm, ids, info_sems.at[0]),
        pltpu.make_async_copy(used_hbm, info_ref.at[pl.ds(1, count - 1)], info_sems.at[1]),
    ]
    for load in loads:
        load.start()
    copies = []
    for side, (out, start) in enumerate(((left_ref, 0), (right_ref, own - reach))):
        for r in range(rows):
            copies.append(
                pltpu.make_async_copy(
                    x_hbm.at[r, pl.ds(start, reach), :],
                    out.at[pl.ds(r * reach, reach), :],
                    sems.at[side * rows + r],
                )
            )
            copies[-1].start()
    for load in loads:
        load.wait()
    info_ref[0] = ids[...] + 1
    for side, (out, start) in enumerate(((left_ref, 0), (right_ref, own - reach))):
        lines = []
        for q in range(PACK_ROWS // rows):
            group = [
                info_ref[k, :, start : start + reach].astype(F32)
                if k < count
                else jnp.zeros((rows, reach), F32)
                for k in range(q * features // reach, (q + 1) * features // reach)
            ]
            lines.append(jnp.concatenate(group, axis=1))
        out[rows * reach :, :] = jnp.concatenate(lines, axis=0).astype(BF)
    for copy in copies:
        copy.wait()


def pack(x, ids, used, reach):
    rows, own, features = x.shape
    packed = shape((rows * reach + PACK_ROWS, features), BF)
    return pl.pallas_call(
        pack_kernel,
        grid=(1,),
        in_specs=[pl.BlockSpec(memory_space=pltpu.HBM)] * 3,
        out_specs=[whole(packed.shape)] * 2 + [whole((1 + used.shape[0], rows, own))],
        out_shape=[packed, packed, shape((1 + used.shape[0], rows, own), jnp.int32)],
        scratch_shapes=[
            pltpu.VMEM(ids.shape, jnp.int32),
            pltpu.SemaphoreType.DMA((2 * rows,)),
            pltpu.SemaphoreType.DMA((2,)),
        ],
        compiler_params=params(6),
        cost_estimate=cost(1e6, 4e6),
        name="pack",
    )(x, ids, used)


def put_masked(lhs, sources, columns, n, features):
    for r, source in enumerate(sources):
        lhs[r * n : (r + 1) * n, :] = source * spread(columns[:, r : r + 1], features)


def conv_inner_kernel(info_ref, x_ref, w_ref, acc_ref, even, odd):
    step = pl.program_id(0)
    rows, own, features = x_ref.shape
    taps = info_ref.shape[0] - 1
    half = taps // 2
    order = [half] + [k for k in range(taps) if k != half]
    buffers = (even, odd)

    def span(k):
        shift = STEP * (k - half)
        return max(0, -shift), own - max(0, shift), shift

    def build(i):
        k = order[i]
        low, high, shift = span(k)
        ids = info_ref[0]
        matched = (ids[:, low + shift : high + shift] == ids[:, low:high]) & (
            info_ref[1 + k][:, low:high] == 1
        )
        put_masked(
            buffers[i % 2],
            [x_ref[r, low + shift : high + shift, :] for r in range(rows)],
            mask_columns(matched), high - low, features,
        )

    def run(i):
        low, high, _ = span(order[i])
        n = high - low
        if i + 1 < taps:
            build(i + 1)
        product = dot(buffers[i % 2][: rows * n, :], w_ref[0], 1, 0).reshape(rows, n, features)
        if i == 0:
            acc_ref[...] = product
        else:
            acc_ref[:, low:high, :] += product

    pl.when(step == 0)(functools.partial(build, 0))
    for i in range(taps):
        pl.when(step == i)(functools.partial(run, i))


def conv_inner(info, x, conv_w):
    rows, own, features = x.shape
    taps = conv_w.shape[0]
    half = taps // 2

    def tap_of(i):
        return jnp.where(i == 0, half, jnp.where(i <= half, i - 1, i))

    return pl.pallas_call(
        conv_inner_kernel,
        grid=(taps,),
        in_specs=[
            whole(info.shape),
            whole(x.shape),
            pl.BlockSpec((1, features, features), lambda i: (tap_of(i), 0, 0)),
        ],
        out_specs=whole(x.shape),
        out_shape=shape(x.shape, F32),
        scratch_shapes=[pltpu.VMEM((rows * own, features), BF)] * 2,
        compiler_params=params(20),
        cost_estimate=cost(2 * rows * own * features * features * taps * 0.72, 11e6),
        name="conv_inner",
    )(info, x, conv_w)


def conv_outer_kernel(
    own_info_ref, left_ref, right_ref, w_ref, vec_ref, acc_hbm, hidden_ref, info_ref, acc, even, odd, sem
):
    step = pl.program_id(0)
    rows, own, features = hidden_ref.shape
    taps = info_ref.shape[0] - 1
    half = taps // 2
    reach = STEP * half
    order = [k for k in range(taps) if k != half]
    buffers = (even, odd)
    load = pltpu.make_async_copy(acc_hbm, acc, sem)

    def span(k):
        n = STEP * abs(k - half)
        return (0 if k < half else own - n), n

    def build(i):
        k = order[i]
        low, n = span(k)
        left = k < half
        source = reach - n if left else 0
        shift = -n if left else n
        at = reach + low
        ids = info_ref[0]
        matched = (info_ref[1 + k][:, at : at + n] == 1) & (
            ids[:, at + shift : at + shift + n] == ids[:, at : at + n]
        )
        halo = left_ref if left else right_ref
        put_masked(
            buffers[i % 2],
            [halo[r * reach + source : r * reach + source + n, :] for r in range(rows)],
            mask_columns(matched), n, features,
        )

    def run(i):
        low, n = span(order[i])
        if i + 1 < len(order):
            build(i + 1)
        product = dot(buffers[i % 2][: rows * n, :], w_ref[0], 1, 0).reshape(rows, n, features)
        acc[:, low : low + n, :] += product

    @pl.when(step == 0)
    def _():
        load.start()
        for halo, at in ((left_ref, 0), (right_ref, reach + own)):
            lines = halo[rows * reach :, :].astype(F32)
            for k in range(taps + 1):
                q, m = divmod(k, features // reach)
                part = lines[q * rows : (q + 1) * rows, m * reach : (m + 1) * reach]
                info_ref[k, :, at : at + reach] = part.astype(jnp.int32)
        info_ref[:, :, reach : reach + own] = own_info_ref[...]
        build(0)
        load.wait()

    for i in range(len(order)):
        pl.when(step == i)(functools.partial(run, i))

    @pl.when(step == len(order) - 1)
    def _():
        hidden_ref[...] = (acc[...] + vec_ref[0:1, :]).astype(BF)


def conv_outer(info, acc, left, right, conv_w, vec):
    rows, own, features = acc.shape
    taps = conv_w.shape[0]
    half = taps // 2
    reach = STEP * half
    info_dims = (1 + taps, rows, own + 2 * reach)
    return pl.pallas_call(
        conv_outer_kernel,
        grid=(taps - 1,),
        in_specs=[
            whole(info.shape),
            whole(left.shape),
            whole(right.shape),
            pl.BlockSpec((1, features, features), lambda i: (jnp.where(i < half, i, i + 1), 0, 0)),
            whole(vec.shape),
            pl.BlockSpec(memory_space=pl.ANY),
        ],
        out_specs=[whole(acc.shape), whole(info_dims)],
        out_shape=[shape(acc.shape, BF), shape(info_dims, jnp.int32)],
        scratch_shapes=[pltpu.VMEM(acc.shape, F32)]
        + [pltpu.VMEM((rows * reach, features), BF)] * 2
        + [pltpu.SemaphoreType.DMA],
        compiler_params=params(18),
        cost_estimate=cost(2 * rows * own * features * features * taps * 0.28, 11e6),
        name="conv_outer",
    )(info, left, right, conv_w, vec, acc)


def place_block(out_ref, value, dest_wide, dest_narrow, rows_at, blocks):
    if blocks == (1, 1):
        out_ref[0, 0, rows_at, :] = value
        return
    rel_wide = lax.axis_index("wide") ^ dest_wide
    rel_narrow = lax.axis_index("narrow") ^ dest_narrow
    index = (rel_wide >> 1) * 8 + (rel_narrow & 1) * 4 + (rel_narrow >> 1)
    out_ref[rel_wide & 1, index, rows_at, :] = value


def ship(pairs, sems):
    copies = [pltpu.make_async_copy(src, dst, sems.at[i]) for i, (src, dst) in enumerate(pairs)]
    for copy in copies:
        copy.start()
    for copy in copies:
        copy.wait()


def gradient_outputs(blocks, height, width):
    if blocks == (1, 1):
        dims = (1, 1, height, width)
        return [shape(dims, BF)], [whole(dims)], []
    n_wide, n_narrow = blocks
    height, width = height // n_narrow, width // n_wide
    dims = (n_wide * n_narrow // 2, height, width)
    return (
        [shape(dims, BF)] * 2,
        [pl.BlockSpec(memory_space=pl.ANY)] * 2,
        [pltpu.VMEM((2,) + dims, BF), pltpu.SemaphoreType.DMA((2,))],
    )


def moments(values):
    centered = values - jnp.mean(values, axis=1, keepdims=True)
    return centered, lax.rsqrt(jnp.mean(centered * centered, axis=1, keepdims=True) + EPS)


def middle_kernel(
    blocks,
    hidden_ref, x_ref, ct_ref, w_in_ref, w_out_ref, vec_ref, b_in_ref,
    out_ref, gmixed_ref, gh_ref, *rest,
):
    if blocks == (1, 1):
        gw_out_ref, gw_in_ref, sums_ref, *rest = rest
    else:
        keep_ref, send_ref, *rest = rest
    (
        act_scr, slope_scr, up_scr, gw_out_acc, gw_in_acc, b_in_acc, gain_one_acc,
        bias_one_acc, gain_two_acc, bias_two_acc, conv_b_acc, *rest,
    ) = rest
    if blocks != (1, 1):
        gw_ref, sums_ref, sems = rest
        gw_out_ref = gw_in_ref = gw_ref
    step = pl.program_id(0)
    steps = pl.num_programs(0)
    size = act_scr.shape[0]
    features, hidden_units = w_in_ref.shape

    @pl.when(step == 0)
    def _():
        for ref in (
            gw_out_acc, gw_in_acc, b_in_acc, gain_one_acc, bias_one_acc, gain_two_acc,
            bias_two_acc, conv_b_acc,
        ):
            ref[...] = jnp.zeros_like(ref)

    gain_one = vec_ref[1:2, :]
    bias_one = vec_ref[2:3, :]
    gain_two = vec_ref[3:4, :]
    bias_two = vec_ref[4:5, :]
    chunk = 512
    count = hidden_units // chunk
    pieces = [slice(j * chunk, (j + 1) * chunk) for j in range(count)]

    hid = hidden_ref[...].reshape(size, features).astype(F32)
    centered, scale = moments(hid * (0.5 + 0.5 * lax.erf(hid * RSQRT2)))
    mixed = x_ref[...].reshape(size, features).astype(F32) + (
        centered * scale * gain_one + bias_one
    )
    mixed_low = mixed.astype(BF)

    def up_part(cols):
        return dot(mixed_low, w_in_ref[:, cols], 1, 0) + b_in_ref[:, cols]

    projected = None
    up = up_part(pieces[0])
    for j, cols in enumerate(pieces):
        ahead = up_part(pieces[j + 1]) if j + 1 < count else None
        cdf, bell = cdf_and_exp(up)
        act_low = (up * cdf).astype(BF)
        slope_scr[:, cols] = cdf + up * bell * RSQRT2PI
        act_scr[:, cols] = act_low
        part = dot(act_low, w_out_ref[cols, :], 1, 0)
        projected = part if projected is None else projected + part
        up = ahead
    centered, scale = moments(projected)
    xhat = centered * scale
    out_ref[...] = (mixed + (xhat * gain_two + bias_two)).astype(BF).reshape(out_ref.shape)
    ct = ct_ref[...].reshape(size, features).astype(F32)
    gain_two_acc[...] += fold(ct * xhat)
    bias_two_acc[...] += fold(ct)
    e = ct * gain_two
    mean_e = jnp.mean(e, axis=1, keepdims=True)
    mean_ex = jnp.mean(e * xhat, axis=1, keepdims=True)
    gproj = (scale * (e - mean_e - xhat * mean_ex)).astype(BF)

    for cols in pieces:
        g_act = dot(gproj, w_out_ref[cols, :], 1, 1)
        up_low = (g_act * slope_scr[:, cols]).astype(BF)
        up_scr[:, cols] = up_low
        b_in_acc[:, cols] += fold(up_low.astype(F32))
    total = dot(up_scr[...], w_in_ref[...], 1, 1)
    for cols in pieces:
        gw_out_acc[cols, :] += dot(act_scr[:, cols], gproj, 0, 0)
        gw_in_acc[:, cols] += dot(mixed_low, up_scr[:, cols], 0, 0)
    g_mixed = ct_ref[...].reshape(size, features).astype(F32) + total
    gmixed_ref[...] = g_mixed.reshape(gmixed_ref.shape)
    hid = hidden_ref[...].reshape(size, features).astype(F32)
    cdf, bell = cdf_and_exp(hid)
    centered, scale = moments(hid * cdf)
    yhat = centered * scale
    gain_one_acc[...] += fold(g_mixed * yhat)
    bias_one_acc[...] += fold(g_mixed)
    e = g_mixed * gain_one
    mean_e = jnp.mean(e, axis=1, keepdims=True)
    mean_ey = jnp.mean(e * yhat, axis=1, keepdims=True)
    g_hidden = scale * (e - mean_e - yhat * mean_ey) * (cdf + hid * bell * RSQRT2PI)
    g_low = g_hidden.astype(BF)
    gh_ref[...] = g_low.reshape(gh_ref.shape)
    conv_b_acc[...] += fold(g_low.astype(F32))

    @pl.when(step == steps - 1)
    def _():
        row = 0
        for ref in (conv_b_acc, gain_one_acc, bias_one_acc, b_in_acc, gain_two_acc, bias_two_acc):
            summed = jnp.sum(ref[...], axis=0, keepdims=True)
            for j in range(ref.shape[1] // 128):
                sums_ref[row : row + 1, :] = summed[:, j * 128 : (j + 1) * 128]
                row += 1
        sums_ref[row:, :] = jnp.zeros_like(sums_ref[row:, :])
        n_wide, n_narrow = blocks
        height, width = features // n_narrow, hidden_units // n_wide
        lanes = gw_in_ref.shape[-1]
        base = 0 if blocks == (1, 1) else hidden_units // n_narrow
        for w in range(n_wide):
            product = gw_in_acc[:, w * width : (w + 1) * width].astype(BF)
            for n in range(n_narrow):
                for j in range(width // lanes):
                    place_block(
                        gw_in_ref,
                        product[n * height : (n + 1) * height, j * lanes : (j + 1) * lanes],
                        w, n, slice(base + j * height, base + (j + 1) * height), blocks,
                    )
        height, width = hidden_units // n_narrow, features // n_wide
        for n in range(n_narrow):
            product = gw_out_acc[n * height : (n + 1) * height, :].astype(BF)
            for w in range(n_wide):
                place_block(
                    gw_out_ref, product[:, w * width : (w + 1) * width], w, n, slice(0, height),
                    blocks,
                )
        if blocks != (1, 1):
            last = gw_ref.shape[2] - 16
            for i, part in enumerate(in_pair(sums_ref[...])):
                for j in range(4):
                    for side in range(2):
                        gw_ref[side, 4 * i + j, last:, :] = part[16 * j : 16 * (j + 1)]
            ship(((gw_ref.at[0], keep_ref), (gw_ref.at[1], send_ref)), sems)


def middle(blocks, hidden, x, ct, w_in, w_out, vec, b_in):
    rows, own, features = x.shape
    hidden_units = w_in.shape[1]
    block_rows = 2
    size = block_rows * own
    total = rows * own
    row_block = pl.BlockSpec((block_rows, own, features), lambda i: (i, 0, 0))
    sums = ((5 * features + hidden_units) // 128 + 63) // 64 * 64
    if blocks == (1, 1):
        dims = [(1, 1, hidden_units, features), (1, 1, features, hidden_units)]
        shapes = [shape(d, BF) for d in dims] + [shape((sums, 128), F32)]
        specs = [whole(v.shape) for v in shapes]
        scratch = []
    else:
        n_wide, n_narrow = blocks
        height = 2 * features * hidden_units // (n_wide * n_narrow * 128) + 16
        shapes = [shape((n_wide * n_narrow // 2, height, 128), BF)] * 2
        specs = [pl.BlockSpec(memory_space=pl.ANY)] * 2
        scratch = [
            pltpu.VMEM((2,) + shapes[0].shape, BF), pltpu.VMEM((sums, 128), F32),
            pltpu.SemaphoreType.DMA((2,)),
        ]
    narrow = pltpu.VMEM((8, features), F32)
    return pl.pallas_call(
        functools.partial(middle_kernel, blocks),
        grid=(rows // block_rows,),
        in_specs=[
            row_block, row_block, row_block, whole(w_in.shape), whole(w_out.shape),
            whole(vec.shape), whole(b_in.shape),
        ],
        out_specs=[row_block, row_block, row_block] + specs,
        out_shape=[shape(x.shape, BF), shape(x.shape, F32), shape(x.shape, BF)] + shapes,
        scratch_shapes=[
            pltpu.VMEM((size, hidden_units), BF), pltpu.VMEM((size, hidden_units), F32),
            pltpu.VMEM((size, hidden_units), BF),
            pltpu.VMEM((hidden_units, features), F32), pltpu.VMEM((features, hidden_units), F32),
            pltpu.VMEM((8, hidden_units), F32), narrow, narrow, narrow, narrow, narrow,
        ] + scratch,
        compiler_params=params(46),
        cost_estimate=cost(2 * total * features * 6 * hidden_units, 34e6),
        name="middle",
    )(hidden, x, ct, w_in, w_out, vec, b_in)


def by_parity(step, run, even, odd):
    pl.when(step % 2 == 0)(lambda: run(even, odd))
    pl.when(step % 2 == 1)(lambda: run(odd, even))


def fill_copies(ext, left_hbm, own_hbm, right_hbm, sems):
    rows, own = own_hbm.shape[0], own_hbm.shape[1]
    reach = (ext.shape[1] - own) // 2
    copies = [pltpu.make_async_copy(own_hbm, ext.at[:, pl.ds(reach, own), :], sems.at[0])]
    for side, (halo, at) in enumerate(((left_hbm, 0), (right_hbm, reach + own))):
        for r in range(rows):
            source = halo.at[r] if len(halo.shape) == 3 else halo.at[pl.ds(r * reach, reach), :]
            copies.append(
                pltpu.make_async_copy(
                    source, ext.at[r, pl.ds(at, reach), :], sems.at[1 + side * rows + r]
                )
            )
    return copies


def build_masked(lhs, ext, info_ref, tap, forward_masks, first=0):
    rows, extended, features = ext.shape
    taps = info_ref.shape[0] - 1
    reach = STEP * (taps // 2)
    own = extended - 2 * reach
    offset = STEP * tap if forward_masks else STEP * (taps - 1 - tap)
    ids = info_ref[0]
    moved = pltpu.roll(ids, extended - offset, 1)[:, :own]
    used = info_ref[1 + tap]
    if forward_masks:
        used = used[:, reach : reach + own]
    else:
        used = pltpu.roll(used, extended - offset, 1)[:, :own]
    columns = mask_columns((moved == ids[:, reach : reach + own]) & (used == 1))
    at = pl.ds(pl.multiple_of(offset, STEP), own)
    for r in range(rows):
        lhs[r * own : (r + 1) * own, :] = ext[r, at, :] * spread(
            columns[:, first + r : first + r + 1], features
        )


def weight_kernel(blocks, first, info_ref, gh_ref, x_hbm, left_hbm, right_hbm, *rest):
    if blocks == (1, 1):
        gw_ref, ext, lhs_even, lhs_odd, fill_sems = rest
    else:
        keep_ref, send_ref, ext, lhs_even, lhs_odd, fill_sems, gw_ref, sems = rest
    step = pl.program_id(0)
    steps = pl.num_programs(0)
    rows, own, features = gh_ref.shape

    @pl.when(step == 0)
    def _():
        copies = fill_copies(ext, left_hbm, x_hbm, right_hbm, fill_sems)
        for copy in copies:
            copy.start()
        for copy in copies:
            copy.wait()
        build_masked(lhs_even, ext, info_ref, first, True)

    n_wide, n_narrow = blocks
    height, width = features // n_narrow, features // n_wide
    rows_at = pl.ds(pl.multiple_of(step * height, height), height)

    def run(lhs, lhs_next):
        build_masked(lhs_next, ext, info_ref, first + jnp.minimum(step + 1, steps - 1), True)
        product = dot(lhs[...], gh_ref[...].reshape(rows * own, features), 0, 0).astype(BF)
        for n in range(n_narrow):
            for w in range(n_wide):
                place_block(
                    gw_ref,
                    product[n * height : (n + 1) * height, w * width : (w + 1) * width],
                    w, n, rows_at, blocks,
                )

    by_parity(step, run, lhs_even, lhs_odd)

    if blocks != (1, 1):

        def shipping(at):
            rows_of = pl.ds(pl.multiple_of(at * height, height), height)
            return [
                pltpu.make_async_copy(
                    gw_ref.at[i, :, rows_of, :], ref.at[:, rows_of, :], sems.at[i]
                )
                for i, ref in enumerate((keep_ref, send_ref))
            ]

        @pl.when(step > 0)
        def _():
            for copy in shipping(step - 1):
                copy.wait()

        for copy in shipping(step):
            copy.start()

        @pl.when(step == steps - 1)
        def _():
            for copy in shipping(step):
                copy.wait()


def weight_gradient(blocks, info, gh, x, left, right, first, taps):
    rows, own, features = x.shape
    shapes, specs, scratch = gradient_outputs(blocks, taps * features, features)
    return pl.pallas_call(
        functools.partial(weight_kernel, blocks, first),
        grid=(taps,),
        in_specs=[whole(info.shape), whole(gh.shape)] + [pl.BlockSpec(memory_space=pl.ANY)] * 3,
        out_specs=specs,
        out_shape=shapes,
        scratch_shapes=[
            pltpu.VMEM((rows, info.shape[2], features), BF),
            pltpu.VMEM((rows * own, features), BF),
            pltpu.VMEM((rows * own, features), BF),
            pltpu.SemaphoreType.DMA((1 + 2 * rows,)),
        ]
        + scratch,
        compiler_params=params(28),
        cost_estimate=cost(2 * rows * own * features * features * taps, 12e6),
        name="weight_gradient",
    )(info, gh, x, left, right)


def input_kernel(
    first, info_ref, w_ref, gh_hbm, left_hbm, right_hbm, gmixed_hbm,
    gx_hbm, ext, lhs_even, lhs_odd, acc, gmixed, fill_sems, in_sem, out_sems,
):
    tap = pl.program_id(0)
    taps = pl.num_programs(0)
    rows, own, features = gmixed.shape
    batch = pl.ds(first, rows)
    base = pltpu.make_async_copy(gmixed_hbm.at[batch], gmixed, in_sem)

    @pl.when(tap == 0)
    def _():
        copies = fill_copies(
            ext, left_hbm.at[batch], gh_hbm.at[batch], right_hbm.at[batch], fill_sems
        )
        for copy in copies:
            copy.start()
        base.start()
        acc[...] = jnp.zeros_like(acc)
        for copy in copies:
            copy.wait()
        build_masked(lhs_even, ext, info_ref, 0, False, first)

    def run(lhs, lhs_next):
        build_masked(lhs_next, ext, info_ref, jnp.minimum(tap + 1, taps - 1), False, first)
        acc[...] += dot(lhs[...], w_ref[0], 1, 1)

    by_parity(tap, run, lhs_even, lhs_odd)

    @pl.when(tap == taps - 1)
    def _():
        base.wait()
        copies = []
        for r in range(rows):
            g_in = acc[r * own : (r + 1) * own, :].astype(BF).astype(F32)
            gmixed[r] = gmixed[r] + g_in
            copies.append(pltpu.make_async_copy(gmixed.at[r], gx_hbm.at[first + r], out_sems.at[r]))
            copies[-1].start()
        for copy in copies:
            copy.wait()


def input_gradient(info, conv_w, gh, left, right, gmixed, first, rows):
    _, own, features = gh.shape
    reach = left.shape[1]
    taps = conv_w.shape[0]
    return pl.pallas_call(
        functools.partial(input_kernel, first),
        grid=(taps,),
        in_specs=[
            whole(info.shape),
            pl.BlockSpec((1, features, features), lambda i: (i, 0, 0)),
        ]
        + [pl.BlockSpec(memory_space=pl.ANY)] * 4,
        out_specs=pl.BlockSpec(memory_space=pl.ANY),
        out_shape=shape(gmixed.shape, F32),
        input_output_aliases={5: 0},
        scratch_shapes=[
            pltpu.VMEM((rows, own + 2 * reach, features), BF),
            pltpu.VMEM((rows * own, features), BF),
            pltpu.VMEM((rows * own, features), BF),
            pltpu.VMEM((rows * own, features), F32),
            pltpu.VMEM((rows, own, features), F32),
            pltpu.SemaphoreType.DMA((1 + 2 * rows,)),
            pltpu.SemaphoreType.DMA,
            pltpu.SemaphoreType.DMA((rows,)),
        ],
        compiler_params=params(20),
        cost_estimate=cost(2 * rows * own * features * features * taps, 12e6),
        name="input_gradient",
    )(info, conv_w, gh, left, right, gmixed)


class Additions(NamedTuple):
    fn: Any
    operands: tuple
    in_specs: list
    out_specs: list
    out_shape: list
    steps: int


def additions_kernel(fn, count, *refs):
    fn(refs[:count], refs[count:])


def alone(work):
    moved = 3 * sum(v.size for v in work.operands)
    return pl.pallas_call(
        functools.partial(additions_kernel, work.fn, len(work.operands)),
        grid=(work.steps,),
        in_specs=work.in_specs,
        out_specs=work.out_specs,
        out_shape=work.out_shape,
        compiler_params=params(8),
        cost_estimate=cost(moved / 2, moved),
        name="additions",
    )(*work.operands)


def flip(value, axis, bit):
    size = lax.axis_size(axis)
    return lax.ppermute(value, axis, [(i, i ^ bit) for i in range(size)])


def add(a, b):
    return a.astype(F32) + b.astype(F32)


def stepwise(block, axis):
    return pl.BlockSpec(block, lambda i: tuple(i if d == axis else 0 for d in range(len(block))))


def after_core(keep, got, top, extra=0):
    end = keep.shape[1] - extra
    operands = [v.reshape((2, 2, 4) + v.shape[1:]) for v in (keep, got)]

    def fn(ins, outs):
        a_keep, a_send, b_keep, b_send = outs
        keep, got = ins
        for y in range(2):
            for x in range(2):
                total = add(keep[y, x, 0, :end], got[y, x, 0, :end]).astype(BF)
                (a_send if x else a_keep)[y, 0, :top, :] = total[:top]
                (b_send if y else b_keep)[x, 0, :, :] = total[top:]
        if extra:
            total = add(keep[0, 0, 0, end:], keep[0, 1, 0, end:]) + add(
                got[0, 0, 0, end:], got[0, 1, 0, end:]
            )
            for i, part in enumerate(in_pair(total)):
                for ref in (a_keep, a_send):
                    ref[i, 0, top:, :] = part

    dims = [(2, 4, top + extra, 128)] * 2 + [(2, 4, end - top, 128)] * 2
    return Additions(
        fn,
        tuple(operands),
        [stepwise((2, 2, 1) + v.shape[3:], 2) for v in operands],
        [stepwise((2, 1) + d[2:], 1) for d in dims],
        [shape(d, BF) for d in dims],
        4,
    )


def after_first(top, a_keep, a_got, b_keep, b_got):
    extra = a_keep.shape[2] - top

    def fn(ins, outs):
        a_keep, a_got, b_keep, b_got = ins
        a_next, a_send, b_next, b_send = outs
        for keep, got, stay, send in (
            (a_keep, a_got, a_next, a_send),
            (b_keep, b_got, b_next, b_send),
        ):
            n = stay.shape[1] if stay is b_next else top
            stay[0, :n] = add(keep[0, 0, :n], got[0, 0, :n]).astype(BF)
            send[0, :n] = add(keep[1, 0, :n], got[1, 0, :n]).astype(BF)
        if extra:
            total = add(a_keep[0, 0, top:], a_keep[1, 0, top:]) + add(
                a_got[0, 0, top:], a_got[1, 0, top:]
            )
            for i, part in enumerate(in_pair(total)):
                for ref in (a_next, a_send):
                    ref[0, top + i * extra : top + (i + 1) * extra] = part

    dims = [(4, top + 2 * extra, 128)] * 2 + [(4, b_keep.shape[2], 128)] * 2
    operands = (a_keep, a_got, b_keep, b_got)
    return Additions(
        fn,
        operands,
        [stepwise((2, 1) + v.shape[2:], 1) for v in operands],
        [stepwise((1,) + d[1:], 0) for d in dims],
        [shape(d, BF) for d in dims],
        4,
    )


def after_second_kernel(top, a_keep, a_got, b_keep, b_got, *outs):
    extra = (a_keep.shape[1] - top) // 2
    end = top + b_keep.shape[1]
    for i, ref in enumerate(outs):
        ref[:top] = add(a_keep[i, :top], a_got[i, :top]).astype(BF)
        ref[top:end] = add(b_keep[i], b_got[i]).astype(BF)
    if extra:
        for z in range(4):
            high, low = slice(top, top + extra), slice(top + extra, top + 2 * extra)
            total = add(a_keep[z, high], a_keep[z, low]) + add(a_got[z, high], a_got[z, low])
            for i, part in enumerate(in_pair(total)):
                at = end + (4 * i + z) * extra
                for ref in outs:
                    ref[at : at + extra] = part


def after_second(top, a_keep, a_got, b_keep, b_got):
    rows = top + b_keep.shape[1] + 4 * (a_keep.shape[1] - top)
    z = small(
        functools.partial(after_second_kernel, top),
        (a_keep, a_got, b_keep, b_got), [(rows, 128)] * 4,
    )
    return (z[0], *(flip(z[i], "narrow", 2 * i) for i in (1, 2, 3)))


def last_ff_kernel(z0, z1, z2, z3, w_out_ref, w_in_ref, sums_ref):
    out_rows, (height, width) = w_out_ref.shape[0], w_in_ref.shape
    total = add(z0[...], z1[...]) + add(z2[...], z3[...])
    w_out_ref[...] = total[:out_rows]
    for j in range(width // 128):
        at = out_rows + j * height
        w_in_ref[:, 128 * j : 128 * (j + 1)] = total[at : at + height]
    end = out_rows + height * width // 128
    rows = sums_ref.shape[0]
    sums_ref[...] = total[end : end + rows] + total[end + rows :]


def last_conv_kernel(z0, z1, z2, z3, out):
    out[...] = add(z0[...], z1[...]) + add(z2[...], z3[...])


def small(kernel, operands, dims, dtype=BF):
    moved = sum(v.size * v.dtype.itemsize for v in operands) * 2
    return pl.pallas_call(
        kernel,
        out_shape=[shape(d, dtype) for d in dims],
        compiler_params=params(12),
        cost_estimate=cost(moved / 2, moved),
        name="additions",
    )(*operands)


def after(value, *others):
    return lax.optimization_barrier((value, others))[0]


def body(
    inputs, conv_w, conv_b, ln1_gain, ln1_bias, w_in, b_in, w_out, ln2_gain, ln2_bias,
    segments, tap_mask, cotangent,
):
    rows, own, features = inputs.shape
    taps = conv_w.shape[0]
    reach = STEP * (taps // 2)
    hidden_units = w_in.shape[1]
    n_wide, n_narrow = lax.axis_size("wide"), lax.axis_size("narrow")
    by_hand = (n_wide, n_narrow) == (4, 8)
    blocks = (4, 8) if by_hand else (1, 1)

    to_right = [(i, i + 1) for i in range(n_wide - 1)]
    to_left = [(i + 1, i) for i in range(n_wide - 1)]

    def halos(value, dim):
        last = value.shape[dim]
        left = lax.ppermute(lax.slice_in_dim(value, last - reach, last, axis=dim), "wide", to_right)
        right = lax.ppermute(lax.slice_in_dim(value, 0, reach, axis=dim), "wide", to_left)
        return left, right

    in_place = functools.partial(pltpu.with_memory_space_constraint, memory_space=pltpu.HBM)
    to_send_left, to_send_right, info = pack(
        in_place(inputs), in_place(segments), in_place(jnp.transpose(tap_mask, (1, 0, 2))), reach
    )
    x_left = lax.ppermute(to_send_right, "wide", to_right)
    x_right = lax.ppermute(to_send_left, "wide", to_left)
    vec = jnp.stack([conv_b, ln1_gain, ln1_bias, ln2_gain, ln2_bias]).astype(F32)
    vec = jnp.pad(vec, ((0, 3), (0, 0)))

    acc = conv_inner(info, in_place(inputs), in_place(conv_w))
    hidden, info = conv_outer(info, acc, x_left, x_right, conv_w, vec)
    out, gmixed, gh, *grads = middle(
        blocks, hidden, inputs, cotangent, w_in, w_out, vec, b_in.astype(F32)[None]
    )
    if not by_hand:
        gh_left, gh_right = halos(gh, 1)
        gconv = weight_gradient(blocks, info, gh, inputs, x_left, x_right, 0, taps)
        gx = input_gradient(info, conv_w, gh, gh_left, gh_right, gmixed, 0, rows)

        def reduce(value, dims, wide_dim, narrow_dim):
            value = lax.psum_scatter(
                value.reshape(dims), "narrow", scatter_dimension=narrow_dim, tiled=True
            )
            return lax.psum_scatter(value, "wide", scatter_dimension=wide_dim, tiled=True).astype(
                F32
            )

        grad_w_out = reduce(grads[0], (hidden_units, features), 1, 0)
        grad_w_in = reduce(grads[1], (features, hidden_units), 1, 0)
        grad_conv = reduce(gconv[0], (taps, features, features), 2, 1)
        sums = lax.psum(grads[2], ("wide", "narrow"))
    else:
        together = lax.optimization_barrier
        cuts = (0, rows // 4, rows - rows // 4, rows)

        def inputs_part(i, gx):
            first, end = cuts[i], cuts[i + 1]
            return input_gradient(info, conv_w, gh, gh_left, gh_right, gx, first, end - first)

        height = features // n_narrow
        f_top = (grads[0].shape[1] - 16) * 3 // 4 // 16 * 16
        c_top = taps * height // 2 // 16 * 16
        f_got = flip(grads[1], "wide", 1)
        gh_left, gh_right = halos(gh, 1)
        f = alone(after_core(grads[0], f_got, f_top, 16))
        f_got = flip(f[1], "narrow", 1), flip(f[3], "wide", 2)
        c = weight_gradient(blocks, info, after(gh, *f), inputs, x_left, x_right, 0, taps)

        c, f, f_got, gh_left, gh_right = together((c, f, f_got, gh_left, gh_right))
        c_got = flip(c[1], "wide", 1)
        f = alone(after_first(f_top, f[0], f_got[0], f[2], f_got[1]))
        f_got = flip(f[1], "wide", 2), flip(f[3], "narrow", 1)
        gx = inputs_part(0, after(gmixed, *f))

        gx, c, c_got, f, f_got = together((gx, c[0], c_got, f, f_got))
        c = alone(after_core(c, c_got, c_top))
        c_got = flip(c[1], "narrow", 1), flip(c[3], "wide", 2)
        f = after_second(f_top, *after((f[0], f_got[0], f[2], f_got[1]), *c))
        gx = inputs_part(1, after(gx, *c, f[0]))

        gx, c, c_got, f = together((gx, c, c_got, f))
        c = alone(after_first(c_top, c[0], c_got[0], c[2], c_got[1]))
        c_got = flip(c[1], "wide", 2), flip(c[3], "narrow", 1)
        gx = inputs_part(2, after(gx, *c))

        gx, c, c_got, f = together((gx, c, c_got, f))
        c = after_second(c_top, c[0], c_got[0], c[2], c_got[1])
        f = after(f, c[0])
        grad_w_out, grad_w_in, sums = small(
            last_ff_kernel, f,
            [(hidden_units // n_narrow, 128), (height, hidden_units // n_wide), (64, 128)],
            F32,
        )
        grad_conv = small(last_conv_kernel, c, [(taps * height, 128)], F32)[0]
        grad_conv = grad_conv.reshape(taps, height, features // n_wide)
    sums = sums.reshape(-1)
    starts = [0, features, 2 * features, 3 * features]
    starts += [starts[-1] + hidden_units, starts[-1] + hidden_units + features]
    sizes = [features, features, features, hidden_units, features, features]
    vectors = [sums[a : a + n] for a, n in zip(starts, sizes, strict=True)]
    return (
        out, gx, grad_conv, vectors[0], vectors[1], vectors[2], grad_w_in, vectors[3],
        grad_w_out, vectors[4], vectors[5],
    )


def solution(mesh):
    split = P("narrow", "wide", None)
    placed = (split,) + (P(),) * 9 + (P("narrow", "wide"), P("narrow", None, "wide"), split)
    return jax.shard_map(
        body,
        mesh=mesh,
        in_specs=placed,
        out_specs=(
            split, split, P(None, "narrow", "wide"), P(), P(), P(), P("narrow", "wide"), P(),
            P("narrow", "wide"), P(), P(),
        ),
        check_vma=False,
    )
```

time: 176 us -> 157 us (0.89)
  waiting for transfers between devices: 29.7 us -> 13.8 us
  Pallas kernels: 98.2 us -> 109 us
  starting transfers between devices: 38.1 us -> 31.2 us
  local copies, waits for them, and re-layouts: 8.37 us -> 1.5 us
    ppermute x18 -> x16, waiting for transfers between devices: 29.7 us -> 13.8 us  [flip(): return lax.ppermute(value, axis, [(i, i ^ bit) for i in range(size)])]
    pallas_call x4 -> x9, Pallas kernels: 37.7 us -> 47.3 us  [the longest x3 24.5 us: input_gradient(): pl.pallas_call(functools.partial(input_kernel, first), grid=(taps,), in_s...]
    ppermute x3 -> x1, starting transfers between devices: 10.7 us -> 2.12 us  [halos(): lax.ppermute(lax.slice_in_dim(value, last - reach, last, axis=dim), 'wide...]
    ppermute x0 -> x2, starting transfers between devices: none -> 3.72 us  [the longest x1 2.42 us: body(): x_left = lax.ppermute(to_send_right, 'wide', to_right)]
    unnamed x28 -> x20, local copies, waits for them, and re-layouts: 3.72 us -> 0.05 us
    slice x2 -> x1, local copies, waits for them, and re-layouts: 3.4 us -> 0.2 us  [halos(): lax.slice_in_dim(value, 0, reach, axis=dim)]
    ppermute x3 -> x1, starting transfers between devices: 4 us -> 1.29 us  [halos(): lax.ppermute(lax.slice_in_dim(value, 0, reach, axis=dim), 'wide', to_left)]
    pallas_call x1, Pallas kernels: 9.56 us -> 11.9 us  [conv_inner(): pl.pallas_call(conv_inner_kernel, grid=(taps,), in_specs=[whole(info.shap...]
  transfers between devices with their start and end apart: 24 -> 20, of which waited for: 10 -> 5; matrix products, arithmetic and copies ran while one was open for 1% -> 1% of each run, Pallas kernels for 27% -> 36%
where the time goes in v3:
time: 157 us
  Pallas kernels  109 us (69%)
  starting transfers between devices  31.2 us (20%)
  waiting for transfers between devices  13.8 us (9%)
    pallas_call x1, Pallas kernels, middle(): pl.pallas_call(functools.partial(middle_kernel, blocks), grid=(rows // bl...  42.4 us
    pallas_call x3, Pallas kernels, input_gradient(): pl.pallas_call(functools.partial(input_kernel, first), grid=(taps,), in_s...  24.5 us
    ppermute x16, starting transfers between devices, flip(): return lax.ppermute(value, axis, [(i, i ^ bit) for i in range(size)])  24.1 us
    pallas_call x1, Pallas kernels, weight_gradient(): pl.pallas_call(functools.partial(weight_kernel, blocks, first), grid=(tap...  16.9 us
    ppermute x16, waiting for transfers between devices, flip(): return lax.ppermute(value, axis, [(i, i ^ bit) for i in range(size)])  13.8 us
    pallas_call x1, Pallas kernels, conv_inner(): pl.pallas_call(conv_inner_kernel, grid=(taps,), in_specs=[whole(info.shap...  11.9 us
    pallas_call x1, Pallas kernels, conv_outer(): pl.pallas_call(conv_outer_kernel, grid=(taps - 1,), in_specs=[whole(info....  5.48 us
    pallas_call x4, Pallas kernels, alone(): pl.pallas_call(functools.partial(additions_kernel, work.fn, len(work.oper...  3.19 us
  transfers between devices with their start and end apart: 20, of which 5 were waited for; matrix products, arithmetic and copies ran while one was open for 1% of the time, Pallas kernels for 36%

profile of v3, /device:TPU:0, one launch (start us, length us, event | category | flops | bytes accessed | tf_op | source)
XLA Modules:
  0.0 156.6 jit_solution(17892713472369344847)
XLA Ops:
  0.7 2.8 %pack.1 = (bf16[1056,512]{1,0:T(8,128)(2,1)S(1)}, bf16[1056,512]{1,0:T(8,128)(2,1)}, s32[10,8,256]{2,1,0:T(8,128)S(1)}) custom-call(bf16[8,256,512]{2,1,0:T(8,128)(2,1)} %x_hbm.3, s32[8,256]{1,0:T(8,128)} %ids_hbm.1, s32[9,8,256]{2,1,0:T(8,128)} %bitcast.27), custom_call_target="tpu_custom_call" | custom-call | flops 20000 | bytes 80000 | tf_op jit(solution)/shard_map/pack/pallas_call | solution.py:113
  3.5 2.4 %collective-permute-start = (bf16[1056,512]{1,0:T(8,128)(2,1)}, bf16[1056,512]{1,0:T(8,128)(2,1)S(1)}, u32[]{:S(2)}, u32[]{:S(2)}) collective-permute-start(bf16[1056,512]{1,0:T(8,128)(2,1)} %get-tuple-element.96), channel_id=1, source_target_pairs={{0,8},{8,16},{16,24},{1,9},{9,17},{17,25},{2,10},{10,18},{18,26},{... | collective-permute-start | bytes 3244040 | tf_op jit(solution)/shard_map/ppermute | solution.py:886
  5.9 1.3 collective-permute-start.1
  7.4 11.9 %conv_inner.1.acc_hbm = f32[8,256,512]{2,1,0:T(8,128)S(1)} custom-call(s32[10,8,256]{2,1,0:T(8,128)S(1)} %get-tuple-element.95.info_ref.own_info_ref, bf16[8,256,512]{2,1,0:T(8,128)(2,1)} %x_hbm.3, bf16[9,512,512]{2,1,0:T(8,128)(2,1)} %w_ref.9), custom_call_target="tpu_custom_call" | custom-call | flops 139156944 | bytes 220000 | tf_op jit(solution)/shard_map/conv_inner/pallas_call | solution.py:184
  19.4 5.5 %conv_outer.1 = (bf16[8,256,512]{2,1,0:T(8,128)(2,1)S(1)}, s32[10,8,512]{2,1,0:T(8,128)S(1)}) custom-call(s32[10,8,256]{2,1,0:T(8,128)S(1)} %get-tuple-element.95.info_ref.own_info_ref, bf16[1056,512]{1,0:T(8,128)(2,1)S(1)} %collective-permute-done.left_ref.left_hbm, bf16[1056,512]{1,0:T(8,128)(2,1)S(1)} %collective-permute-done.1.right_ref.right_hbm, ...), custom_call_target="tpu_custom_call" | custom-call | flops 54116588 | bytes 220000 | tf_op jit(solution)/shard_map/conv_outer/pallas_call | solution.py:269
  24.9 42.4 %middle.1 = (bf16[8,256,512]{2,1,0:T(8,128)(2,1)}, f32[8,256,512]{2,1,0:T(8,128)}, bf16[8,256,512]{2,1,0:T(8,128)(2,1)S(1)}, bf16[16,528,128]{2,1,0:T(8,128)(2,1)}, bf16[16,528,128]{2,1,0:T(8,128)(2,1)}) custom-call(bf16[8,256,512]{2,1,0:T(8,128)(2,1)S(1)} %get-tuple-element.98.hidden_ref, bf16[8,256,512]{2,1,0:T(8,128)(2,1)S(1)} %copy-done, ...), custom_call_target="tpu_custom_call" | custom-call | flops 515396064 | bytes 680000 | tf_op jit(solution)/shard_map/middle/pallas_call | solution.py:484
  67.3 5.6 %collective-permute-start.2 = (bf16[16,528,128]{2,1,0:T(8,128)(2,1)}, bf16[16,528,128]{2,1,0:T(8,128)(2,1)S(1)}, u32[]{:S(2)}, u32[]{:S(2)}) collective-permute-start(bf16[16,528,128]{2,1,0:T(8,128)(2,1)} %get-tuple-element.103), channel_id=1, source_target_pairs={{0,8},{8,0},{16,24},{24,16},{1,9},{9,1},{17,25},{25,17},{2,10},{10... | collective-permute-start | bytes 6488072 | tf_op jit(solution)/shard_map/ppermute | solution.py:730
  73.1 2.1 %collective-permute-start.5 = (bf16[8,128,512]{2,1,0:T(8,128)(2,1)S(1)}, bf16[8,128,512]{2,1,0:T(8,128)(2,1)S(1)}, u32[]{:S(2)}, u32[]{:S(2)}) collective-permute-start(bf16[8,128,512]{2,1,0:T(8,128)(2,1)S(1)} %get-tuple-element.180), channel_id=1, source_target_pairs={{0,8},{8,16},{16,24},{1,9},{9,17},{17,25},{2,10},{10,18},{18,26},{... | collective-permute-start | bytes 3145736 | tf_op jit(solution)/shard_map/ppermute | solution.py:878
  75.3 1.3 collective-permute-start.6
  77.0 1.0 additions.8
  78.0 1.6 collective-permute-start.3
  79.6 2.0 %collective-permute-start.4 = (bf16[2,4,128,128]{3,2,1,0:T(8,128)(2,1)S(1)}, bf16[2,4,128,128]{3,2,1,0:T(8,128)(2,1)S(1)}, u32[]{:S(2)}, u32[]{:S(2)}) collective-permute-start(bf16[2,4,128,128]{3,2,1,0:T(8,128)(2,1)S(1)} %get-tuple-element.107), channel_id=1, source_target_pairs={{0,16},{8,24},{16,0},{24,8},{1,17},{9,25},{17,1},{25,9},{2,18},{10... | collective-permute-start | bytes 786440 | tf_op jit(solution)/shard_map/ppermute | solution.py:730
  81.6 16.9 %weight_gradient.1 = (bf16[16,576,128]{2,1,0:T(8,128)(2,1)S(1)}, bf16[16,576,128]{2,1,0:T(8,128)(2,1)S(1)}) custom-call(s32[10,8,512]{2,1,0:T(8,128)S(1)} %get-tuple-element.100.info_ref, bf16[8,256,512]{2,1,0:T(8,128)(2,1)S(1)} %get-tuple-element.108.gh_ref.gh_hbm, bf16[8,256,512]{2,1,0:T(8,128)(2,1)S(1)} %copy-done, ...), custom_call_target="tpu_custom_call" | custom-call | flops 193273536 | bytes 240000 | tf_op jit(solution)/shard_map/weight_gradient/pallas_call | solution.py:609
  98.5 0.7 collective-permute-done.3.refs_1_
  99.8 1.5 collective-permute-start.9
  101.4 7.0 %input_gradient.3.gmixed_hbm = f32[8,256,512]{2,1,0:T(8,128)} custom-call(s32[10,8,512]{2,1,0:T(8,128)S(1)} %get-tuple-element.100.info_ref, bf16[9,512,512]{2,1,0:T(8,128)(2,1)S(1)} %bitcast.20, bf16[8,256,512]{2,1,0:T(8,128)(2,1)S(1)} %get-tuple-element.108.gh_ref.gh_hbm, ...), custom_call_target="tpu_custom_call", output_to_operand_aliasing={{}: (5, {})} | custom-call | flops 48318384 | bytes 240000 | tf_op jit(solution)/shard_map/input_gradient/pallas_call | solution.py:674
  108.4 3.6 %collective-permute-done.8.a_got = bf16[4,416,128]{2,1,0:T(8,128)(2,1)S(1)} collective-permute-done((bf16[4,416,128]{2,1,0:T(8,128)(2,1)S(1)}, bf16[4,416,128]{2,1,0:T(8,128)(2,1)S(1)}, u32[]{:S(2)}, u32[]{:S(2)}) %collective-permute-start.8) | collective-permute-done | bytes 426016 | tf_op jit(solution)/shard_map/ppermute | solution.py:730
  112.0 1.1 additions.10
  113.1 1.6 collective-permute-start.10
  115.1 1.6 %collective-permute-start.12 = (bf16[640,128]{1,0:T(8,128)(2,1)S(1)}, bf16[640,128]{1,0:T(8,128)(2,1)S(1)}, u32[]{:S(2)}, u32[]{:S(2)}) collective-permute-start(bf16[640,128]{1,0:T(8,128)(2,1)S(1)} %get-tuple-element.142), channel_id=1, source_target_pairs={{0,2},{1,3},{2,0},{3,1},{4,6},{5,7},{6,4},{7,5},{8,10},{9,11},{10,... | collective-permute-start | bytes 491528 | tf_op jit(solution)/shard_map/ppermute | solution.py:730
  116.7 2.6 %collective-permute-start.13 = (bf16[640,128]{1,0:T(8,128)(2,1)S(1)}, bf16[640,128]{1,0:T(8,128)(2,1)S(1)}, u32[]{:S(2)}, u32[]{:S(2)}) collective-permute-start(bf16[640,128]{1,0:T(8,128)(2,1)S(1)} %get-tuple-element.143), channel_id=1, source_target_pairs={{0,4},{1,5},{2,6},{3,7},{4,0},{5,1},{6,2},{7,3},{8,12},{9,13},{10,... | collective-permute-start | bytes 491528 | tf_op jit(solution)/shard_map/ppermute | solution.py:730
  119.5 10.6 %input_gradient.4.gmixed_hbm = f32[8,256,512]{2,1,0:T(8,128)} custom-call(s32[10,8,512]{2,1,0:T(8,128)S(1)} %get-tuple-element.100.info_ref, bf16[9,512,512]{2,1,0:T(8,128)(2,1)S(1)} %bitcast.20, bf16[8,256,512]{2,1,0:T(8,128)(2,1)S(1)} %get-tuple-element.108.gh_ref.gh_hbm, ...), custom_call_target="tpu_custom_call", output_to_operand_aliasing={{}: (5, {})} | custom-call | flops 96636768 | bytes 240000 | tf_op jit(solution)/shard_map/input_gradient/pallas_call | solution.py:674
  130.1 1.4 collective-permute-done.13.z2
  132.1 1.6 %collective-permute-start.15 = (bf16[4,288,128]{2,1,0:T(8,128)(2,1)S(1)}, bf16[4,288,128]{2,1,0:T(8,128)(2,1)S(1)}, u32[]{:S(2)}, u32[]{:S(2)}) collective-permute-start(bf16[4,288,128]{2,1,0:T(8,128)(2,1)S(1)} %get-tuple-element.151), channel_id=1, source_target_pairs={{0,16},{8,24},{16,0},{24,8},{1,17},{9,25},{17,1},{25,9},{2,18},{10... | collective-permute-start | bytes 884744 | tf_op jit(solution)/shard_map/ppermute | solution.py:730
  134.3 7.0 %input_gradient.5 = f32[8,256,512]{2,1,0:T(8,128)} custom-call(s32[10,8,512]{2,1,0:T(8,128)S(1)} %get-tuple-element.100.info_ref, bf16[9,512,512]{2,1,0:T(8,128)(2,1)S(1)} %bitcast.20, bf16[8,256,512]{2,1,0:T(8,128)(2,1)S(1)} %get-tuple-element.108.gh_ref.gh_hbm, ...), custom_call_target="tpu_custom_call", output_to_operand_aliasing={{}: (5, {})} | custom-call | flops 48318384 | bytes 240000 | tf_op jit(solution)/shard_map/input_gradient/pallas_call | solution.py:674
  141.4 2.4 %collective-permute-start.17 = (bf16[576,128]{1,0:T(8,128)(2,1)S(1)}, bf16[576,128]{1,0:T(8,128)(2,1)S(1)}, u32[]{:S(2)}, u32[]{:S(2)}) collective-permute-start(bf16[576,128]{1,0:T(8,128)(2,1)S(1)} %get-tuple-element.165), channel_id=1, source_target_pairs={{0,2},{1,3},{2,0},{3,1},{4,6},{5,7},{6,4},{7,5},{8,10},{9,11},{10,... | collective-permute-start | bytes 442376 | tf_op jit(solution)/shard_map/ppermute | solution.py:730
  143.8 1.1 collective-permute-start.18
  144.9 1.4 collective-permute-start.19
  146.3 0.7 additions.15
  147.0 0.6 slice_bitcast_fusion
  148.2 7.6 %collective-permute-done.18.z2 = bf16[576,128]{1,0:T(8,128)(2,1)S(1)} collective-permute-done((bf16[576,128]{1,0:T(8,128)(2,1)S(1)}, bf16[576,128]{1,0:T(8,128)(2,1)S(1)}, u32[]{:S(2)}, u32[]{:S(2)}) %collective-permute-start.18) | collective-permute-done | bytes 147488 | tf_op jit(solution)/shard_map/ppermute | solution.py:730
  155.8 0.8 additions.14
  (56 shorter events, 3.9 us)
Async XLA Ops:
  0.6 6.6 %copy-start.3 = (bf16[512]{0:T(512)(128)(2,1)S(1)}, bf16[512]{0:T(512)(128)(2,1)}, u32[]{:S(2)}) copy-start(bf16[512]{0:T(512)(128)(2,1)} %param.15) | copy-start | bytes 3076
  0.7 6.6 %copy-start.4 = (bf16[512]{0:T(512)(128)(2,1)S(1)}, bf16[512]{0:T(512)(128)(2,1)}, u32[]{:S(2)}) copy-start(bf16[512]{0:T(512)(128)(2,1)} %param.16) | copy-start | bytes 3076
  0.7 6.6 %copy-start.5 = (bf16[512]{0:T(512)(128)(2,1)S(1)}, bf16[512]{0:T(512)(128)(2,1)}, u32[]{:S(2)}) copy-start(bf16[512]{0:T(512)(128)(2,1)} %param.17) | copy-start | bytes 3076
  0.7 6.6 %copy-start.6 = (bf16[512]{0:T(512)(128)(2,1)S(1)}, bf16[512]{0:T(512)(128)(2,1)}, u32[]{:S(2)}) copy-start(bf16[512]{0:T(512)(128)(2,1)} %param.21) | copy-start | bytes 3076
  0.7 6.6 %copy-start.7 = (bf16[512]{0:T(512)(128)(2,1)S(1)}, bf16[512]{0:T(512)(128)(2,1)}, u32[]{:S(2)}) copy-start(bf16[512]{0:T(512)(128)(2,1)} %param.22) | copy-start | bytes 3076
  0.7 6.6 %copy-start.2 = (bf16[2048]{0:T(1024)(128)(2,1)S(1)}, bf16[2048]{0:T(1024)(128)(2,1)}, u32[]{:S(2)}) copy-start(bf16[2048]{0:T(1024)(128)(2,1)} %param.19) | copy-start | bytes 12292
  3.5 15.9 %collective-permute-start = (bf16[1056,512]{1,0:T(8,128)(2,1)}, bf16[1056,512]{1,0:T(8,128)(2,1)S(1)}, u32[]{:S(2)}, u32[]{:S(2)}) collective-permute-start(bf16[1056,512]{1,0:T(8,128)(2,1)} %get-tuple-element.96), channel_id=1, source_target_pairs={{0,8},{8,16},{16,24},{1,9},{9,17},{17,25},{2,10},{10,18},{18,26},{... | collective-permute-start | bytes 3244040 | tf_op jit(solution)/shard_map/ppermute | solution.py:886
  5.9 13.5 %collective-permute-start.1 = (bf16[1056,512]{1,0:T(8,128)(2,1)S(1)}, bf16[1056,512]{1,0:T(8,128)(2,1)S(1)}, u32[]{:S(2)}, u32[]{:S(2)}) collective-permute-start(bf16[1056,512]{1,0:T(8,128)(2,1)S(1)} %get-tuple-element.97), channel_id=1, source_target_pairs={{8,0},{16,8},{24,16},{9,1},{17,9},{25,17},{10,2},{18,10},{26,18},{... | collective-permute-start | bytes 3244040 | tf_op jit(solution)/shard_map/ppermute | solution.py:887
  7.4 12.0 %slice-start = ((s8[4718592]{0:T(1024)(128)(4,1)}), s8[4194304]{0:T(1024)(128)(4,1)S(1)}, s32[]{:S(2)}) async-start(s8[4718592]{0:T(1024)(128)(4,1)} %bitcast.19), calls=%async_computation | async-start | bytes 8388608
  7.4 12.0 %slice-start.1 = ((s8[4718592]{0:T(1024)(128)(4,1)}), s8[524288]{0:T(1024)(128)(4,1)S(1)}, s32[]{:S(2)}) async-start(s8[4718592]{0:T(1024)(128)(4,1)} %bitcast.19), calls=%async_computation.1 | async-start | bytes 1048576
  19.4 5.5 %copy-start = (bf16[8,256,512]{2,1,0:T(8,128)(2,1)S(1)}, bf16[8,256,512]{2,1,0:T(8,128)(2,1)}, u32[]{:S(2)}) copy-start(bf16[8,256,512]{2,1,0:T(8,128)(2,1)} %x_hbm.3) | copy-start | bytes 6291460
  67.3 9.7 %copy-start.1 = (bf16[16,528,128]{2,1,0:T(8,128)(2,1)S(1)}, bf16[16,528,128]{2,1,0:T(8,128)(2,1)}, u32[]{:S(2)}) copy-start(bf16[16,528,128]{2,1,0:T(8,128)(2,1)} %get-tuple-element.102) | copy-start | bytes 6488068
  67.3 9.7 %collective-permute-start.2 = (bf16[16,528,128]{2,1,0:T(8,128)(2,1)}, bf16[16,528,128]{2,1,0:T(8,128)(2,1)S(1)}, u32[]{:S(2)}, u32[]{:S(2)}) collective-permute-start(bf16[16,528,128]{2,1,0:T(8,128)(2,1)} %get-tuple-element.103), channel_id=1, source_target_pairs={{0,8},{8,0},{16,24},{24,16},{1,9},{9,1},{17,25},{25,17},{2,10},{10... | collective-permute-start | bytes 6488072 | tf_op jit(solution)/shard_map/ppermute | solution.py:730
  73.1 25.3 %collective-permute-start.5 = (bf16[8,128,512]{2,1,0:T(8,128)(2,1)S(1)}, bf16[8,128,512]{2,1,0:T(8,128)(2,1)S(1)}, u32[]{:S(2)}, u32[]{:S(2)}) collective-permute-start(bf16[8,128,512]{2,1,0:T(8,128)(2,1)S(1)} %get-tuple-element.180), channel_id=1, source_target_pairs={{0,8},{8,16},{16,24},{1,9},{9,17},{17,25},{2,10},{10,18},{18,26},{... | collective-permute-start | bytes 3145736 | tf_op jit(solution)/shard_map/ppermute | solution.py:878
  75.3 23.2 %collective-permute-start.6 = (bf16[8,128,512]{2,1,0:T(8,128)(2,1)S(1)}, bf16[8,128,512]{2,1,0:T(8,128)(2,1)S(1)}, u32[]{:S(2)}, u32[]{:S(2)}) collective-permute-start(bf16[8,128,512]{2,1,0:T(8,128)(2,1)S(1)} %get-tuple-element.179), channel_id=1, source_target_pairs={{8,0},{16,8},{24,16},{9,1},{17,9},{25,17},{10,2},{18,10},{26,18},{... | collective-permute-start | bytes 3145736 | tf_op jit(solution)/shard_map/ppermute | solution.py:879
  78.0 21.1 %collective-permute-start.3 = (bf16[2,4,400,128]{3,2,1,0:T(8,128)(2,1)S(1)}, bf16[2,4,400,128]{3,2,1,0:T(8,128)(2,1)S(1)}, u32[]{:S(2)}, u32[]{:S(2)}) collective-permute-start(bf16[2,4,400,128]{3,2,1,0:T(8,128)(2,1)S(1)} %get-tuple-element.105), channel_id=1, source_target_pairs={{0,1},{1,0},{2,3},{3,2},{4,5},{5,4},{6,7},{7,6},{8,9},{9,8},{10,11... | collective-permute-start | bytes 2457608 | tf_op jit(solution)/shard_map/ppermute | solution.py:730
  79.6 18.9 %collective-permute-start.4 = (bf16[2,4,128,128]{3,2,1,0:T(8,128)(2,1)S(1)}, bf16[2,4,128,128]{3,2,1,0:T(8,128)(2,1)S(1)}, u32[]{:S(2)}, u32[]{:S(2)}) collective-permute-start(bf16[2,4,128,128]{3,2,1,0:T(8,128)(2,1)S(1)} %get-tuple-element.107), channel_id=1, source_target_pairs={{0,16},{8,24},{16,0},{24,8},{1,17},{9,25},{17,1},{25,9},{2,18},{10... | collective-permute-start | bytes 786440 | tf_op jit(solution)/shard_map/ppermute | solution.py:730
  99.2 12.8 %collective-permute-start.7 = (bf16[16,576,128]{2,1,0:T(8,128)(2,1)S(1)}, bf16[16,576,128]{2,1,0:T(8,128)(2,1)S(1)}, u32[]{:S(2)}, u32[]{:S(2)}) collective-permute-start(bf16[16,576,128]{2,1,0:T(8,128)(2,1)S(1)} %get-tuple-element.124), channel_id=1, source_target_pairs={{0,8},{8,0},{16,24},{24,16},{1,9},{9,1},{17,25},{25,17},{2,10},{10... | collective-permute-start | bytes 7077896 | tf_op jit(solution)/shard_map/ppermute | solution.py:730
  99.8 12.2 %collective-permute-start.8 = (bf16[4,416,128]{2,1,0:T(8,128)(2,1)S(1)}, bf16[4,416,128]{2,1,0:T(8,128)(2,1)S(1)}, u32[]{:S(2)}, u32[]{:S(2)}) collective-permute-start(bf16[4,416,128]{2,1,0:T(8,128)(2,1)S(1)} %get-tuple-element.119), channel_id=1, source_target_pairs={{0,16},{8,24},{16,0},{24,8},{1,17},{9,25},{17,1},{25,9},{2,18},{10... | collective-permute-start | bytes 1277960 | tf_op jit(solution)/shard_map/ppermute | solution.py:730
  99.8 8.5 %collective-permute-start.9 = (bf16[4,128,128]{2,1,0:T(8,128)(2,1)S(1)}, bf16[4,128,128]{2,1,0:T(8,128)(2,1)S(1)}, u32[]{:S(2)}, u32[]{:S(2)}) collective-permute-start(bf16[4,128,128]{2,1,0:T(8,128)(2,1)S(1)} %get-tuple-element.121), channel_id=1, source_target_pairs={{0,1},{1,0},{2,3},{3,2},{4,5},{5,4},{6,7},{7,6},{8,9},{9,8},{10,11... | collective-permute-start | bytes 393224 | tf_op jit(solution)/shard_map/ppermute | solution.py:730
  113.1 18.5 %collective-permute-start.10 = (bf16[2,4,288,128]{3,2,1,0:T(8,128)(2,1)S(1)}, bf16[2,4,288,128]{3,2,1,0:T(8,128)(2,1)S(1)}, u32[]{:S(2)}, u32[]{:S(2)}) collective-permute-start(bf16[2,4,288,128]{3,2,1,0:T(8,128)(2,1)S(1)} %get-tuple-element.129), channel_id=1, source_target_pairs={{0,1},{1,0},{2,3},{3,2},{4,5},{5,4},{6,7},{7,6},{8,9},{9,8},{10,11... | collective-permute-start | bytes 1769480 | tf_op jit(solution)/shard_map/ppermute | solution.py:730
  114.7 16.9 %collective-permute-start.11 = (bf16[2,4,288,128]{3,2,1,0:T(8,128)(2,1)S(1)}, bf16[2,4,288,128]{3,2,1,0:T(8,128)(2,1)S(1)}, u32[]{:S(2)}, u32[]{:S(2)}) collective-permute-start(bf16[2,4,288,128]{3,2,1,0:T(8,128)(2,1)S(1)} %get-tuple-element.131), channel_id=1, source_target_pairs={{0,16},{8,24},{16,0},{24,8},{1,17},{9,25},{17,1},{25,9},{2,18},{10... | collective-permute-start | bytes 1769480 | tf_op jit(solution)/shard_map/ppermute | solution.py:730
  115.1 15.0 %collective-permute-start.12 = (bf16[640,128]{1,0:T(8,128)(2,1)S(1)}, bf16[640,128]{1,0:T(8,128)(2,1)S(1)}, u32[]{:S(2)}, u32[]{:S(2)}) collective-permute-start(bf16[640,128]{1,0:T(8,128)(2,1)S(1)} %get-tuple-element.142), channel_id=1, source_target_pairs={{0,2},{1,3},{2,0},{3,1},{4,6},{5,7},{6,4},{7,5},{8,10},{9,11},{10,... | collective-permute-start | bytes 491528 | tf_op jit(solution)/shard_map/ppermute | solution.py:730
  116.7 14.8 %collective-permute-start.13 = (bf16[640,128]{1,0:T(8,128)(2,1)S(1)}, bf16[640,128]{1,0:T(8,128)(2,1)S(1)}, u32[]{:S(2)}, u32[]{:S(2)}) collective-permute-start(bf16[640,128]{1,0:T(8,128)(2,1)S(1)} %get-tuple-element.143), channel_id=1, source_target_pairs={{0,4},{1,5},{2,6},{3,7},{4,0},{5,1},{6,2},{7,3},{8,12},{9,13},{10,... | collective-permute-start | bytes 491528 | tf_op jit(solution)/shard_map/ppermute | solution.py:730
  119.3 12.2 %collective-permute-start.14 = (bf16[640,128]{1,0:T(8,128)(2,1)S(1)}, bf16[640,128]{1,0:T(8,128)(2,1)S(1)}, u32[]{:S(2)}, u32[]{:S(2)}) collective-permute-start(bf16[640,128]{1,0:T(8,128)(2,1)S(1)} %get-tuple-element.144), channel_id=1, source_target_pairs={{0,6},{1,7},{2,4},{3,5},{4,2},{5,3},{6,0},{7,1},{8,14},{9,15},{10,... | collective-permute-start | bytes 491528 | tf_op jit(solution)/shard_map/ppermute | solution.py:730
  132.1 9.1 %collective-permute-start.15 = (bf16[4,288,128]{2,1,0:T(8,128)(2,1)S(1)}, bf16[4,288,128]{2,1,0:T(8,128)(2,1)S(1)}, u32[]{:S(2)}, u32[]{:S(2)}) collective-permute-start(bf16[4,288,128]{2,1,0:T(8,128)(2,1)S(1)} %get-tuple-element.151), channel_id=1, source_target_pairs={{0,16},{8,24},{16,0},{24,8},{1,17},{9,25},{17,1},{25,9},{2,18},{10... | collective-permute-start | bytes 884744 | tf_op jit(solution)/shard_map/ppermute | solution.py:730
  133.8 7.5 %collective-permute-start.16 = (bf16[4,288,128]{2,1,0:T(8,128)(2,1)S(1)}, bf16[4,288,128]{2,1,0:T(8,128)(2,1)S(1)}, u32[]{:S(2)}, u32[]{:S(2)}) collective-permute-start(bf16[4,288,128]{2,1,0:T(8,128)(2,1)S(1)} %get-tuple-element.153), channel_id=1, source_target_pairs={{0,1},{1,0},{2,3},{3,2},{4,5},{5,4},{6,7},{7,6},{8,9},{9,8},{10,11... | collective-permute-start | bytes 884744 | tf_op jit(solution)/shard_map/ppermute | solution.py:730
  141.4 6.8 %collective-permute-start.17 = (bf16[576,128]{1,0:T(8,128)(2,1)S(1)}, bf16[576,128]{1,0:T(8,128)(2,1)S(1)}, u32[]{:S(2)}, u32[]{:S(2)}) collective-permute-start(bf16[576,128]{1,0:T(8,128)(2,1)S(1)} %get-tuple-element.165), channel_id=1, source_target_pairs={{0,2},{1,3},{2,0},{3,1},{4,6},{5,7},{6,4},{7,5},{8,10},{9,11},{10,... | collective-permute-start | bytes 442376 | tf_op jit(solution)/shard_map/ppermute | solution.py:730
  143.8 12.0 %collective-permute-start.18 = (bf16[576,128]{1,0:T(8,128)(2,1)S(1)}, bf16[576,128]{1,0:T(8,128)(2,1)S(1)}, u32[]{:S(2)}, u32[]{:S(2)}) collective-permute-start(bf16[576,128]{1,0:T(8,128)(2,1)S(1)} %get-tuple-element.166), channel_id=1, source_target_pairs={{0,4},{1,5},{2,6},{3,7},{4,0},{5,1},{6,2},{7,3},{8,12},{9,13},{10,... | collective-permute-start | bytes 442376 | tf_op jit(solution)/shard_map/ppermute | solution.py:730
  144.9 10.9 %collective-permute-start.19 = (bf16[576,128]{1,0:T(8,128)(2,1)S(1)}, bf16[576,128]{1,0:T(8,128)(2,1)S(1)}, u32[]{:S(2)}, u32[]{:S(2)}) collective-permute-start(bf16[576,128]{1,0:T(8,128)(2,1)S(1)} %get-tuple-element.167), channel_id=1, source_target_pairs={{0,6},{1,7},{2,4},{3,5},{4,2},{5,3},{6,0},{7,1},{8,14},{9,15},{10,... | collective-permute-start | bytes 442376 | tf_op jit(solution)/shard_map/ppermute | solution.py:730

commit v4 on v3

--- a/solution.py
+++ b/solution.py
@@ -63,15 +63,24 @@
     return values.reshape(-1, 8, values.shape[-1]).sum(0)
 
 
+def pair_sides():
+    odd = lax.axis_index("wide") % 2
+    return 1 - odd, odd
+
+
 PACK_ROWS = 32
 
 
 def pack_kernel(
-    x_hbm, ids_hbm, used_hbm, left_ref, right_ref, info_ref, ids, sems, info_sems
+    x_hbm, ids_hbm, used_hbm, near_ref, far_ref, info_ref, ids, sems, info_sems
 ):
     rows, own, features = x_hbm.shape
     count = info_ref.shape[0]
-    reach = (left_ref.shape[0] - PACK_ROWS) // rows
+    reach = (near_ref.shape[0] - PACK_ROWS) // rows
+    near, far = pair_sides()
+    ends = tuple(
+        (ref, pl.multiple_of(side * (own - reach), reach)) for ref, side in ((near_ref, near), (far_ref, far))
+    )
     loads = [
         pltpu.make_async_copy(ids_hbm, ids, info_sems.at[0]),
         pltpu.make_async_copy(used_hbm, info_ref.at[pl.ds(1, count - 1)], info_sems.at[1]),
@@ -79,7 +88,7 @@
     for load in loads:
         load.start()
     copies = []
-    for side, (out, start) in enumerate(((left_ref, 0), (right_ref, own - reach))):
+    for side, (out, start) in enumerate(ends):
         for r in range(rows):
             copies.append(
                 pltpu.make_async_copy(
@@ -92,11 +101,11 @@
     for load in loads:
         load.wait()
     info_ref[0] = ids[...] + 1
-    for side, (out, start) in enumerate(((left_ref, 0), (right_ref, own - reach))):
+    for side, (out, start) in enumerate(ends):
         lines = []
         for q in range(PACK_ROWS // rows):
             group = [
-                info_ref[k, :, start : start + reach].astype(F32)
+                info_ref[k, :, pl.ds(start, reach)].astype(F32)
                 if k < count
                 else jnp.zeros((rows, reach), F32)
                 for k in range(q * features // reach, (q + 1) * features // reach)
@@ -192,58 +201,69 @@
         out_specs=whole(x.shape),
         out_shape=shape(x.shape, F32),
         scratch_shapes=[pltpu.VMEM((rows * own, features), BF)] * 2,
-        compiler_params=params(20),
+        compiler_params=params(12),
         cost_estimate=cost(2 * rows * own * features * features * taps * 0.72, 11e6),
         name="conv_inner",
     )(info, x, conv_w)
 
 
 def conv_outer_kernel(
-    own_info_ref, left_ref, right_ref, w_ref, vec_ref, acc_hbm, hidden_ref, info_ref, acc, even, odd, sem
+    own_info_ref, near_hbm, far_hbm, low_w_ref, high_w_ref, vec_ref, acc_hbm,
+    hidden_ref, info_ref, acc, *rest,
 ):
+    even, odd, (halos, sem, halo_sems) = rest[:2], rest[2:4], rest[4:]
     step = pl.program_id(0)
     rows, own, features = hidden_ref.shape
     taps = info_ref.shape[0] - 1
     half = taps // 2
     reach = STEP * half
-    order = [k for k in range(taps) if k != half]
-    buffers = (even, odd)
+    buffers = ((even[0], even[1]), (odd[0], odd[1]))
     load = pltpu.make_async_copy(acc_hbm, acc, sem)
 
     def span(k):
         n = STEP * abs(k - half)
         return (0 if k < half else own - n), n
 
+    def sides(i):
+        return (i, low_w_ref, 0), (taps - 1 - i, high_w_ref, 1)
+
     def build(i):
-        k = order[i]
-        low, n = span(k)
-        left = k < half
-        source = reach - n if left else 0
-        shift = -n if left else n
-        at = reach + low
-        ids = info_ref[0]
-        matched = (info_ref[1 + k][:, at : at + n] == 1) & (
-            ids[:, at + shift : at + shift + n] == ids[:, at : at + n]
-        )
-        halo = left_ref if left else right_ref
-        put_masked(
-            buffers[i % 2],
-            [halo[r * reach + source : r * reach + source + n, :] for r in range(rows)],
-            mask_columns(matched), n, features,
-        )
+        for k, _, side in sides(i):
+            low, n = span(k)
+            source = 0 if side else reach - n
+            at = reach + low
+            shift = n if side else -n
+            ids = info_ref[0]
+            matched = (info_ref[1 + k][:, at : at + n] == 1) & (
+                ids[:, at + shift : at + shift + n] == ids[:, at : at + n]
+            )
+            put_masked(
+                buffers[i % 2][side],
+                [halos[side, r * reach + source : r * reach + source + n, :] for r in range(rows)],
+                mask_columns(matched), n, features,
+            )
 
     def run(i):
-        low, n = span(order[i])
-        if i + 1 < len(order):
+        if i + 1 < half:
             build(i + 1)
-        product = dot(buffers[i % 2][: rows * n, :], w_ref[0], 1, 0).reshape(rows, n, features)
-        acc[:, low : low + n, :] += product
+        for k, w_ref, side in sides(i):
+            low, n = span(k)
+            product = dot(buffers[i % 2][side][: rows * n, :], w_ref[0], 1, 0)
+            acc[:, low : low + n, :] += product.reshape(rows, n, features)
 
     @pl.when(step == 0)
     def _():
+        copies = [
+            pltpu.make_async_copy(src, halos.at[side], halo_sems.at[i])
+            for i, (src, side) in enumerate(zip((near_hbm, far_hbm), pair_sides(), strict=True))
+        ]
+        for copy in copies:
+            copy.start()
         load.start()
-        for halo, at in ((left_ref, 0), (right_ref, reach + own)):
-            lines = halo[rows * reach :, :].astype(F32)
+        for copy in copies:
+            copy.wait()
+        for side, at in enumerate((0, reach + own)):
+            lines = halos[side, rows * reach :, :].astype(F32)
             for k in range(taps + 1):
                 q, m = divmod(k, features // reach)
                 part = lines[q * rows : (q + 1) * rows, m * reach : (m + 1) * reach]
@@ -252,15 +272,15 @@
         build(0)
         load.wait()
 
-    for i in range(len(order)):
+    for i in range(half):
         pl.when(step == i)(functools.partial(run, i))
 
-    @pl.when(step == len(order) - 1)
+    @pl.when(step == half - 1)
     def _():
         hidden_ref[...] = (acc[...] + vec_ref[0:1, :]).astype(BF)
 
 
-def conv_outer(info, acc, left, right, conv_w, vec):
+def conv_outer(info, acc, near, far, conv_w, vec):
     rows, own, features = acc.shape
     taps = conv_w.shape[0]
     half = taps // 2
@@ -268,24 +288,29 @@
     info_dims = (1 + taps, rows, own + 2 * reach)
     return pl.pallas_call(
         conv_outer_kernel,
-        grid=(taps - 1,),
+        grid=(half,),
         in_specs=[
             whole(info.shape),
-            whole(left.shape),
-            whole(right.shape),
-            pl.BlockSpec((1, features, features), lambda i: (jnp.where(i < half, i, i + 1), 0, 0)),
+            pl.BlockSpec(memory_space=pl.ANY),
+            pl.BlockSpec(memory_space=pl.ANY),
+            pl.BlockSpec((1, features, features), lambda i: (i, 0, 0)),
+            pl.BlockSpec((1, features, features), lambda i: (taps - 1 - i, 0, 0)),
             whole(vec.shape),
             pl.BlockSpec(memory_space=pl.ANY),
         ],
         out_specs=[whole(acc.shape), whole(info_dims)],
         out_shape=[shape(acc.shape, BF), shape(info_dims, jnp.int32)],
         scratch_shapes=[pltpu.VMEM(acc.shape, F32)]
-        + [pltpu.VMEM((rows * reach, features), BF)] * 2
-        + [pltpu.SemaphoreType.DMA],
-        compiler_params=params(18),
+        + [pltpu.VMEM((rows * reach, features), BF)] * 4
+        + [
+            pltpu.VMEM((2,) + near.shape, BF),
+            pltpu.SemaphoreType.DMA,
+            pltpu.SemaphoreType.DMA((2,)),
+        ],
+        compiler_params=params(14),
         cost_estimate=cost(2 * rows * own * features * features * taps * 0.28, 11e6),
         name="conv_outer",
-    )(info, left, right, conv_w, vec, acc)
+    )(info, near, far, conv_w, conv_w, vec, acc)
 
 
 def place_block(out_ref, value, dest_wide, dest_narrow, rows_at, blocks):
@@ -296,14 +321,6 @@
     rel_narrow = lax.axis_index("narrow") ^ dest_narrow
     index = (rel_wide >> 1) * 8 + (rel_narrow & 1) * 4 + (rel_narrow >> 1)
     out_ref[rel_wide & 1, index, rows_at, :] = value
-
-
-def ship(pairs, sems):
-    copies = [pltpu.make_async_copy(src, dst, sems.at[i]) for i, (src, dst) in enumerate(pairs)]
-    for copy in copies:
-        copy.start()
-    for copy in copies:
-        copy.wait()
 
 
 def gradient_outputs(blocks, height, width):
@@ -327,7 +344,7 @@
 
 def middle_kernel(
     blocks,
-    hidden_ref, x_ref, ct_ref, w_in_ref, w_out_ref, vec_ref, b_in_ref,
+    hidden_ref, x_ref, ct_ref, w_in_hbm, w_out_hbm, vec_ref, b_in_ref,
     out_ref, gmixed_ref, gh_ref, *rest,
 ):
     if blocks == (1, 1):
@@ -335,7 +352,7 @@
     else:
         keep_ref, send_ref, *rest = rest
     (
-        act_scr, slope_scr, up_scr, gw_out_acc, gw_in_acc, b_in_acc, gain_one_acc,
+        w_in_ref, w_out_ref, load_sems, act_scr, slope_scr, up_scr, gw_out_acc, gw_in_acc, b_in_acc, gain_one_acc,
         bias_one_acc, gain_two_acc, bias_two_acc, conv_b_acc, *rest,
     ) = rest
     if blocks != (1, 1):
@@ -345,14 +362,21 @@
     steps = pl.num_programs(0)
     size = act_scr.shape[0]
     features, hidden_units = w_in_ref.shape
+    loads = [
+        pltpu.make_async_copy(src, dst, load_sems.at[i])
+        for i, (src, dst) in enumerate(((w_in_hbm, w_in_ref), (w_out_hbm, w_out_ref)))
+    ]
 
     @pl.when(step == 0)
     def _():
+        for load in loads:
+            load.start()
         for ref in (
-            gw_out_acc, gw_in_acc, b_in_acc, gain_one_acc, bias_one_acc, gain_two_acc,
-            bias_two_acc, conv_b_acc,
+            b_in_acc, gain_one_acc, bias_one_acc, gain_two_acc, bias_two_acc, conv_b_acc,
         ):
             ref[...] = jnp.zeros_like(ref)
+        for load in loads:
+            load.wait()
 
     gain_one = vec_ref[1:2, :]
     bias_one = vec_ref[2:3, :]
@@ -401,8 +425,10 @@
         b_in_acc[:, cols] += fold(up_low.astype(F32))
     total = dot(up_scr[...], w_in_ref[...], 1, 1)
     for cols in pieces:
-        gw_out_acc[cols, :] += dot(act_scr[:, cols], gproj, 0, 0)
-        gw_in_acc[:, cols] += dot(mixed_low, up_scr[:, cols], 0, 0)
+        before = jnp.where(step == 0, 0.0, gw_out_acc[cols, :])
+        gw_out_acc[cols, :] = before + dot(act_scr[:, cols], gproj, 0, 0)
+        before = jnp.where(step == 0, 0.0, gw_in_acc[:, cols])
+        gw_in_acc[:, cols] = before + dot(mixed_low, up_scr[:, cols], 0, 0)
     g_mixed = ct_ref[...].reshape(size, features).astype(F32) + total
     gmixed_ref[...] = g_mixed.reshape(gmixed_ref.shape)
     hid = hidden_ref[...].reshape(size, features).astype(F32)
@@ -421,6 +447,29 @@
 
     @pl.when(step == steps - 1)
     def _():
+        n_wide, n_narrow = blocks
+        height, width = hidden_units // n_narrow, features // n_wide
+        base = 0 if blocks == (1, 1) else height
+        for n in range(n_narrow):
+            product = gw_out_acc[n * height : (n + 1) * height, :].astype(BF)
+            for w in range(n_wide):
+                place_block(
+                    gw_out_ref, product[:, w * width : (w + 1) * width], w, n, slice(0, height),
+                    blocks,
+                )
+        copies = []
+
+        def ship(rows):
+            for i, ref in enumerate((keep_ref, send_ref)):
+                copies.append(
+                    pltpu.make_async_copy(
+                        gw_ref.at[i, :, rows, :], ref.at[:, rows, :], sems.at[len(copies)]
+                    )
+                )
+                copies[-1].start()
+
+        if blocks != (1, 1):
+            ship(pl.ds(0, base))
         row = 0
         for ref in (conv_b_acc, gain_one_acc, bias_one_acc, b_in_acc, gain_two_acc, bias_two_acc):
             summed = jnp.sum(ref[...], axis=0, keepdims=True)
@@ -428,10 +477,8 @@
                 sums_ref[row : row + 1, :] = summed[:, j * 128 : (j + 1) * 128]
                 row += 1
         sums_ref[row:, :] = jnp.zeros_like(sums_ref[row:, :])
-        n_wide, n_narrow = blocks
         height, width = features // n_narrow, hidden_units // n_wide
         lanes = gw_in_ref.shape[-1]
-        base = 0 if blocks == (1, 1) else hidden_units // n_narrow
         for w in range(n_wide):
             product = gw_in_acc[:, w * width : (w + 1) * width].astype(BF)
             for n in range(n_narrow):
@@ -441,21 +488,15 @@
                         product[n * height : (n + 1) * height, j * lanes : (j + 1) * lanes],
                         w, n, slice(base + j * height, base + (j + 1) * height), blocks,
                     )
-        height, width = hidden_units // n_narrow, features // n_wide
-        for n in range(n_narrow):
-            product = gw_out_acc[n * height : (n + 1) * height, :].astype(BF)
-            for w in range(n_wide):
-                place_block(
-                    gw_out_ref, product[:, w * width : (w + 1) * width], w, n, slice(0, height),
-                    blocks,
-                )
         if blocks != (1, 1):
             last = gw_ref.shape[2] - 16
             for i, part in enumerate(in_pair(sums_ref[...])):
                 for j in range(4):
                     for side in range(2):
                         gw_ref[side, 4 * i + j, last:, :] = part[16 * j : 16 * (j + 1)]
-            ship(((gw_ref.at[0], keep_ref), (gw_ref.at[1], send_ref)), sems)
+            ship(pl.ds(base, gw_ref.shape[2] - base))
+            for copy in copies:
+                copy.wait()
 
 
 def middle(blocks, hidden, x, ct, w_in, w_out, vec, b_in):
@@ -478,45 +519,45 @@
         specs = [pl.BlockSpec(memory_space=pl.ANY)] * 2
         scratch = [
             pltpu.VMEM((2,) + shapes[0].shape, BF), pltpu.VMEM((sums, 128), F32),
-            pltpu.SemaphoreType.DMA((2,)),
+            pltpu.SemaphoreType.DMA((4,)),
         ]
     narrow = pltpu.VMEM((8, features), F32)
     return pl.pallas_call(
         functools.partial(middle_kernel, blocks),
         grid=(rows // block_rows,),
         in_specs=[
-            row_block, row_block, row_block, whole(w_in.shape), whole(w_out.shape),
-            whole(vec.shape), whole(b_in.shape),
+            row_block, row_block, row_block, pl.BlockSpec(memory_space=pl.ANY),
+            pl.BlockSpec(memory_space=pl.ANY), whole(vec.shape), whole(b_in.shape),
         ],
         out_specs=[row_block, row_block, row_block] + specs,
         out_shape=[shape(x.shape, BF), shape(x.shape, F32), shape(x.shape, BF)] + shapes,
         scratch_shapes=[
+            pltpu.VMEM(w_in.shape, BF), pltpu.VMEM(w_out.shape, BF), pltpu.SemaphoreType.DMA((2,)),
             pltpu.VMEM((size, hidden_units), BF), pltpu.VMEM((size, hidden_units), F32),
             pltpu.VMEM((size, hidden_units), BF),
             pltpu.VMEM((hidden_units, features), F32), pltpu.VMEM((features, hidden_units), F32),
             pltpu.VMEM((8, hidden_units), F32), narrow, narrow, narrow, narrow, narrow,
         ] + scratch,
-        compiler_params=params(46),
+        compiler_params=params(34),
         cost_estimate=cost(2 * total * features * 6 * hidden_units, 34e6),
         name="middle",
     )(hidden, x, ct, w_in, w_out, vec, b_in)
 
 
-def by_parity(step, run, even, odd):
-    pl.when(step % 2 == 0)(lambda: run(even, odd))
-    pl.when(step % 2 == 1)(lambda: run(odd, even))
-
-
-def fill_copies(ext, left_hbm, own_hbm, right_hbm, sems):
+GROUP = 3
+
+
+def fill_copies(ext, near_hbm, own_hbm, far_hbm, sems):
     rows, own = own_hbm.shape[0], own_hbm.shape[1]
     reach = (ext.shape[1] - own) // 2
     copies = [pltpu.make_async_copy(own_hbm, ext.at[:, pl.ds(reach, own), :], sems.at[0])]
-    for side, (halo, at) in enumerate(((left_hbm, 0), (right_hbm, reach + own))):
+    for i, (halo, side) in enumerate(zip((near_hbm, far_hbm), pair_sides(), strict=True)):
+        at = pl.multiple_of(side * (reach + own), reach)
         for r in range(rows):
             source = halo.at[r] if len(halo.shape) == 3 else halo.at[pl.ds(r * reach, reach), :]
             copies.append(
                 pltpu.make_async_copy(
-                    source, ext.at[r, pl.ds(at, reach), :], sems.at[1 + side * rows + r]
+                    source, ext.at[r, pl.ds(at, reach), :], sems.at[1 + i * rows + r]
                 )
             )
     return copies
@@ -543,31 +584,34 @@
         )
 
 
-def weight_kernel(blocks, first, info_ref, gh_ref, x_hbm, left_hbm, right_hbm, *rest):
+def weight_kernel(blocks, info_ref, gh_ref, x_hbm, near_hbm, far_hbm, *rest):
     if blocks == (1, 1):
-        gw_ref, ext, lhs_even, lhs_odd, fill_sems = rest
+        gw_ref, ext, *lhs, fill_sems = rest
     else:
-        keep_ref, send_ref, ext, lhs_even, lhs_odd, fill_sems, gw_ref, sems = rest
+        keep_ref, send_ref, ext, *lhs, fill_sems, gw_ref, sems = rest
     step = pl.program_id(0)
     steps = pl.num_programs(0)
     rows, own, features = gh_ref.shape
 
     @pl.when(step == 0)
     def _():
-        copies = fill_copies(ext, left_hbm, x_hbm, right_hbm, fill_sems)
+        copies = fill_copies(ext, near_hbm, x_hbm, far_hbm, fill_sems)
         for copy in copies:
             copy.start()
         for copy in copies:
             copy.wait()
-        build_masked(lhs_even, ext, info_ref, first, True)
+        build_masked(lhs[0], ext, info_ref, 0, True)
 
     n_wide, n_narrow = blocks
     height, width = features // n_narrow, features // n_wide
-    rows_at = pl.ds(pl.multiple_of(step * height, height), height)
-
-    def run(lhs, lhs_next):
-        build_masked(lhs_next, ext, info_ref, first + jnp.minimum(step + 1, steps - 1), True)
-        product = dot(lhs[...], gh_ref[...].reshape(rows * own, features), 0, 0).astype(BF)
+    last_tap = GROUP * steps - 1
+    for j in range(GROUP):
+        tap = GROUP * step + j
+        build_masked(
+            lhs[(j + 1) % GROUP], ext, info_ref, jnp.minimum(tap + 1, last_tap), True
+        )
+        product = dot(lhs[j][...], gh_ref[...].reshape(rows * own, features), 0, 0).astype(BF)
+        rows_at = pl.ds(pl.multiple_of(tap * height, height), height)
         for n in range(n_narrow):
             for w in range(n_wide):
                 place_block(
@@ -576,12 +620,11 @@
                     w, n, rows_at, blocks,
                 )
 
-    by_parity(step, run, lhs_even, lhs_odd)
-
     if blocks != (1, 1):
 
         def shipping(at):
-            rows_of = pl.ds(pl.multiple_of(at * height, height), height)
+            size = GROUP * height
+            rows_of = pl.ds(pl.multiple_of(at * size, size), size)
             return [
                 pltpu.make_async_copy(
                     gw_ref.at[i, :, rows_of, :], ref.at[:, rows_of, :], sems.at[i]
@@ -603,42 +646,42 @@
                 copy.wait()
 
 
-def weight_gradient(blocks, info, gh, x, left, right, first, taps):
+def weight_gradient(blocks, info, gh, x, near, far, taps):
     rows, own, features = x.shape
     shapes, specs, scratch = gradient_outputs(blocks, taps * features, features)
     return pl.pallas_call(
-        functools.partial(weight_kernel, blocks, first),
-        grid=(taps,),
+        functools.partial(weight_kernel, blocks),
+        grid=(taps // GROUP,),
         in_specs=[whole(info.shape), whole(gh.shape)] + [pl.BlockSpec(memory_space=pl.ANY)] * 3,
         out_specs=specs,
         out_shape=shapes,
         scratch_shapes=[
             pltpu.VMEM((rows, info.shape[2], features), BF),
-            pltpu.VMEM((rows * own, features), BF),
-            pltpu.VMEM((rows * own, features), BF),
+            *[pltpu.VMEM((rows * own, features), BF)] * GROUP,
             pltpu.SemaphoreType.DMA((1 + 2 * rows,)),
         ]
         + scratch,
-        compiler_params=params(28),
+        compiler_params=params(18),
         cost_estimate=cost(2 * rows * own * features * features * taps, 12e6),
         name="weight_gradient",
-    )(info, gh, x, left, right)
+    )(info, gh, x, near, far)
 
 
 def input_kernel(
-    first, info_ref, w_ref, gh_hbm, left_hbm, right_hbm, gmixed_hbm,
-    gx_hbm, ext, lhs_even, lhs_odd, acc, gmixed, fill_sems, in_sem, out_sems,
+    first, info_ref, w_ref, gh_hbm, near_hbm, far_hbm, gmixed_hbm,
+    gx_hbm, ext, *rest,
 ):
-    tap = pl.program_id(0)
-    taps = pl.num_programs(0)
+    *lhs, acc, gmixed, fill_sems, in_sem, out_sems = rest
+    step = pl.program_id(0)
+    steps = pl.num_programs(0)
     rows, own, features = gmixed.shape
     batch = pl.ds(first, rows)
     base = pltpu.make_async_copy(gmixed_hbm.at[batch], gmixed, in_sem)
 
-    @pl.when(tap == 0)
+    @pl.when(step == 0)
     def _():
         copies = fill_copies(
-            ext, left_hbm.at[batch], gh_hbm.at[batch], right_hbm.at[batch], fill_sems
+            ext, near_hbm.at[batch], gh_hbm.at[batch], far_hbm.at[batch], fill_sems
         )
         for copy in copies:
             copy.start()
@@ -646,15 +689,17 @@
         acc[...] = jnp.zeros_like(acc)
         for copy in copies:
             copy.wait()
-        build_masked(lhs_even, ext, info_ref, 0, False, first)
-
-    def run(lhs, lhs_next):
-        build_masked(lhs_next, ext, info_ref, jnp.minimum(tap + 1, taps - 1), False, first)
-        acc[...] += dot(lhs[...], w_ref[0], 1, 1)
-
-    by_parity(tap, run, lhs_even, lhs_odd)
-
-    @pl.when(tap == taps - 1)
+        build_masked(lhs[0], ext, info_ref, 0, False, first)
+
+    last_tap = GROUP * steps - 1
+    for j in range(GROUP):
+        tap = GROUP * step + j
+        build_masked(
+            lhs[(j + 1) % GROUP], ext, info_ref, jnp.minimum(tap + 1, last_tap), False, first
+        )
+        acc[...] += dot(lhs[j][...], w_ref[j], 1, 1)
+
+    @pl.when(step == steps - 1)
     def _():
         base.wait()
         copies = []
@@ -667,16 +712,16 @@
             copy.wait()
 
 
-def input_gradient(info, conv_w, gh, left, right, gmixed, first, rows):
+def input_gradient(info, conv_w, gh, near, far, gmixed, first, rows):
     _, own, features = gh.shape
-    reach = left.shape[1]
+    reach = STEP * (conv_w.shape[0] // 2)
     taps = conv_w.shape[0]
     return pl.pallas_call(
         functools.partial(input_kernel, first),
-        grid=(taps,),
+        grid=(taps // GROUP,),
         in_specs=[
             whole(info.shape),
-            pl.BlockSpec((1, features, features), lambda i: (i, 0, 0)),
+            pl.BlockSpec((GROUP, features, features), lambda i: (i, 0, 0)),
         ]
         + [pl.BlockSpec(memory_space=pl.ANY)] * 4,
         out_specs=pl.BlockSpec(memory_space=pl.ANY),
@@ -684,18 +729,17 @@
         input_output_aliases={5: 0},
         scratch_shapes=[
             pltpu.VMEM((rows, own + 2 * reach, features), BF),
-            pltpu.VMEM((rows * own, features), BF),
-            pltpu.VMEM((rows * own, features), BF),
+            *[pltpu.VMEM((rows * own, features), BF)] * GROUP,
             pltpu.VMEM((rows * own, features), F32),
             pltpu.VMEM((rows, own, features), F32),
             pltpu.SemaphoreType.DMA((1 + 2 * rows,)),
             pltpu.SemaphoreType.DMA,
             pltpu.SemaphoreType.DMA((rows,)),
         ],
-        compiler_params=params(20),
+        compiler_params=params(10 + rows),
         cost_estimate=cost(2 * rows * own * features * features * taps, 12e6),
         name="input_gradient",
-    )(info, conv_w, gh, left, right, gmixed)
+    )(info, conv_w, gh, near, far, gmixed)
 
 
 class Additions(NamedTuple):
@@ -870,33 +914,37 @@
     by_hand = (n_wide, n_narrow) == (4, 8)
     blocks = (4, 8) if by_hand else (1, 1)
 
-    to_right = [(i, i + 1) for i in range(n_wide - 1)]
-    to_left = [(i + 1, i) for i in range(n_wide - 1)]
-
-    def halos(value, dim):
-        last = value.shape[dim]
-        left = lax.ppermute(lax.slice_in_dim(value, last - reach, last, axis=dim), "wide", to_right)
-        right = lax.ppermute(lax.slice_in_dim(value, 0, reach, axis=dim), "wide", to_left)
-        return left, right
+    near_pairs = [(i, i ^ 1) for i in range(n_wide)]
+    far_pairs = [(i, i + 1 if i % 2 else i - 1) for i in range(1, n_wide - 1)]
+
+    def exchange(near, far):
+        far = lax.ppermute(far, "wide", far_pairs)
+        return lax.ppermute(near, "wide", near_pairs), far
+
+    def halos(value):
+        ends = [
+            lax.dynamic_slice_in_dim(value, side * (own - reach), reach, axis=1)
+            for side in pair_sides()
+        ]
+        return exchange(*ends)
 
     in_place = functools.partial(pltpu.with_memory_space_constraint, memory_space=pltpu.HBM)
-    to_send_left, to_send_right, info = pack(
+    *ends, info = pack(
         in_place(inputs), in_place(segments), in_place(jnp.transpose(tap_mask, (1, 0, 2))), reach
     )
-    x_left = lax.ppermute(to_send_right, "wide", to_right)
-    x_right = lax.ppermute(to_send_left, "wide", to_left)
+    x_near, x_far = exchange(*ends)
     vec = jnp.stack([conv_b, ln1_gain, ln1_bias, ln2_gain, ln2_bias]).astype(F32)
     vec = jnp.pad(vec, ((0, 3), (0, 0)))
 
     acc = conv_inner(info, in_place(inputs), in_place(conv_w))
-    hidden, info = conv_outer(info, acc, x_left, x_right, conv_w, vec)
+    hidden, info = conv_outer(info, acc, x_near, x_far, conv_w, vec)
     out, gmixed, gh, *grads = middle(
         blocks, hidden, inputs, cotangent, w_in, w_out, vec, b_in.astype(F32)[None]
     )
     if not by_hand:
-        gh_left, gh_right = halos(gh, 1)
-        gconv = weight_gradient(blocks, info, gh, inputs, x_left, x_right, 0, taps)
-        gx = input_gradient(info, conv_w, gh, gh_left, gh_right, gmixed, 0, rows)
+        gh_near, gh_far = halos(gh)
+        gconv = weight_gradient(blocks, info, gh, inputs, x_near, x_far, taps)
+        gx = input_gradient(info, conv_w, gh, gh_near, gh_far, gmixed, 0, rows)
 
         def reduce(value, dims, wide_dim, narrow_dim):
             value = lax.psum_scatter(
@@ -912,22 +960,22 @@
         sums = lax.psum(grads[2], ("wide", "narrow"))
     else:
         together = lax.optimization_barrier
-        cuts = (0, rows // 4, rows - rows // 4, rows)
+        cuts = (0, (3 * rows + 4) // 8, rows - rows // 4, rows)
 
         def inputs_part(i, gx):
             first, end = cuts[i], cuts[i + 1]
-            return input_gradient(info, conv_w, gh, gh_left, gh_right, gx, first, end - first)
+            return input_gradient(info, conv_w, gh, gh_near, gh_far, gx, first, end - first)
 
         height = features // n_narrow
         f_top = (grads[0].shape[1] - 16) * 3 // 4 // 16 * 16
         c_top = taps * height // 2 // 16 * 16
         f_got = flip(grads[1], "wide", 1)
-        gh_left, gh_right = halos(gh, 1)
+        gh_near, gh_far = halos(gh)
         f = alone(after_core(grads[0], f_got, f_top, 16))
         f_got = flip(f[1], "narrow", 1), flip(f[3], "wide", 2)
-        c = weight_gradient(blocks, info, after(gh, *f), inputs, x_left, x_right, 0, taps)
-
-        c, f, f_got, gh_left, gh_right = together((c, f, f_got, gh_left, gh_right))
+        c = weight_gradient(blocks, info, after(gh, *f), inputs, x_near, x_far, taps)
+
+        c, f, f_got, gh_near, gh_far = together((c, f, f_got, gh_near, gh_far))
         c_got = flip(c[1], "wide", 1)
         f = alone(after_first(f_top, f[0], f_got[0], f[2], f_got[1]))
         f_got = flip(f[1], "wide", 2), flip(f[3], "narrow", 1)

time: 157 us -> 153 us (0.975)
  Pallas kernels: 109 us -> 101 us
  waiting for transfers between devices: 13.8 us -> 19.4 us
  starting transfers between devices: 31.2 us -> 27.5 us
    pallas_call x5, Pallas kernels: 46.8 us -> 40.7 us  [the longest x3 20.5 us: input_gradient(): pl.pallas_call(functools.partial(input_kernel, first), grid=(taps // GROU...]
    ppermute x16, waiting for transfers between devices: 13.8 us -> 19.4 us  [flip(): return lax.ppermute(value, axis, [(i, i ^ bit) for i in range(size)])]
    ppermute x4, starting transfers between devices: 7.13 us -> 2.17 us  [the longest x2 1.58 us: exchange(): far = lax.ppermute(far, 'wide', far_pairs)]
    pallas_call x1, Pallas kernels: 42.4 us -> 38.5 us  [middle(): pl.pallas_call(functools.partial(middle_kernel, blocks), grid=(rows // bl...]
    pallas_call x4, Pallas kernels: 3.19 us -> 5.21 us  [alone(): pl.pallas_call(functools.partial(additions_kernel, work.fn, len(work.oper...]
  transfers between devices with their start and end apart: 20 -> 20, of which waited for: 5 -> 6; matrix products, arithmetic and copies ran while one was open for 1% -> 1% of each run, Pallas kernels for 36% -> 34%
where the time goes in v4:
time: 153 us; the launch traced here: 152 us
  Pallas kernels  101 us (66%)
  starting transfers between devices  27.5 us (18%)
  waiting for transfers between devices  19.4 us (13%)
  local copies, waits for them, and re-layouts  2.92 us (2%)
    pallas_call x1, Pallas kernels, middle(): pl.pallas_call(functools.partial(middle_kernel, blocks), grid=(rows // bl...  38.5 us
    ppermute x16, starting transfers between devices, flip(): return lax.ppermute(value, axis, [(i, i ^ bit) for i in range(size)])  25.4 us
    pallas_call x3, Pallas kernels, input_gradient(): pl.pallas_call(functools.partial(input_kernel, first), grid=(taps // GROU...  20.5 us
    ppermute x16, waiting for transfers between devices, flip(): return lax.ppermute(value, axis, [(i, i ^ bit) for i in range(size)])  19.4 us
    pallas_call x1, Pallas kernels, weight_gradient(): pl.pallas_call(functools.partial(weight_kernel, blocks), grid=(taps // GR...  15.3 us
    pallas_call x1, Pallas kernels, conv_inner(): pl.pallas_call(conv_inner_kernel, grid=(taps,), in_specs=[whole(info.shap...  11.9 us
    pallas_call x4, Pallas kernels, alone(): pl.pallas_call(functools.partial(additions_kernel, work.fn, len(work.oper...  5.21 us
    pallas_call x1, Pallas kernels, conv_outer(): pl.pallas_call(conv_outer_kernel, grid=(half,), in_specs=[whole(info.shap...  4.91 us
  transfers between devices with their start and end apart: 20, of which 6 were waited for; matrix products, arithmetic and copies ran while one was open for 1% of the time, Pallas kernels for 34%

profile of v4, /device:TPU:0, one launch (start us, length us, event | category | flops | bytes accessed | tf_op | source)
XLA Modules:
  0.0 152.2 jit_solution(16099365086732905766)
XLA Ops:
  0.7 3.1 %pack.1 = (bf16[1056,512]{1,0:T(8,128)(2,1)}, bf16[1056,512]{1,0:T(8,128)(2,1)}, s32[10,8,256]{2,1,0:T(8,128)S(1)}) custom-call(bf16[8,256,512]{2,1,0:T(8,128)(2,1)} %x_hbm.3, s32[8,256]{1,0:T(8,128)} %ids_hbm.1, s32[9,8,256]{2,1,0:T(8,128)} %bitcast.28), custom_call_target="tpu_custom_call" | custom-call | flops 20000 | bytes 80000 | tf_op jit(solution)/shard_map/pack/pallas_call | solution.py:122
  5.3 11.9 %conv_inner.1.acc_hbm = f32[8,256,512]{2,1,0:T(8,128)S(1)} custom-call(s32[10,8,256]{2,1,0:T(8,128)S(1)} %get-tuple-element.95.info_ref.own_info_ref, bf16[8,256,512]{2,1,0:T(8,128)(2,1)} %x_hbm.3, bf16[9,512,512]{2,1,0:T(8,128)(2,1)} %w_ref.7), custom_call_target="tpu_custom_call" | custom-call | flops 139156944 | bytes 220000 | tf_op jit(solution)/shard_map/conv_inner/pallas_call | solution.py:193
  17.3 4.9 %conv_outer.1 = (bf16[8,256,512]{2,1,0:T(8,128)(2,1)S(1)}, s32[10,8,512]{2,1,0:T(8,128)S(1)}) custom-call(s32[10,8,256]{2,1,0:T(8,128)S(1)} %get-tuple-element.95.info_ref.own_info_ref, bf16[1056,512]{1,0:T(8,128)(2,1)S(1)} %collective-permute-done.near_hbm, bf16[1056,512]{1,0:T(8,128)(2,1)S(1)} %collective-permute-done.1.far_hbm, ...), custom_call_target="tpu_custom_call" | custom-call | flops 54116588 | bytes 220000 | tf_op jit(solution)/shard_map/conv_outer/pallas_call | solution.py:289
  22.3 38.5 %middle.1 = (bf16[8,256,512]{2,1,0:T(8,128)(2,1)}, f32[8,256,512]{2,1,0:T(8,128)}, bf16[8,256,512]{2,1,0:T(8,128)(2,1)S(1)}, bf16[16,528,128]{2,1,0:T(8,128)(2,1)S(1)}, bf16[16,528,128]{2,1,0:T(8,128)(2,1)}) custom-call(bf16[8,256,512]{2,1,0:T(8,128)(2,1)S(1)} %get-tuple-element.98.hidden_ref, bf16[8,256,512]{2,1,0:T(8,128)(2,1)S(1)} %copy-done, ...), custom_call_target="tpu_custom_call" | custom-call | flops 515396064 | bytes 680000 | tf_op jit(solution)/shard_map/middle/pallas_call | solution.py:525
  60.8 1.4 copy-done.4
  62.2 4.6 %collective-permute-start.2 = (bf16[16,528,128]{2,1,0:T(8,128)(2,1)}, bf16[16,528,128]{2,1,0:T(8,128)(2,1)}, u32[]{:S(2)}, u32[]{:S(2)}) collective-permute-start(bf16[16,528,128]{2,1,0:T(8,128)(2,1)} %get-tuple-element.103), channel_id=1, source_target_pairs={{0,8},{8,0},{16,24},{24,16},{1,9},{9,1},{17,25},{25,17},{2,10},{10... | collective-permute-start | bytes 6488072 | tf_op jit(solution)/shard_map/ppermute | solution.py:774
  67.1 0.9 collective-permute-start.6
  68.0 3.4 %collective-permute-done.2 = bf16[16,528,128]{2,1,0:T(8,128)(2,1)} collective-permute-done((bf16[16,528,128]{2,1,0:T(8,128)(2,1)}, bf16[16,528,128]{2,1,0:T(8,128)(2,1)}, u32[]{:S(2)}, u32[]{:S(2)}) %collective-permute-start.2) | collective-permute-done | bytes 2162720 | tf_op jit(solution)/shard_map/ppermute | solution.py:774
  71.3 3.0 %additions.8 = (bf16[2,4,400,128]{3,2,1,0:T(8,128)(2,1)S(1)}, bf16[2,4,400,128]{3,2,1,0:T(8,128)(2,1)S(1)}, bf16[2,4,128,128]{3,2,1,0:T(8,128)(2,1)S(1)}, bf16[2,4,128,128]{3,2,1,0:T(8,128)(2,1)S(1)}) custom-call(bf16[2,2,4,528,128]{4,3,2,1,0:T(8,128)(2,1)S(1)} %bitcast.25, bf16[2,2,4,528,128]{4,3,2,1,0:T(8,128)(2,1)} %bitcast.3.refs_1_), custom_call_target="tpu_custom_call" | custom-call | flops 64880 | bytes 129761 | tf_op jit(solution)/shard_map/additions/pallas_call | solution.py:760
  74.4 2.1 %collective-permute-start.3 = (bf16[2,4,400,128]{3,2,1,0:T(8,128)(2,1)S(1)}, bf16[2,4,400,128]{3,2,1,0:T(8,128)(2,1)S(1)}, u32[]{:S(2)}, u32[]{:S(2)}) collective-permute-start(bf16[2,4,400,128]{3,2,1,0:T(8,128)(2,1)S(1)} %get-tuple-element.105), channel_id=1, source_target_pairs={{0,1},{1,0},{2,3},{3,2},{4,5},{5,4},{6,7},{7,6},{8,9},{9,8},{10,11... | collective-permute-start | bytes 2457608 | tf_op jit(solution)/shard_map/ppermute | solution.py:774
  76.5 1.5 %collective-permute-start.4 = (bf16[2,4,128,128]{3,2,1,0:T(8,128)(2,1)S(1)}, bf16[2,4,128,128]{3,2,1,0:T(8,128)(2,1)S(1)}, u32[]{:S(2)}, u32[]{:S(2)}) collective-permute-start(bf16[2,4,128,128]{3,2,1,0:T(8,128)(2,1)S(1)} %get-tuple-element.107), channel_id=1, source_target_pairs={{0,16},{8,24},{16,0},{24,8},{1,17},{9,25},{17,1},{25,9},{2,18},{10... | collective-permute-start | bytes 786440 | tf_op jit(solution)/shard_map/ppermute | solution.py:774
  78.1 15.3 %weight_gradient.1 = (bf16[16,576,128]{2,1,0:T(8,128)(2,1)S(1)}, bf16[16,576,128]{2,1,0:T(8,128)(2,1)S(1)}) custom-call(s32[10,8,512]{2,1,0:T(8,128)S(1)} %get-tuple-element.100.info_ref, bf16[8,256,512]{2,1,0:T(8,128)(2,1)S(1)} %get-tuple-element.108.gh_ref.gh_hbm, bf16[8,256,512]{2,1,0:T(8,128)(2,1)S(1)} %copy-done.1, ...), custom_call_target="tpu_custom_call" | custom-call | flops 193273536 | bytes 240000 | tf_op jit(solution)/shard_map/weight_gradient/pallas_call | solution.py:652
  93.4 2.0 %collective-permute-done.3.refs_1_ = bf16[2,4,400,128]{3,2,1,0:T(8,128)(2,1)S(1)} collective-permute-done((bf16[2,4,400,128]{3,2,1,0:T(8,128)(2,1)S(1)}, bf16[2,4,400,128]{3,2,1,0:T(8,128)(2,1)S(1)}, u32[]{:S(2)}, u32[]{:S(2)}) %collective-permute-start.3) | collective-permute-done | bytes 819232 | tf_op jit(solution)/shard_map/ppermute | solution.py:774
  96.0 1.4 collective-permute-start.8
  97.3 1.5 collective-permute-start.9
  98.8 7.5 %input_gradient.3.gmixed_hbm = f32[8,256,512]{2,1,0:T(8,128)} custom-call(s32[10,8,512]{2,1,0:T(8,128)S(1)} %get-tuple-element.100.info_ref, bf16[9,512,512]{2,1,0:T(8,128)(2,1)S(1)} %bitcast.22, bf16[8,256,512]{2,1,0:T(8,128)(2,1)S(1)} %get-tuple-element.108.gh_ref.gh_hbm, ...), custom_call_target="tpu_custom_call", output_to_operand_aliasing={{}: (5, {})} | custom-call | flops 72477576 | bytes 240000 | tf_op jit(solution)/shard_map/input_gradient/pallas_call | solution.py:719
  106.3 2.0 %collective-permute-done.8.a_got = bf16[4,416,128]{2,1,0:T(8,128)(2,1)S(1)} collective-permute-done((bf16[4,416,128]{2,1,0:T(8,128)(2,1)S(1)}, bf16[4,416,128]{2,1,0:T(8,128)(2,1)S(1)}, u32[]{:S(2)}, u32[]{:S(2)}) %collective-permute-start.8) | collective-permute-done | bytes 426016 | tf_op jit(solution)/shard_map/ppermute | solution.py:774
  108.3 1.1 additions.10
  109.4 1.8 %collective-permute-start.10 = (bf16[2,4,288,128]{3,2,1,0:T(8,128)(2,1)S(1)}, bf16[2,4,288,128]{3,2,1,0:T(8,128)(2,1)S(1)}, u32[]{:S(2)}, u32[]{:S(2)}) collective-permute-start(bf16[2,4,288,128]{3,2,1,0:T(8,128)(2,1)S(1)} %get-tuple-element.129), channel_id=1, source_target_pairs={{0,1},{1,0},{2,3},{3,2},{4,5},{5,4},{6,7},{7,6},{8,9},{9,8},{10,11... | collective-permute-start | bytes 1769480 | tf_op jit(solution)/shard_map/ppermute | solution.py:774
  111.2 1.0 collective-permute-start.11
  112.4 1.6 %collective-permute-start.12 = (bf16[640,128]{1,0:T(8,128)(2,1)S(1)}, bf16[640,128]{1,0:T(8,128)(2,1)S(1)}, u32[]{:S(2)}, u32[]{:S(2)}) collective-permute-start(bf16[640,128]{1,0:T(8,128)(2,1)S(1)} %get-tuple-element.142), channel_id=1, source_target_pairs={{0,2},{1,3},{2,0},{3,1},{4,6},{5,7},{6,4},{7,5},{8,10},{9,11},{10,... | collective-permute-start | bytes 491528 | tf_op jit(solution)/shard_map/ppermute | solution.py:774
  114.0 2.6 %collective-permute-start.13 = (bf16[640,128]{1,0:T(8,128)(2,1)S(1)}, bf16[640,128]{1,0:T(8,128)(2,1)S(1)}, u32[]{:S(2)}, u32[]{:S(2)}) collective-permute-start(bf16[640,128]{1,0:T(8,128)(2,1)S(1)} %get-tuple-element.143), channel_id=1, source_target_pairs={{0,4},{1,5},{2,6},{3,7},{4,0},{5,1},{6,2},{7,3},{8,12},{9,13},{10,... | collective-permute-start | bytes 491528 | tf_op jit(solution)/shard_map/ppermute | solution.py:774
  116.8 7.5 %input_gradient.4.gmixed_hbm = f32[8,256,512]{2,1,0:T(8,128)} custom-call(s32[10,8,512]{2,1,0:T(8,128)S(1)} %get-tuple-element.100.info_ref, bf16[9,512,512]{2,1,0:T(8,128)(2,1)S(1)} %bitcast.22, bf16[8,256,512]{2,1,0:T(8,128)(2,1)S(1)} %get-tuple-element.108.gh_ref.gh_hbm, ...), custom_call_target="tpu_custom_call", output_to_operand_aliasing={{}: (5, {})} | custom-call | flops 72477576 | bytes 240000 | tf_op jit(solution)/shard_map/input_gradient/pallas_call | solution.py:719
  124.3 4.4 %collective-permute-done.13.z2 = bf16[640,128]{1,0:T(8,128)(2,1)S(1)} collective-permute-done((bf16[640,128]{1,0:T(8,128)(2,1)S(1)}, bf16[640,128]{1,0:T(8,128)(2,1)S(1)}, u32[]{:S(2)}, u32[]{:S(2)}) %collective-permute-start.13) | collective-permute-done | bytes 163872 | tf_op jit(solution)/shard_map/ppermute | solution.py:774
  129.3 1.0 collective-permute-start.15
  130.9 5.5 %input_gradient.5 = f32[8,256,512]{2,1,0:T(8,128)} custom-call(s32[10,8,512]{2,1,0:T(8,128)S(1)} %get-tuple-element.100.info_ref, bf16[9,512,512]{2,1,0:T(8,128)(2,1)S(1)} %bitcast.22, bf16[8,256,512]{2,1,0:T(8,128)(2,1)S(1)} %get-tuple-element.108.gh_ref.gh_hbm, ...), custom_call_target="tpu_custom_call", output_to_operand_aliasing={{}: (5, {})} | custom-call | flops 48318384 | bytes 240000 | tf_op jit(solution)/shard_map/input_gradient/pallas_call | solution.py:719
  137.2 2.4 %collective-permute-start.17 = (bf16[576,128]{1,0:T(8,128)(2,1)S(1)}, bf16[576,128]{1,0:T(8,128)(2,1)S(1)}, u32[]{:S(2)}, u32[]{:S(2)}) collective-permute-start(bf16[576,128]{1,0:T(8,128)(2,1)S(1)} %get-tuple-element.165), channel_id=1, source_target_pairs={{0,2},{1,3},{2,0},{3,1},{4,6},{5,7},{6,4},{7,5},{8,10},{9,11},{10,... | collective-permute-start | bytes 442376 | tf_op jit(solution)/shard_map/ppermute | solution.py:774
  139.6 1.6 %collective-permute-start.18 = (bf16[576,128]{1,0:T(8,128)(2,1)S(1)}, bf16[576,128]{1,0:T(8,128)(2,1)S(1)}, u32[]{:S(2)}, u32[]{:S(2)}) collective-permute-start(bf16[576,128]{1,0:T(8,128)(2,1)S(1)} %get-tuple-element.166), channel_id=1, source_target_pairs={{0,4},{1,5},{2,6},{3,7},{4,0},{5,1},{6,2},{7,3},{8,12},{9,13},{10,... | collective-permute-start | bytes 442376 | tf_op jit(solution)/shard_map/ppermute | solution.py:774
  141.2 1.4 collective-permute-start.19
  142.5 0.7 additions.15
  144.5 7.0 %collective-permute-done.18.z2 = bf16[576,128]{1,0:T(8,128)(2,1)S(1)} collective-permute-done((bf16[576,128]{1,0:T(8,128)(2,1)S(1)}, bf16[576,128]{1,0:T(8,128)(2,1)S(1)}, u32[]{:S(2)}, u32[]{:S(2)}) %collective-permute-start.18) | collective-permute-done | bytes 147488 | tf_op jit(solution)/shard_map/ppermute | solution.py:774
  151.4 0.8 additions.14
  (75 shorter events, 5.6 us)
Async XLA Ops:
  3.9 13.4 %collective-permute-start = (bf16[1056,512]{1,0:T(8,128)(2,1)}, bf16[1056,512]{1,0:T(8,128)(2,1)S(1)}, u32[]{:S(2)}, u32[]{:S(2)}) collective-permute-start(bf16[1056,512]{1,0:T(8,128)(2,1)} %get-tuple-element.96), channel_id=1, source_target_pairs={{0,8},{8,0},{16,24},{24,16},{1,9},{9,1},{17,25},{25,17},{2,10},{10... | collective-permute-start | bytes 3244040 | tf_op jit(solution)/shard_map/ppermute | solution.py:922
  4.4 12.9 %collective-permute-start.1 = (bf16[1056,512]{1,0:T(8,128)(2,1)}, bf16[1056,512]{1,0:T(8,128)(2,1)S(1)}, u32[]{:S(2)}, u32[]{:S(2)}) collective-permute-start(bf16[1056,512]{1,0:T(8,128)(2,1)} %get-tuple-element.97), channel_id=1, source_target_pairs={{8,16},{16,8},{9,17},{17,9},{10,18},{18,10},{11,19},{19,11},{12,20... | collective-permute-start | bytes 3244040 | tf_op jit(solution)/shard_map/ppermute | solution.py:921
  5.3 12.0 %slice-start = ((s8[4718592]{0:T(1024)(128)(4,1)}), s8[4194304]{0:T(1024)(128)(4,1)S(1)}, s32[]{:S(2)}) async-start(s8[4718592]{0:T(1024)(128)(4,1)} %bitcast.19), calls=%async_computation | async-start | bytes 8388608
  5.3 12.0 %slice-start.1 = ((s8[4718592]{0:T(1024)(128)(4,1)}), s8[524288]{0:T(1024)(128)(4,1)S(1)}, s32[]{:S(2)}) async-start(s8[4718592]{0:T(1024)(128)(4,1)} %bitcast.19), calls=%async_computation.1 | async-start | bytes 1048576
  17.2 5.0 %copy-start = (bf16[8,256,512]{2,1,0:T(8,128)(2,1)S(1)}, bf16[8,256,512]{2,1,0:T(8,128)(2,1)}, u32[]{:S(2)}) copy-start(bf16[8,256,512]{2,1,0:T(8,128)(2,1)} %x_hbm.3) | copy-start | bytes 6291460
  17.2 5.0 %copy-start.6 = (bf16[8,256,512]{2,1,0:T(8,128)(2,1)S(1)}, bf16[8,256,512]{2,1,0:T(8,128)(2,1)}, u32[]{:S(2)}) copy-start(bf16[8,256,512]{2,1,0:T(8,128)(2,1)} %ct_ref.1) | copy-start | bytes 6291460
  17.3 5.0 %copy-start.7 = (bf16[512,2048]{1,0:T(8,128)(2,1)S(1)}, bf16[512,2048]{1,0:T(8,128)(2,1)}, u32[]{:S(2)}) copy-start(bf16[512,2048]{1,0:T(8,128)(2,1)} %w_in_hbm.1) | copy-start | bytes 6291460
  17.3 5.0 %copy-start.8 = (bf16[2048,512]{1,0:T(8,128)(2,1)S(1)}, bf16[2048,512]{1,0:T(8,128)(2,1)}, u32[]{:S(2)}) copy-start(bf16[2048,512]{1,0:T(8,128)(2,1)} %w_out_hbm.1) | copy-start | bytes 6291460
  17.3 4.9 %copy-start.2 = (bf16[1056,512]{1,0:T(8,128)(2,1)}, bf16[1056,512]{1,0:T(8,128)(2,1)S(1)}, u32[]{:S(2)}) copy-start(bf16[1056,512]{1,0:T(8,128)(2,1)S(1)} %collective-permute-done.1.far_hbm) | copy-start | bytes 3244036
  62.2 9.1 %collective-permute-start.2 = (bf16[16,528,128]{2,1,0:T(8,128)(2,1)}, bf16[16,528,128]{2,1,0:T(8,128)(2,1)}, u32[]{:S(2)}, u32[]{:S(2)}) collective-permute-start(bf16[16,528,128]{2,1,0:T(8,128)(2,1)} %get-tuple-element.103), channel_id=1, source_target_pairs={{0,8},{8,0},{16,24},{24,16},{1,9},{9,1},{17,25},{25,17},{2,10},{10... | collective-permute-start | bytes 6488072 | tf_op jit(solution)/shard_map/ppermute | solution.py:774
  66.8 4.5 %copy-start.5 = (bf16[16,528,128]{2,1,0:T(8,128)(2,1)S(1)}, bf16[16,528,128]{2,1,0:T(8,128)(2,1)}, u32[]{:S(2)}) copy-start(bf16[16,528,128]{2,1,0:T(8,128)(2,1)} %copy-done.4) | copy-start | bytes 6488068
  67.0 26.4 %collective-permute-start.5 = (bf16[8,128,512]{2,1,0:T(8,128)(2,1)S(1)}, bf16[8,128,512]{2,1,0:T(8,128)(2,1)S(1)}, u32[]{:S(2)}, u32[]{:S(2)}) collective-permute-start(bf16[8,128,512]{2,1,0:T(8,128)(2,1)S(1)} %get-tuple-element.180), channel_id=1, source_target_pairs={{0,8},{8,0},{16,24},{24,16},{1,9},{9,1},{17,25},{25,17},{2,10},{10... | collective-permute-start | bytes 3145736 | tf_op jit(solution)/shard_map/ppermute | solution.py:922
  67.1 26.3 %collective-permute-start.6 = (bf16[8,128,512]{2,1,0:T(8,128)(2,1)S(1)}, bf16[8,128,512]{2,1,0:T(8,128)(2,1)S(1)}, u32[]{:S(2)}, u32[]{:S(2)}) collective-permute-start(bf16[8,128,512]{2,1,0:T(8,128)(2,1)S(1)} %get-tuple-element.179), channel_id=1, source_target_pairs={{8,16},{16,8},{9,17},{17,9},{10,18},{18,10},{11,19},{19,11},{12,20... | collective-permute-start | bytes 3145736 | tf_op jit(solution)/shard_map/ppermute | solution.py:921
  71.3 6.7 %copy-start.1 = (bf16[8,256,512]{2,1,0:T(8,128)(2,1)S(1)}, bf16[8,256,512]{2,1,0:T(8,128)(2,1)}, u32[]{:S(2)}) copy-start(bf16[8,256,512]{2,1,0:T(8,128)(2,1)} %x_hbm.3) | copy-start | bytes 6291460
  71.3 6.7 %copy-start.3 = (bf16[1056,512]{1,0:T(8,128)(2,1)S(1)}, bf16[1056,512]{1,0:T(8,128)(2,1)}, u32[]{:S(2)}) copy-start(bf16[1056,512]{1,0:T(8,128)(2,1)} %copy-done.2) | copy-start | bytes 3244036
  74.4 21.1 %collective-permute-start.3 = (bf16[2,4,400,128]{3,2,1,0:T(8,128)(2,1)S(1)}, bf16[2,4,400,128]{3,2,1,0:T(8,128)(2,1)S(1)}, u32[]{:S(2)}, u32[]{:S(2)}) collective-permute-start(bf16[2,4,400,128]{3,2,1,0:T(8,128)(2,1)S(1)} %get-tuple-element.105), channel_id=1, source_target_pairs={{0,1},{1,0},{2,3},{3,2},{4,5},{5,4},{6,7},{7,6},{8,9},{9,8},{10,11... | collective-permute-start | bytes 2457608 | tf_op jit(solution)/shard_map/ppermute | solution.py:774
  76.5 16.9 %collective-permute-start.4 = (bf16[2,4,128,128]{3,2,1,0:T(8,128)(2,1)S(1)}, bf16[2,4,128,128]{3,2,1,0:T(8,128)(2,1)S(1)}, u32[]{:S(2)}, u32[]{:S(2)}) collective-permute-start(bf16[2,4,128,128]{3,2,1,0:T(8,128)(2,1)S(1)} %get-tuple-element.107), channel_id=1, source_target_pairs={{0,16},{8,24},{16,0},{24,8},{1,17},{9,25},{17,1},{25,9},{2,18},{10... | collective-permute-start | bytes 786440 | tf_op jit(solution)/shard_map/ppermute | solution.py:774
  78.1 20.8 %slice-start.2 = ((s8[4718592]{0:T(1024)(128)(4,1)}), s8[4194304]{0:T(1024)(128)(4,1)S(1)}, s32[]{:S(2)}) async-start(s8[4718592]{0:T(1024)(128)(4,1)} %bitcast.21), calls=%async_computation.2 | async-start | bytes 8388608
  78.1 20.7 %slice-start.3 = ((s8[4718592]{0:T(1024)(128)(4,1)}), s8[524288]{0:T(1024)(128)(4,1)S(1)}, s32[]{:S(2)}) async-start(s8[4718592]{0:T(1024)(128)(4,1)} %bitcast.21), calls=%async_computation.3 | async-start | bytes 1048576
  95.4 12.8 %collective-permute-start.7 = (bf16[16,576,128]{2,1,0:T(8,128)(2,1)S(1)}, bf16[16,576,128]{2,1,0:T(8,128)(2,1)S(1)}, u32[]{:S(2)}, u32[]{:S(2)}) collective-permute-start(bf16[16,576,128]{2,1,0:T(8,128)(2,1)S(1)} %get-tuple-element.124), channel_id=1, source_target_pairs={{0,8},{8,0},{16,24},{24,16},{1,9},{9,1},{17,25},{25,17},{2,10},{10... | collective-permute-start | bytes 7077896 | tf_op jit(solution)/shard_map/ppermute | solution.py:774
  96.0 12.3 %collective-permute-start.8 = (bf16[4,416,128]{2,1,0:T(8,128)(2,1)S(1)}, bf16[4,416,128]{2,1,0:T(8,128)(2,1)S(1)}, u32[]{:S(2)}, u32[]{:S(2)}) collective-permute-start(bf16[4,416,128]{2,1,0:T(8,128)(2,1)S(1)} %get-tuple-element.119), channel_id=1, source_target_pairs={{0,16},{8,24},{16,0},{24,8},{1,17},{9,25},{17,1},{25,9},{2,18},{10... | collective-permute-start | bytes 1277960 | tf_op jit(solution)/shard_map/ppermute | solution.py:774
  97.3 9.0 %collective-permute-start.9 = (bf16[4,128,128]{2,1,0:T(8,128)(2,1)S(1)}, bf16[4,128,128]{2,1,0:T(8,128)(2,1)S(1)}, u32[]{:S(2)}, u32[]{:S(2)}) collective-permute-start(bf16[4,128,128]{2,1,0:T(8,128)(2,1)S(1)} %get-tuple-element.121), channel_id=1, source_target_pairs={{0,1},{1,0},{2,3},{3,2},{4,5},{5,4},{6,7},{7,6},{8,9},{9,8},{10,11... | collective-permute-start | bytes 393224 | tf_op jit(solution)/shard_map/ppermute | solution.py:774
  109.4 19.3 %collective-permute-start.10 = (bf16[2,4,288,128]{3,2,1,0:T(8,128)(2,1)S(1)}, bf16[2,4,288,128]{3,2,1,0:T(8,128)(2,1)S(1)}, u32[]{:S(2)}, u32[]{:S(2)}) collective-permute-start(bf16[2,4,288,128]{3,2,1,0:T(8,128)(2,1)S(1)} %get-tuple-element.129), channel_id=1, source_target_pairs={{0,1},{1,0},{2,3},{3,2},{4,5},{5,4},{6,7},{7,6},{8,9},{9,8},{10,11... | collective-permute-start | bytes 1769480 | tf_op jit(solution)/shard_map/ppermute | solution.py:774
  111.2 17.5 %collective-permute-start.11 = (bf16[2,4,288,128]{3,2,1,0:T(8,128)(2,1)S(1)}, bf16[2,4,288,128]{3,2,1,0:T(8,128)(2,1)S(1)}, u32[]{:S(2)}, u32[]{:S(2)}) collective-permute-start(bf16[2,4,288,128]{3,2,1,0:T(8,128)(2,1)S(1)} %get-tuple-element.131), channel_id=1, source_target_pairs={{0,16},{8,24},{16,0},{24,8},{1,17},{9,25},{17,1},{25,9},{2,18},{10... | collective-permute-start | bytes 1769480 | tf_op jit(solution)/shard_map/ppermute | solution.py:774
  112.4 11.9 %collective-permute-start.12 = (bf16[640,128]{1,0:T(8,128)(2,1)S(1)}, bf16[640,128]{1,0:T(8,128)(2,1)S(1)}, u32[]{:S(2)}, u32[]{:S(2)}) collective-permute-start(bf16[640,128]{1,0:T(8,128)(2,1)S(1)} %get-tuple-element.142), channel_id=1, source_target_pairs={{0,2},{1,3},{2,0},{3,1},{4,6},{5,7},{6,4},{7,5},{8,10},{9,11},{10,... | collective-permute-start | bytes 491528 | tf_op jit(solution)/shard_map/ppermute | solution.py:774
  114.0 14.7 %collective-permute-start.13 = (bf16[640,128]{1,0:T(8,128)(2,1)S(1)}, bf16[640,128]{1,0:T(8,128)(2,1)S(1)}, u32[]{:S(2)}, u32[]{:S(2)}) collective-permute-start(bf16[640,128]{1,0:T(8,128)(2,1)S(1)} %get-tuple-element.143), channel_id=1, source_target_pairs={{0,4},{1,5},{2,6},{3,7},{4,0},{5,1},{6,2},{7,3},{8,12},{9,13},{10,... | collective-permute-start | bytes 491528 | tf_op jit(solution)/shard_map/ppermute | solution.py:774
  116.6 12.1 %collective-permute-start.14 = (bf16[640,128]{1,0:T(8,128)(2,1)S(1)}, bf16[640,128]{1,0:T(8,128)(2,1)S(1)}, u32[]{:S(2)}, u32[]{:S(2)}) collective-permute-start(bf16[640,128]{1,0:T(8,128)(2,1)S(1)} %get-tuple-element.144), channel_id=1, source_target_pairs={{0,6},{1,7},{2,4},{3,5},{4,2},{5,3},{6,0},{7,1},{8,14},{9,15},{10,... | collective-permute-start | bytes 491528 | tf_op jit(solution)/shard_map/ppermute | solution.py:774
  129.3 7.1 %collective-permute-start.15 = (bf16[4,288,128]{2,1,0:T(8,128)(2,1)S(1)}, bf16[4,288,128]{2,1,0:T(8,128)(2,1)S(1)}, u32[]{:S(2)}, u32[]{:S(2)}) collective-permute-start(bf16[4,288,128]{2,1,0:T(8,128)(2,1)S(1)} %get-tuple-element.151), channel_id=1, source_target_pairs={{0,16},{8,24},{16,0},{24,8},{1,17},{9,25},{17,1},{25,9},{2,18},{10... | collective-permute-start | bytes 884744 | tf_op jit(solution)/shard_map/ppermute | solution.py:774
  130.3 6.7 %collective-permute-start.16 = (bf16[4,288,128]{2,1,0:T(8,128)(2,1)S(1)}, bf16[4,288,128]{2,1,0:T(8,128)(2,1)S(1)}, u32[]{:S(2)}, u32[]{:S(2)}) collective-permute-start(bf16[4,288,128]{2,1,0:T(8,128)(2,1)S(1)} %get-tuple-element.153), channel_id=1, source_target_pairs={{0,1},{1,0},{2,3},{3,2},{4,5},{5,4},{6,7},{7,6},{8,9},{9,8},{10,11... | collective-permute-start | bytes 884744 | tf_op jit(solution)/shard_map/ppermute | solution.py:774
  137.2 7.3 %collective-permute-start.17 = (bf16[576,128]{1,0:T(8,128)(2,1)S(1)}, bf16[576,128]{1,0:T(8,128)(2,1)S(1)}, u32[]{:S(2)}, u32[]{:S(2)}) collective-permute-start(bf16[576,128]{1,0:T(8,128)(2,1)S(1)} %get-tuple-element.165), channel_id=1, source_target_pairs={{0,2},{1,3},{2,0},{3,1},{4,6},{5,7},{6,4},{7,5},{8,10},{9,11},{10,... | collective-permute-start | bytes 442376 | tf_op jit(solution)/shard_map/ppermute | solution.py:774
  139.6 11.9 %collective-permute-start.18 = (bf16[576,128]{1,0:T(8,128)(2,1)S(1)}, bf16[576,128]{1,0:T(8,128)(2,1)S(1)}, u32[]{:S(2)}, u32[]{:S(2)}) collective-permute-start(bf16[576,128]{1,0:T(8,128)(2,1)S(1)} %get-tuple-element.166), channel_id=1, source_target_pairs={{0,4},{1,5},{2,6},{3,7},{4,0},{5,1},{6,2},{7,3},{8,12},{9,13},{10,... | collective-permute-start | bytes 442376 | tf_op jit(solution)/shard_map/ppermute | solution.py:774
  141.2 10.3 %collective-permute-start.19 = (bf16[576,128]{1,0:T(8,128)(2,1)S(1)}, bf16[576,128]{1,0:T(8,128)(2,1)S(1)}, u32[]{:S(2)}, u32[]{:S(2)}) collective-permute-start(bf16[576,128]{1,0:T(8,128)(2,1)S(1)} %get-tuple-element.167), channel_id=1, source_target_pairs={{0,6},{1,7},{2,4},{3,5},{4,2},{5,3},{6,0},{7,1},{8,14},{9,15},{10,... | collective-permute-start | bytes 442376 | tf_op jit(solution)/shard_map/ppermute | solution.py:774
  (7 other events, 28.3 us)

commit v5 on v4

--- a/solution.py
+++ b/solution.py
@@ -967,13 +967,13 @@
             return input_gradient(info, conv_w, gh, gh_near, gh_far, gx, first, end - first)
 
         height = features // n_narrow
-        f_top = (grads[0].shape[1] - 16) * 3 // 4 // 16 * 16
+        f_top = (grads[0].shape[1] - 16) * 11 // 16 // 16 * 16
         c_top = taps * height // 2 // 16 * 16
         f_got = flip(grads[1], "wide", 1)
         gh_near, gh_far = halos(gh)
         f = alone(after_core(grads[0], f_got, f_top, 16))
         f_got = flip(f[1], "narrow", 1), flip(f[3], "wide", 2)
-        c = weight_gradient(blocks, info, after(gh, *f), inputs, x_near, x_far, taps)
+        c = weight_gradient(blocks, info, after(gh, *f), in_place(inputs), in_place(x_near), in_place(x_far), taps)
 
         c, f, f_got, gh_near, gh_far = together((c, f, f_got, gh_near, gh_far))
         c_got = flip(c[1], "wide", 1)

time: 153 us -> 150 us (0.980)
  no operation moved by 1% of the time
where the time goes in v5:
time: 150 us
  Pallas kernels  99.8 us (67%)
  starting transfers between devices  27.5 us (18%)
  waiting for transfers between devices  18.3 us (12%)
  local copies, waits for them, and re-layouts  2.92 us (2%)
    pallas_call x1, Pallas kernels, middle(): pl.pallas_call(functools.partial(middle_kernel, blocks), grid=(rows // bl...  38.5 us
    ppermute x16, starting transfers between devices, flip(): return lax.ppermute(value, axis, [(i, i ^ bit) for i in range(size)])  25.4 us
    pallas_call x3, Pallas kernels, input_gradient(): pl.pallas_call(functools.partial(input_kernel, first), grid=(taps // GROU...  20.5 us
    ppermute x16, waiting for transfers between devices, flip(): return lax.ppermute(value, axis, [(i, i ^ bit) for i in range(size)])  18.3 us
    pallas_call x1, Pallas kernels, weight_gradient(): pl.pallas_call(functools.partial(weight_kernel, blocks), grid=(taps // GR...  14.1 us
    pallas_call x1, Pallas kernels, conv_inner(): pl.pallas_call(conv_inner_kernel, grid=(taps,), in_specs=[whole(info.shap...  11.9 us
    pallas_call x4, Pallas kernels, alone(): pl.pallas_call(functools.partial(additions_kernel, work.fn, len(work.oper...  4.97 us
    pallas_call x1, Pallas kernels, conv_outer(): pl.pallas_call(conv_outer_kernel, grid=(half,), in_specs=[whole(info.shap...  4.91 us
  transfers between devices with their start and end apart: 20, of which 6 were waited for; matrix products, arithmetic and copies ran while one was open for 1% of the time, Pallas kernels for 34%

profile of v5, /device:TPU:0, one launch (start us, length us, event | category | flops | bytes accessed | tf_op | source)
XLA Modules:
  0.0 149.7 jit_solution(4998826490839853553)
XLA Ops:
  0.7 3.1 %pack.1 = (bf16[1056,512]{1,0:T(8,128)(2,1)}, bf16[1056,512]{1,0:T(8,128)(2,1)}, s32[10,8,256]{2,1,0:T(8,128)S(1)}) custom-call(bf16[8,256,512]{2,1,0:T(8,128)(2,1)} %x_hbm.3, s32[8,256]{1,0:T(8,128)} %ids_hbm.1, s32[9,8,256]{2,1,0:T(8,128)} %bitcast.28), custom_call_target="tpu_custom_call" | custom-call | flops 20000 | bytes 80000 | tf_op jit(solution)/shard_map/pack/pallas_call | solution.py:122
  5.3 11.9 %conv_inner.1.acc_hbm = f32[8,256,512]{2,1,0:T(8,128)S(1)} custom-call(s32[10,8,256]{2,1,0:T(8,128)S(1)} %get-tuple-element.95.info_ref.own_info_ref, bf16[8,256,512]{2,1,0:T(8,128)(2,1)} %x_hbm.3, bf16[9,512,512]{2,1,0:T(8,128)(2,1)} %w_ref.7), custom_call_target="tpu_custom_call" | custom-call | flops 139156944 | bytes 220000 | tf_op jit(solution)/shard_map/conv_inner/pallas_call | solution.py:193
  17.4 4.9 %conv_outer.1 = (bf16[8,256,512]{2,1,0:T(8,128)(2,1)S(1)}, s32[10,8,512]{2,1,0:T(8,128)S(1)}) custom-call(s32[10,8,256]{2,1,0:T(8,128)S(1)} %get-tuple-element.95.info_ref.own_info_ref, bf16[1056,512]{1,0:T(8,128)(2,1)S(1)} %collective-permute-done.near_hbm, bf16[1056,512]{1,0:T(8,128)(2,1)S(1)} %collective-permute-done.1.far_hbm, ...), custom_call_target="tpu_custom_call" | custom-call | flops 54116588 | bytes 220000 | tf_op jit(solution)/shard_map/conv_outer/pallas_call | solution.py:289
  22.3 38.5 %middle.1 = (bf16[8,256,512]{2,1,0:T(8,128)(2,1)}, f32[8,256,512]{2,1,0:T(8,128)}, bf16[8,256,512]{2,1,0:T(8,128)(2,1)S(1)}, bf16[16,528,128]{2,1,0:T(8,128)(2,1)S(1)}, bf16[16,528,128]{2,1,0:T(8,128)(2,1)}) custom-call(bf16[8,256,512]{2,1,0:T(8,128)(2,1)S(1)} %get-tuple-element.98.hidden_ref, bf16[8,256,512]{2,1,0:T(8,128)(2,1)S(1)} %copy-done, ...), custom_call_target="tpu_custom_call" | custom-call | flops 515396064 | bytes 680000 | tf_op jit(solution)/shard_map/middle/pallas_call | solution.py:525
  60.8 1.4 copy-done.3
  62.2 4.6 %collective-permute-start.2 = (bf16[16,528,128]{2,1,0:T(8,128)(2,1)}, bf16[16,528,128]{2,1,0:T(8,128)(2,1)}, u32[]{:S(2)}, u32[]{:S(2)}) collective-permute-start(bf16[16,528,128]{2,1,0:T(8,128)(2,1)} %get-tuple-element.103), channel_id=1, source_target_pairs={{0,8},{8,0},{16,24},{24,16},{1,9},{9,1},{17,25},{25,17},{2,10},{10... | collective-permute-start | bytes 6488072 | tf_op jit(solution)/shard_map/ppermute | solution.py:774
  67.1 0.9 collective-permute-start.6
  68.0 3.4 %collective-permute-done.2 = bf16[16,528,128]{2,1,0:T(8,128)(2,1)} collective-permute-done((bf16[16,528,128]{2,1,0:T(8,128)(2,1)}, bf16[16,528,128]{2,1,0:T(8,128)(2,1)}, u32[]{:S(2)}, u32[]{:S(2)}) %collective-permute-start.2) | collective-permute-done | bytes 2162720 | tf_op jit(solution)/shard_map/ppermute | solution.py:774
  71.4 2.8 %additions.8 = (bf16[2,4,368,128]{3,2,1,0:T(8,128)(2,1)S(1)}, bf16[2,4,368,128]{3,2,1,0:T(8,128)(2,1)S(1)}, bf16[2,4,160,128]{3,2,1,0:T(8,128)(2,1)S(1)}, bf16[2,4,160,128]{3,2,1,0:T(8,128)(2,1)S(1)}) custom-call(bf16[2,2,4,528,128]{4,3,2,1,0:T(8,128)(2,1)S(1)} %bitcast.25, bf16[2,2,4,528,128]{4,3,2,1,0:T(8,128)(2,1)} %bitcast.3.refs_1_), custom_call_target="tpu_custom_call" | custom-call | flops 64880 | bytes 129761 | tf_op jit(solution)/shard_map/additions/pallas_call | solution.py:760
  74.2 2.1 %collective-permute-start.3 = (bf16[2,4,368,128]{3,2,1,0:T(8,128)(2,1)S(1)}, bf16[2,4,368,128]{3,2,1,0:T(8,128)(2,1)S(1)}, u32[]{:S(2)}, u32[]{:S(2)}) collective-permute-start(bf16[2,4,368,128]{3,2,1,0:T(8,128)(2,1)S(1)} %get-tuple-element.105), channel_id=1, source_target_pairs={{0,1},{1,0},{2,3},{3,2},{4,5},{5,4},{6,7},{7,6},{8,9},{9,8},{10,11... | collective-permute-start | bytes 2261000 | tf_op jit(solution)/shard_map/ppermute | solution.py:774
  76.3 1.4 collective-permute-start.4
  77.7 14.1 %weight_gradient.1 = (bf16[16,576,128]{2,1,0:T(8,128)(2,1)S(1)}, bf16[16,576,128]{2,1,0:T(8,128)(2,1)S(1)}) custom-call(s32[10,8,512]{2,1,0:T(8,128)S(1)} %get-tuple-element.100.info_ref, bf16[8,256,512]{2,1,0:T(8,128)(2,1)S(1)} %get-tuple-element.108.gh_ref.gh_hbm, bf16[8,256,512]{2,1,0:T(8,128)(2,1)} %x_hbm.3, bf16[1056,512]{1,0:T(8,128)(2,1)} %copy-done.1, ...), custom_call_target="tpu_custom_call" | custom-call | flops 193273536 | bytes 240000 | tf_op jit(solution)/shard_map/weight_gradient/pallas_call | solution.py:652
  91.8 1.8 %collective-permute-done.3.refs_1_ = bf16[2,4,368,128]{3,2,1,0:T(8,128)(2,1)S(1)} collective-permute-done((bf16[2,4,368,128]{3,2,1,0:T(8,128)(2,1)S(1)}, bf16[2,4,368,128]{3,2,1,0:T(8,128)(2,1)S(1)}, u32[]{:S(2)}, u32[]{:S(2)}) %collective-permute-start.3) | collective-permute-done | bytes 753696 | tf_op jit(solution)/shard_map/ppermute | solution.py:774
  94.2 1.5 collective-permute-start.8
  95.7 1.5 collective-permute-start.9
  97.2 7.5 %input_gradient.3.gmixed_hbm = f32[8,256,512]{2,1,0:T(8,128)} custom-call(s32[10,8,512]{2,1,0:T(8,128)S(1)} %get-tuple-element.100.info_ref, bf16[9,512,512]{2,1,0:T(8,128)(2,1)S(1)} %bitcast.22, bf16[8,256,512]{2,1,0:T(8,128)(2,1)S(1)} %get-tuple-element.108.gh_ref.gh_hbm, ...), custom_call_target="tpu_custom_call", output_to_operand_aliasing={{}: (5, {})} | custom-call | flops 72477576 | bytes 240000 | tf_op jit(solution)/shard_map/input_gradient/pallas_call | solution.py:719
  104.7 1.1 collective-permute-done.8.a_got
  105.8 1.1 additions.10
  106.9 1.8 %collective-permute-start.10 = (bf16[2,4,288,128]{3,2,1,0:T(8,128)(2,1)S(1)}, bf16[2,4,288,128]{3,2,1,0:T(8,128)(2,1)S(1)}, u32[]{:S(2)}, u32[]{:S(2)}) collective-permute-start(bf16[2,4,288,128]{3,2,1,0:T(8,128)(2,1)S(1)} %get-tuple-element.129), channel_id=1, source_target_pairs={{0,1},{1,0},{2,3},{3,2},{4,5},{5,4},{6,7},{7,6},{8,9},{9,8},{10,11... | collective-permute-start | bytes 1769480 | tf_op jit(solution)/shard_map/ppermute | solution.py:774
  108.7 1.2 collective-permute-start.11
  110.0 1.6 %collective-permute-start.12 = (bf16[640,128]{1,0:T(8,128)(2,1)S(1)}, bf16[640,128]{1,0:T(8,128)(2,1)S(1)}, u32[]{:S(2)}, u32[]{:S(2)}) collective-permute-start(bf16[640,128]{1,0:T(8,128)(2,1)S(1)} %get-tuple-element.142), channel_id=1, source_target_pairs={{0,2},{1,3},{2,0},{3,1},{4,6},{5,7},{6,4},{7,5},{8,10},{9,11},{10,... | collective-permute-start | bytes 491528 | tf_op jit(solution)/shard_map/ppermute | solution.py:774
  111.6 2.6 %collective-permute-start.13 = (bf16[640,128]{1,0:T(8,128)(2,1)S(1)}, bf16[640,128]{1,0:T(8,128)(2,1)S(1)}, u32[]{:S(2)}, u32[]{:S(2)}) collective-permute-start(bf16[640,128]{1,0:T(8,128)(2,1)S(1)} %get-tuple-element.143), channel_id=1, source_target_pairs={{0,4},{1,5},{2,6},{3,7},{4,0},{5,1},{6,2},{7,3},{8,12},{9,13},{10,... | collective-permute-start | bytes 491528 | tf_op jit(solution)/shard_map/ppermute | solution.py:774
  114.5 7.5 %input_gradient.4.gmixed_hbm = f32[8,256,512]{2,1,0:T(8,128)} custom-call(s32[10,8,512]{2,1,0:T(8,128)S(1)} %get-tuple-element.100.info_ref, bf16[9,512,512]{2,1,0:T(8,128)(2,1)S(1)} %bitcast.22, bf16[8,256,512]{2,1,0:T(8,128)(2,1)S(1)} %get-tuple-element.108.gh_ref.gh_hbm, ...), custom_call_target="tpu_custom_call", output_to_operand_aliasing={{}: (5, {})} | custom-call | flops 72477576 | bytes 240000 | tf_op jit(solution)/shard_map/input_gradient/pallas_call | solution.py:719
  121.9 4.4 %collective-permute-done.13.z2 = bf16[640,128]{1,0:T(8,128)(2,1)S(1)} collective-permute-done((bf16[640,128]{1,0:T(8,128)(2,1)S(1)}, bf16[640,128]{1,0:T(8,128)(2,1)S(1)}, u32[]{:S(2)}, u32[]{:S(2)}) %collective-permute-start.13) | collective-permute-done | bytes 163872 | tf_op jit(solution)/shard_map/ppermute | solution.py:774
  126.9 0.9 collective-permute-start.15
  128.4 5.5 %input_gradient.5 = f32[8,256,512]{2,1,0:T(8,128)} custom-call(s32[10,8,512]{2,1,0:T(8,128)S(1)} %get-tuple-element.100.info_ref, bf16[9,512,512]{2,1,0:T(8,128)(2,1)S(1)} %bitcast.22, bf16[8,256,512]{2,1,0:T(8,128)(2,1)S(1)} %get-tuple-element.108.gh_ref.gh_hbm, ...), custom_call_target="tpu_custom_call", output_to_operand_aliasing={{}: (5, {})} | custom-call | flops 48318384 | bytes 240000 | tf_op jit(solution)/shard_map/input_gradient/pallas_call | solution.py:719
  134.7 2.4 %collective-permute-start.17 = (bf16[576,128]{1,0:T(8,128)(2,1)S(1)}, bf16[576,128]{1,0:T(8,128)(2,1)S(1)}, u32[]{:S(2)}, u32[]{:S(2)}) collective-permute-start(bf16[576,128]{1,0:T(8,128)(2,1)S(1)} %get-tuple-element.165), channel_id=1, source_target_pairs={{0,2},{1,3},{2,0},{3,1},{4,6},{5,7},{6,4},{7,5},{8,10},{9,11},{10,... | collective-permute-start | bytes 442376 | tf_op jit(solution)/shard_map/ppermute | solution.py:774
  137.1 1.6 %collective-permute-start.18 = (bf16[576,128]{1,0:T(8,128)(2,1)S(1)}, bf16[576,128]{1,0:T(8,128)(2,1)S(1)}, u32[]{:S(2)}, u32[]{:S(2)}) collective-permute-start(bf16[576,128]{1,0:T(8,128)(2,1)S(1)} %get-tuple-element.166), channel_id=1, source_target_pairs={{0,4},{1,5},{2,6},{3,7},{4,0},{5,1},{6,2},{7,3},{8,12},{9,13},{10,... | collective-permute-start | bytes 442376 | tf_op jit(solution)/shard_map/ppermute | solution.py:774
  138.7 1.4 collective-permute-start.19
  140.0 0.7 additions.15
  142.0 6.9 %collective-permute-done.18.z2 = bf16[576,128]{1,0:T(8,128)(2,1)S(1)} collective-permute-done((bf16[576,128]{1,0:T(8,128)(2,1)S(1)}, bf16[576,128]{1,0:T(8,128)(2,1)S(1)}, u32[]{:S(2)}, u32[]{:S(2)}) %collective-permute-start.18) | collective-permute-done | bytes 147488 | tf_op jit(solution)/shard_map/ppermute | solution.py:774
  148.9 0.8 additions.14
  (73 shorter events, 5.6 us)
Async XLA Ops:
  0.7 4.5 %copy-start.8 = (bf16[2048]{0:T(1024)(128)(2,1)S(1)}, bf16[2048]{0:T(1024)(128)(2,1)}, u32[]{:S(2)}) copy-start(bf16[2048]{0:T(1024)(128)(2,1)} %param.19) | copy-start | bytes 12292
  3.9 13.4 %collective-permute-start = (bf16[1056,512]{1,0:T(8,128)(2,1)}, bf16[1056,512]{1,0:T(8,128)(2,1)S(1)}, u32[]{:S(2)}, u32[]{:S(2)}) collective-permute-start(bf16[1056,512]{1,0:T(8,128)(2,1)} %get-tuple-element.96), channel_id=1, source_target_pairs={{0,8},{8,0},{16,24},{24,16},{1,9},{9,1},{17,25},{25,17},{2,10},{10... | collective-permute-start | bytes 3244040 | tf_op jit(solution)/shard_map/ppermute | solution.py:922
  4.4 12.9 %collective-permute-start.1 = (bf16[1056,512]{1,0:T(8,128)(2,1)}, bf16[1056,512]{1,0:T(8,128)(2,1)S(1)}, u32[]{:S(2)}, u32[]{:S(2)}) collective-permute-start(bf16[1056,512]{1,0:T(8,128)(2,1)} %get-tuple-element.97), channel_id=1, source_target_pairs={{8,16},{16,8},{9,17},{17,9},{10,18},{18,10},{11,19},{19,11},{12,20... | collective-permute-start | bytes 3244040 | tf_op jit(solution)/shard_map/ppermute | solution.py:921
  5.3 12.1 %slice-start = ((s8[4718592]{0:T(1024)(128)(4,1)}), s8[4194304]{0:T(1024)(128)(4,1)S(1)}, s32[]{:S(2)}) async-start(s8[4718592]{0:T(1024)(128)(4,1)} %bitcast.19), calls=%async_computation | async-start | bytes 8388608
  5.3 12.1 %slice-start.1 = ((s8[4718592]{0:T(1024)(128)(4,1)}), s8[524288]{0:T(1024)(128)(4,1)S(1)}, s32[]{:S(2)}) async-start(s8[4718592]{0:T(1024)(128)(4,1)} %bitcast.19), calls=%async_computation.1 | async-start | bytes 1048576
  17.2 5.1 %copy-start = (bf16[8,256,512]{2,1,0:T(8,128)(2,1)S(1)}, bf16[8,256,512]{2,1,0:T(8,128)(2,1)}, u32[]{:S(2)}) copy-start(bf16[8,256,512]{2,1,0:T(8,128)(2,1)} %x_hbm.3) | copy-start | bytes 6291460
  17.2 5.1 %copy-start.5 = (bf16[8,256,512]{2,1,0:T(8,128)(2,1)S(1)}, bf16[8,256,512]{2,1,0:T(8,128)(2,1)}, u32[]{:S(2)}) copy-start(bf16[8,256,512]{2,1,0:T(8,128)(2,1)} %ct_ref.1) | copy-start | bytes 6291460
  17.3 5.0 %copy-start.6 = (bf16[512,2048]{1,0:T(8,128)(2,1)S(1)}, bf16[512,2048]{1,0:T(8,128)(2,1)}, u32[]{:S(2)}) copy-start(bf16[512,2048]{1,0:T(8,128)(2,1)} %w_in_hbm.1) | copy-start | bytes 6291460
  17.3 5.0 %copy-start.7 = (bf16[2048,512]{1,0:T(8,128)(2,1)S(1)}, bf16[2048,512]{1,0:T(8,128)(2,1)}, u32[]{:S(2)}) copy-start(bf16[2048,512]{1,0:T(8,128)(2,1)} %w_out_hbm.1) | copy-start | bytes 6291460
  17.3 5.0 %copy-start.1 = (bf16[1056,512]{1,0:T(8,128)(2,1)}, bf16[1056,512]{1,0:T(8,128)(2,1)S(1)}, u32[]{:S(2)}) copy-start(bf16[1056,512]{1,0:T(8,128)(2,1)S(1)} %collective-permute-done.near_hbm) | copy-start | bytes 3244036
  17.3 4.9 %copy-start.2 = (bf16[1056,512]{1,0:T(8,128)(2,1)}, bf16[1056,512]{1,0:T(8,128)(2,1)S(1)}, u32[]{:S(2)}) copy-start(bf16[1056,512]{1,0:T(8,128)(2,1)S(1)} %collective-permute-done.1.far_hbm) | copy-start | bytes 3244036
  62.2 9.2 %collective-permute-start.2 = (bf16[16,528,128]{2,1,0:T(8,128)(2,1)}, bf16[16,528,128]{2,1,0:T(8,128)(2,1)}, u32[]{:S(2)}, u32[]{:S(2)}) collective-permute-start(bf16[16,528,128]{2,1,0:T(8,128)(2,1)} %get-tuple-element.103), channel_id=1, source_target_pairs={{0,8},{8,0},{16,24},{24,16},{1,9},{9,1},{17,25},{25,17},{2,10},{10... | collective-permute-start | bytes 6488072 | tf_op jit(solution)/shard_map/ppermute | solution.py:774
  66.8 4.5 %copy-start.4 = (bf16[16,528,128]{2,1,0:T(8,128)(2,1)S(1)}, bf16[16,528,128]{2,1,0:T(8,128)(2,1)}, u32[]{:S(2)}) copy-start(bf16[16,528,128]{2,1,0:T(8,128)(2,1)} %copy-done.3) | copy-start | bytes 6488068
  67.1 24.7 %collective-permute-start.5 = (bf16[8,128,512]{2,1,0:T(8,128)(2,1)S(1)}, bf16[8,128,512]{2,1,0:T(8,128)(2,1)S(1)}, u32[]{:S(2)}, u32[]{:S(2)}) collective-permute-start(bf16[8,128,512]{2,1,0:T(8,128)(2,1)S(1)} %get-tuple-element.180), channel_id=1, source_target_pairs={{0,8},{8,0},{16,24},{24,16},{1,9},{9,1},{17,25},{25,17},{2,10},{10... | collective-permute-start | bytes 3145736 | tf_op jit(solution)/shard_map/ppermute | solution.py:922
  67.1 24.7 %collective-permute-start.6 = (bf16[8,128,512]{2,1,0:T(8,128)(2,1)S(1)}, bf16[8,128,512]{2,1,0:T(8,128)(2,1)S(1)}, u32[]{:S(2)}, u32[]{:S(2)}) collective-permute-start(bf16[8,128,512]{2,1,0:T(8,128)(2,1)S(1)} %get-tuple-element.179), channel_id=1, source_target_pairs={{8,16},{16,8},{9,17},{17,9},{10,18},{18,10},{11,19},{19,11},{12,20... | collective-permute-start | bytes 3145736 | tf_op jit(solution)/shard_map/ppermute | solution.py:921
  74.2 19.5 %collective-permute-start.3 = (bf16[2,4,368,128]{3,2,1,0:T(8,128)(2,1)S(1)}, bf16[2,4,368,128]{3,2,1,0:T(8,128)(2,1)S(1)}, u32[]{:S(2)}, u32[]{:S(2)}) collective-permute-start(bf16[2,4,368,128]{3,2,1,0:T(8,128)(2,1)S(1)} %get-tuple-element.105), channel_id=1, source_target_pairs={{0,1},{1,0},{2,3},{3,2},{4,5},{5,4},{6,7},{7,6},{8,9},{9,8},{10,11... | collective-permute-start | bytes 2261000 | tf_op jit(solution)/shard_map/ppermute | solution.py:774
  76.3 15.5 %collective-permute-start.4 = (bf16[2,4,160,128]{3,2,1,0:T(8,128)(2,1)S(1)}, bf16[2,4,160,128]{3,2,1,0:T(8,128)(2,1)S(1)}, u32[]{:S(2)}, u32[]{:S(2)}) collective-permute-start(bf16[2,4,160,128]{3,2,1,0:T(8,128)(2,1)S(1)} %get-tuple-element.107), channel_id=1, source_target_pairs={{0,16},{8,24},{16,0},{24,8},{1,17},{9,25},{17,1},{25,9},{2,18},{10... | collective-permute-start | bytes 983048 | tf_op jit(solution)/shard_map/ppermute | solution.py:774
  77.7 19.5 %slice-start.2 = ((s8[4718592]{0:T(1024)(128)(4,1)}), s8[4194304]{0:T(1024)(128)(4,1)S(1)}, s32[]{:S(2)}) async-start(s8[4718592]{0:T(1024)(128)(4,1)} %bitcast.21), calls=%async_computation.2 | async-start | bytes 8388608
  77.7 19.5 %slice-start.3 = ((s8[4718592]{0:T(1024)(128)(4,1)}), s8[524288]{0:T(1024)(128)(4,1)S(1)}, s32[]{:S(2)}) async-start(s8[4718592]{0:T(1024)(128)(4,1)} %bitcast.21), calls=%async_computation.3 | async-start | bytes 1048576
  93.6 12.1 %collective-permute-start.7 = (bf16[16,576,128]{2,1,0:T(8,128)(2,1)S(1)}, bf16[16,576,128]{2,1,0:T(8,128)(2,1)S(1)}, u32[]{:S(2)}, u32[]{:S(2)}) collective-permute-start(bf16[16,576,128]{2,1,0:T(8,128)(2,1)S(1)} %get-tuple-element.124), channel_id=1, source_target_pairs={{0,8},{8,0},{16,24},{24,16},{1,9},{9,1},{17,25},{25,17},{2,10},{10... | collective-permute-start | bytes 7077896 | tf_op jit(solution)/shard_map/ppermute | solution.py:774
  94.2 11.6 %collective-permute-start.8 = (bf16[4,384,128]{2,1,0:T(8,128)(2,1)S(1)}, bf16[4,384,128]{2,1,0:T(8,128)(2,1)S(1)}, u32[]{:S(2)}, u32[]{:S(2)}) collective-permute-start(bf16[4,384,128]{2,1,0:T(8,128)(2,1)S(1)} %get-tuple-element.119), channel_id=1, source_target_pairs={{0,16},{8,24},{16,0},{24,8},{1,17},{9,25},{17,1},{25,9},{2,18},{10... | collective-permute-start | bytes 1179656 | tf_op jit(solution)/shard_map/ppermute | solution.py:774
  95.7 9.0 %collective-permute-start.9 = (bf16[4,160,128]{2,1,0:T(8,128)(2,1)S(1)}, bf16[4,160,128]{2,1,0:T(8,128)(2,1)S(1)}, u32[]{:S(2)}, u32[]{:S(2)}) collective-permute-start(bf16[4,160,128]{2,1,0:T(8,128)(2,1)S(1)} %get-tuple-element.121), channel_id=1, source_target_pairs={{0,1},{1,0},{2,3},{3,2},{4,5},{5,4},{6,7},{7,6},{8,9},{9,8},{10,11... | collective-permute-start | bytes 491528 | tf_op jit(solution)/shard_map/ppermute | solution.py:774
  106.9 19.5 %collective-permute-start.10 = (bf16[2,4,288,128]{3,2,1,0:T(8,128)(2,1)S(1)}, bf16[2,4,288,128]{3,2,1,0:T(8,128)(2,1)S(1)}, u32[]{:S(2)}, u32[]{:S(2)}) collective-permute-start(bf16[2,4,288,128]{3,2,1,0:T(8,128)(2,1)S(1)} %get-tuple-element.129), channel_id=1, source_target_pairs={{0,1},{1,0},{2,3},{3,2},{4,5},{5,4},{6,7},{7,6},{8,9},{9,8},{10,11... | collective-permute-start | bytes 1769480 | tf_op jit(solution)/shard_map/ppermute | solution.py:774
  108.7 17.7 %collective-permute-start.11 = (bf16[2,4,288,128]{3,2,1,0:T(8,128)(2,1)S(1)}, bf16[2,4,288,128]{3,2,1,0:T(8,128)(2,1)S(1)}, u32[]{:S(2)}, u32[]{:S(2)}) collective-permute-start(bf16[2,4,288,128]{3,2,1,0:T(8,128)(2,1)S(1)} %get-tuple-element.131), channel_id=1, source_target_pairs={{0,16},{8,24},{16,0},{24,8},{1,17},{9,25},{17,1},{25,9},{2,18},{10... | collective-permute-start | bytes 1769480 | tf_op jit(solution)/shard_map/ppermute | solution.py:774
  110.0 11.9 %collective-permute-start.12 = (bf16[640,128]{1,0:T(8,128)(2,1)S(1)}, bf16[640,128]{1,0:T(8,128)(2,1)S(1)}, u32[]{:S(2)}, u32[]{:S(2)}) collective-permute-start(bf16[640,128]{1,0:T(8,128)(2,1)S(1)} %get-tuple-element.142), channel_id=1, source_target_pairs={{0,2},{1,3},{2,0},{3,1},{4,6},{5,7},{6,4},{7,5},{8,10},{9,11},{10,... | collective-permute-start | bytes 491528 | tf_op jit(solution)/shard_map/ppermute | solution.py:774
  111.6 14.7 %collective-permute-start.13 = (bf16[640,128]{1,0:T(8,128)(2,1)S(1)}, bf16[640,128]{1,0:T(8,128)(2,1)S(1)}, u32[]{:S(2)}, u32[]{:S(2)}) collective-permute-start(bf16[640,128]{1,0:T(8,128)(2,1)S(1)} %get-tuple-element.143), channel_id=1, source_target_pairs={{0,4},{1,5},{2,6},{3,7},{4,0},{5,1},{6,2},{7,3},{8,12},{9,13},{10,... | collective-permute-start | bytes 491528 | tf_op jit(solution)/shard_map/ppermute | solution.py:774
  114.2 12.1 %collective-permute-start.14 = (bf16[640,128]{1,0:T(8,128)(2,1)S(1)}, bf16[640,128]{1,0:T(8,128)(2,1)S(1)}, u32[]{:S(2)}, u32[]{:S(2)}) collective-permute-start(bf16[640,128]{1,0:T(8,128)(2,1)S(1)} %get-tuple-element.144), channel_id=1, source_target_pairs={{0,6},{1,7},{2,4},{3,5},{4,2},{5,3},{6,0},{7,1},{8,14},{9,15},{10,... | collective-permute-start | bytes 491528 | tf_op jit(solution)/shard_map/ppermute | solution.py:774
  126.9 7.0 %collective-permute-start.15 = (bf16[4,288,128]{2,1,0:T(8,128)(2,1)S(1)}, bf16[4,288,128]{2,1,0:T(8,128)(2,1)S(1)}, u32[]{:S(2)}, u32[]{:S(2)}) collective-permute-start(bf16[4,288,128]{2,1,0:T(8,128)(2,1)S(1)} %get-tuple-element.151), channel_id=1, source_target_pairs={{0,16},{8,24},{16,0},{24,8},{1,17},{9,25},{17,1},{25,9},{2,18},{10... | collective-permute-start | bytes 884744 | tf_op jit(solution)/shard_map/ppermute | solution.py:774
  127.9 6.7 %collective-permute-start.16 = (bf16[4,288,128]{2,1,0:T(8,128)(2,1)S(1)}, bf16[4,288,128]{2,1,0:T(8,128)(2,1)S(1)}, u32[]{:S(2)}, u32[]{:S(2)}) collective-permute-start(bf16[4,288,128]{2,1,0:T(8,128)(2,1)S(1)} %get-tuple-element.153), channel_id=1, source_target_pairs={{0,1},{1,0},{2,3},{3,2},{4,5},{5,4},{6,7},{7,6},{8,9},{9,8},{10,11... | collective-permute-start | bytes 884744 | tf_op jit(solution)/shard_map/ppermute | solution.py:774
  134.7 7.3 %collective-permute-start.17 = (bf16[576,128]{1,0:T(8,128)(2,1)S(1)}, bf16[576,128]{1,0:T(8,128)(2,1)S(1)}, u32[]{:S(2)}, u32[]{:S(2)}) collective-permute-start(bf16[576,128]{1,0:T(8,128)(2,1)S(1)} %get-tuple-element.165), channel_id=1, source_target_pairs={{0,2},{1,3},{2,0},{3,1},{4,6},{5,7},{6,4},{7,5},{8,10},{9,11},{10,... | collective-permute-start | bytes 442376 | tf_op jit(solution)/shard_map/ppermute | solution.py:774
  137.1 11.8 %collective-permute-start.18 = (bf16[576,128]{1,0:T(8,128)(2,1)S(1)}, bf16[576,128]{1,0:T(8,128)(2,1)S(1)}, u32[]{:S(2)}, u32[]{:S(2)}) collective-permute-start(bf16[576,128]{1,0:T(8,128)(2,1)S(1)} %get-tuple-element.166), channel_id=1, source_target_pairs={{0,4},{1,5},{2,6},{3,7},{4,0},{5,1},{6,2},{7,3},{8,12},{9,13},{10,... | collective-permute-start | bytes 442376 | tf_op jit(solution)/shard_map/ppermute | solution.py:774
  138.7 10.3 %collective-permute-start.19 = (bf16[576,128]{1,0:T(8,128)(2,1)S(1)}, bf16[576,128]{1,0:T(8,128)(2,1)S(1)}, u32[]{:S(2)}, u32[]{:S(2)}) collective-permute-start(bf16[576,128]{1,0:T(8,128)(2,1)S(1)} %get-tuple-element.167), channel_id=1, source_target_pairs={{0,6},{1,7},{2,4},{3,5},{4,2},{5,3},{6,0},{7,1},{8,14},{9,15},{10,... | collective-permute-start | bytes 442376 | tf_op jit(solution)/shard_map/ppermute | solution.py:774
  (6 other events, 23.8 us)
